TPU v7x, 256 devices: a whole 4x4x8 slice. The times are simulated.
256 devices in a mesh: seq: 16 (over z, core), ch: 16 (over y, x).
Axes of the slice: x: 4, y: 4, z: 8, core: 2. Of those that a mesh axis runs over, the one named last changes fastest.
Arguments:
- query: bfloat16 [2048, 8192], P('seq', 'ch'), may hold values from -6 to 6
- key: bfloat16 [2048, 8192], P('seq', 'ch'), may hold values from -6 to 6
- value: bfloat16 [2048, 8192], P('seq', 'ch'), may hold values from -6 to 6
- short_taps: float32 [3, 3, 8192], P(None, None, 'ch'), may hold values from -3 to 3
- decay_rate: float32 [16, 8192], P(None, 'ch'), may hold values from 0.00012207031 to 0.05
- residue: float32 [16, 8192], P(None, 'ch'), may hold values from -2 to 2
- skip_gain: float32 [8192], P('ch'), may hold values from -4 to 4
- out_weight: bfloat16 [8192, 8192], P('ch', 'seq'), may hold values from -0.09375 to 0.09375
- grad_out: bfloat16 [2048, 8192], P('seq', 'ch'), may hold values from -6 to 6
Outputs:
- mixed: bfloat16 [2048, 8192], P('seq', 'ch')
- grad_query: bfloat16 [2048, 8192], P('seq', 'ch')
- grad_key: bfloat16 [2048, 8192], P('seq', 'ch')
- grad_value: bfloat16 [2048, 8192], P('seq', 'ch')
All inputs are finite; a program needn't handle non-finite values.
Results may differ from a plain program's by a relative error of at most 0.017.
Values may be sent and summed in bfloat16 or wider, within the bound.
A program may use at most 128 MiB of HBM per device.

v0:
```python
import math

import jax
import jax.numpy as jnp
from jax import lax
from jax.sharding import PartitionSpec as P


def from_behind(block, axis, distance):
    devices = range(lax.axis_size(axis))
    route = [(i - distance, i) for i in devices if i - distance in devices]
    return lax.ppermute(block, axis, route)


def entering(shard, axis, join, neutral, backward):
    count = lax.axis_size(axis)
    place = lax.axis_index(axis)
    ahead = count - 1 - place if backward else place
    gathered = jax.tree.map(
        lambda a, kind: lax.all_gather(a.astype(kind), axis), shard, (jnp.bfloat16, jnp.bfloat16)
    )
    state = jax.tree.map(lambda a, e: jnp.zeros_like(a) + jnp.asarray(e, a.dtype), shard, neutral)

    def one(turn, state):
        source = count - 1 - turn if backward else turn
        return join(
            state,
            jax.tree.map(
                lambda a, own: lax.dynamic_index_in_dim(a, source, 0, False).astype(own.dtype),
                gathered,
                shard,
            ),
        )

    return lax.fori_loop(0, ahead, one, state)


def chain_combine(earlier, later):
    return (earlier[0] * later[0], earlier[1] * later[0] + later[1])


def per_device(query, key, value, short_taps, decay_rate, residue, skip_gain, out_weight, grad_out):
    tok_rows, chan_width = query.shape
    tap_count = short_taps.shape[0]
    mode_count = decay_rate.shape[0]
    highest = lax.Precision.HIGHEST
    streams = jnp.stack([query, key, value])
    before = from_behind(streams[:, tok_rows - (tap_count - 1) :, :], "seq", 1)
    extended = jnp.concatenate([before, streams], axis=1).astype(jnp.float32)
    featured = jnp.zeros((3, tok_rows, chan_width), jnp.float32)
    for tap_index in range(tap_count):
        begin = tap_count - 1 - tap_index
        featured = (
            featured + short_taps[tap_index][:, None, :] * extended[:, begin : begin + tok_rows, :]
        )
    q_short = featured[0]
    k_short = featured[1]
    v_short = featured[2]
    gated = k_short * v_short
    columns = lax.all_gather(out_weight, "seq", axis=1, tiled=True)
    block_len = math.gcd(tok_rows, 128)
    block_count = tok_rows // block_len
    mode_scale = residue * jnp.sqrt(-jnp.expm1(-2.0 * decay_rate))
    offsets = jnp.arange(block_len).astype(jnp.float32)
    decay_pos = jnp.exp(-decay_rate[None, :, :] * offsets[:, None, None])
    filter_block = jnp.sum(mode_scale[None, :, :] * decay_pos, axis=1)
    filter_padded = jnp.concatenate(
        [jnp.zeros((block_len, chan_width), jnp.float32), filter_block], axis=0
    )
    lag_steps = jnp.arange(block_len)
    lag_index = block_len + lag_steps[:, None] - lag_steps[None, :]
    toeplitz = jnp.take(filter_padded, lag_index, axis=0)
    to_end = jnp.flip(decay_pos, 0)
    from_entry = mode_scale[None, :, :] * decay_pos * jnp.exp(-decay_rate)[None, :, :]
    step_decay = jnp.exp(-decay_rate * block_len)
    device_decay = jnp.exp(-decay_rate * tok_rows)
    block_steps = jnp.arange(block_count).astype(jnp.float32)
    block_decay = jnp.exp(-decay_rate[None, :, :] * block_len * block_steps[:, None, None])

    def local_pass(signal):
        blocks = signal.reshape(block_count, block_len, chan_width)
        intra = jnp.einsum("ijc,bjc->bic", toeplitz, blocks, precision=highest)
        ends = jnp.einsum("jnc,bjc->bnc", to_end, blocks, precision=highest)

        def advance(state, end_state):
            return (state * step_decay + end_state, state)

        final, entries = lax.scan(advance, jnp.zeros((mode_count, chan_width), jnp.float32), ends)
        return (intra, entries, final)

    def finish(intra, entries, entry_dev):
        starts = entries + block_decay * entry_dev[None, :, :]
        result = intra + jnp.einsum("inc,bnc->bic", from_entry, starts, precision=highest)
        return result.reshape(tok_rows, chan_width)

    def carried(final, later):
        identity = (jnp.ones_like(device_decay), jnp.zeros_like(final))
        if later:
            prefix = entering((device_decay, final), "seq", chain_combine, identity, True)
        else:
            prefix = entering((device_decay, final), "seq", chain_combine, identity, False)
        return prefix[1]

    intra, entries, final = local_pass(gated)
    entry_dev = carried(final, False)
    long_out = finish(intra, entries, entry_dev) + skip_gain[None, :] * gated
    mixer = (q_short * long_out).astype(jnp.bfloat16)
    partial_value = jnp.dot(mixer, columns, preferred_element_type=jnp.float32)
    mixed = lax.psum_scatter(
        partial_value.astype(jnp.bfloat16), "ch", scatter_dimension=1, tiled=True
    )
    grad_mixer = lax.dot_general(
        lax.all_gather(grad_out, "ch", axis=1, tiled=True),
        columns,
        (((1,), (1,)), ((), ())),
        preferred_element_type=jnp.float32,
    )
    grad_qshort = grad_mixer * long_out
    grad_long = grad_mixer * q_short
    intra_b, entries_b, final_b = local_pass(jnp.flip(grad_long, 0))
    exit_dev = carried(final_b, True)
    grad_gated = jnp.flip(finish(intra_b, entries_b, exit_dev), 0) + skip_gain[None, :] * grad_long
    grad_stack = jnp.stack([grad_qshort, grad_gated * v_short, grad_gated * k_short])
    after = from_behind(grad_stack[:, : tap_count - 1, :], "seq", -1)
    extended_back = jnp.concatenate([grad_stack, after], axis=1)
    grads = jnp.zeros((3, tok_rows, chan_width), jnp.float32)
    for tap_index in range(tap_count):
        grads = (
            grads
            + short_taps[tap_index][:, None, :]
            * extended_back[:, tap_index : tap_index + tok_rows, :]
        )
    grads = grads.astype(jnp.bfloat16)
    return (mixed, grads[0], grads[1], grads[2])


def solution(mesh):
    in_specs = (
        P("seq", "ch"),
        P("seq", "ch"),
        P("seq", "ch"),
        P(None, None, "ch"),
        P(None, "ch"),
        P(None, "ch"),
        P("ch"),
        P("ch", "seq"),
        P("seq", "ch"),
    )
    out_specs = (P("seq", "ch"), P("seq", "ch"), P("seq", "ch"), P("seq", "ch"))
    return jax.shard_map(
        per_device, mesh=mesh, in_specs=in_specs, out_specs=out_specs, check_vma=False
    )
```

profile of v0, /device:TPU:65, one launch (start us, length us, event | category | flops | bytes accessed | tf_op | source)
XLA Modules:
  0.0 292.9 jit_solution(6199740509660682278)
XLA Ops:
  7.2 0.7 all-gather.8.cloned.1.call-update
  7.9 0.7 all-gather.6.cloned.1.call-update
  8.7 0.7 pad_maximum_fusion.2
  9.4 4.1 %collective-permute-start = (bf16[3,2,512]{2,1,0:T(2,128)(2,1)S(1)}, bf16[3,2,512]{2,1,0:T(2,128)(2,1)S(1)}, u32[]{:S(2)}, u32[]{:S(2)}) collective-permute-start(bf16[3,2,512]{2,1,0:T(2,128)(2,1)S(1)} %pad_maximum_fusion.2), channel_id=1, source_target_pairs={{0,16},{16,32},{32,48},{48,64},{64,80},{80,96},{96,112},{112,128},... | collective-permute-start | bytes 18440 | tf_op jit(solution)/shard_map/ppermute | solution.py:12
  13.6 0.7 slice_bitcast_fusion.6
  14.3 0.8 sqrt_multiply_fusion
  15.1 3.1 %multiply_exponential_fusion = (f32[128,16,512]{2,1,0:T(8,128)}, f32[128,512]{1,0:T(8,128)S(1)}) fusion(f32[128]{0:T(128)S(1)} %iota_convert_fusion, f32[16,512]{1,0:T(8,128)S(1)} %get-tuple-element.208, f32[16,512]{1,0:T(8,128)S(1)} %get-tuple-element.207), kind=kLoop, calls=%fused_computation.12 | loop fusion | flops 3080192 | bytes 4522496 | tf_op jit(solution)/shard_map/exp | solution.py:65
  18.5 64.1 %gather_fusion = f32[16384,512]{1,0:T(8,128)} fusion(f32[256,512]{1,0:T(8,128)S(1)} %concatenate.10, s32[16384]{0:T(1024)S(1)} %fusion.10), kind=kCustom, calls=%fused_computation | custom fusion | bytes 67174400 | tf_op jit(solution)/shard_map/jit(_take)/gather | solution.py:72
  83.1 38.1 %all-gather.6.cloned.1.call-done = bf16[512,8192]{1,0:T(8,128)(2,1)} async-done(((bf16[512,512]{1,0:T(8,128)(2,1)}), bf16[512,8192]{1,0:T(8,128)(2,1)}) %all-gather.6.cloned.1.call-update) | async-done | bytes 8388624 | tf_op jit(solution)/shard_map/all_gather | solution.py:60
  121.2 6.9 %fusion.8 = (f32[128,512]{1,0:T(8,128)S(1)}, f32[128,512]{1,0:T(8,128)S(1)}) fusion(f32[3,128,512]{2,1,0:T(8,128)S(1)} %fusion.3, bf16[128,8192]{1,0:T(8,128)(2,1)} %all-gather.8.cloned.1.call-done, bf16[512,8192]{1,0:T(8,128)(2,1)} %all-gather.6.cloned.1.call-done), kind=kOutput, calls=%fused_computation.40 | convolution fusion | flops 1073807360 | bytes 11272192 | tf_op jit(solution)/shard_map/dot_general | solution.py:112
  128.3 3.1 %multiply_reduce_fusion.3 = (f32[512,16]{0,1:T(8,128)S(1)}, f32[512,16]{0,1:T(8,128)S(1)}) fusion(f32[128,16,512]{2,1,0:T(8,128)} %get-tuple-element.199, f32[512,128]{0,1:T(8,128)S(1)} %bitcast.129, f32[512,128]{0,1:T(8,128)S(1)} %multiply_bitcast_fusion.1), kind=kLoop, calls=%fused_computation.9 | loop fusion | flops 4177920 | bytes 4784128 | tf_op jit(solution)/shard_map/jnc,bjc->bnc/dot_general | solution.py:83
  131.4 16.5 %all-gather = bf16[256,512]{1,0:T(8,128)(2,1)S(1)} all-gather(bf16[16,512]{1,0:T(8,128)(2,1)S(1)} %get-tuple-element.205), channel_id=2, replica_groups=mesh['seq'=16,'ch'=16] {'seq'}, dimensions={0}, use_global_device_ids=true | all-gather | bytes 278528 | tf_op jit(solution)/shard_map/all_gather | solution.py:20
  147.9 15.2 %all-gather.2 = bf16[256,512]{1,0:T(8,128)(2,1)S(1)} all-gather(bf16[16,512]{1,0:T(8,128)(2,1)S(1)} %get-tuple-element.206), channel_id=4, replica_groups=mesh['seq'=16,'ch'=16] {'seq'}, dimensions={0}, use_global_device_ids=true | all-gather | bytes 278528 | tf_op jit(solution)/shard_map/all_gather | solution.py:20
  163.0 0.4 while.17
  163.5 16.4 %all-gather.1 = bf16[256,512]{1,0:T(8,128)(2,1)S(1)} all-gather(bf16[16,512]{1,0:T(8,128)(2,1)S(1)} %get-tuple-element.204), channel_id=3, replica_groups=mesh['seq'=16,'ch'=16] {'seq'}, dimensions={0}, use_global_device_ids=true | all-gather | bytes 278528 | tf_op jit(solution)/shard_map/all_gather | solution.py:20
  179.9 0.4 while.16
  180.4 18.0 %multiply_reduce_fusion = (f32[512,128]{0,1:T(8,128)S(1)}, f32[512,128]{0,1:T(8,128)S(1)}) fusion(f32[128,128,512]{2,1,0:T(8,128)} %bitcast.128, f32[512,128]{0,1:T(8,128)S(1)} %bitcast.130, pred[128,128]{1,0:T(8,128)(4,1)S(1)} %fusion.13, f32[512,128]{0,1:T(8,128)S(1)} %multiply_bitcast_fusion.1), kind=kLoop, calls=%fused_computation.5 | loop fusion | flops 41811968 | bytes 34619392 | tf_op jit(solution)/shard_map/ijc,bjc->bic/dot_general | solution.py:82
  198.4 2.5 multiply_reduce_fusion.2
  201.3 6.0 %convolution_convert_fusion = bf16[128,8192]{1,0:T(8,128)(2,1)} fusion(bf16[512,8192]{1,0:T(8,128)(2,1)} %all-gather.6.cloned.1.call-done, f32[128,512]{1,0:T(8,128)S(1)} %get-tuple-element.195, f32[3,128,512]{2,1,0:T(8,128)S(1)} %fusion.3), kind=kOutput, calls=%fused_computation.7 | convolution fusion | flops 1074921472 | bytes 11010048 | tf_op jit(solution)/shard_map/dot_general | solution.py:108
  207.4 2.0 collective-permute-start.1
  209.4 3.0 %collective-permute-done.1 = f32[3,2,512]{2,1,0:T(2,128)S(1)} collective-permute-done((f32[3,2,512]{2,1,0:T(2,128)S(1)}, f32[3,2,512]{2,1,0:T(2,128)S(1)}, u32[]{:S(2)}, u32[]{:S(2)}) %collective-permute-start.1) | collective-permute-done | bytes 12320 | tf_op jit(solution)/shard_map/ppermute | solution.py:12
  212.5 0.3 fusion.1
  212.7 0.8 slice_bitcast_fusion.1
  213.5 72.8 %reduce-scatter.2.cloned.1.call-done = bf16[128,512]{1,0:T(8,128)(2,1)} async-done(((bf16[128,8192]{1,0:T(8,128)(2,1)}), bf16[128,512]{1,0:T(8,128)(2,1)}) %reduce-scatter.2.cloned.1.call-update) | async-done | bytes 131088 | tf_op jit(solution)/shard_map/reduce_scatter | solution.py:109
  (50 shorter events, 1.7 us)
Async XLA Ops:
  7.2 75.9 %all-gather.8.cloned.1.call-start = ((), (), s32[]{:S(2)}) async-start(), calls=%async_computation.3 | async-start | bytes 2228224 | tf_op jit(solution)/shard_map/all_gather | solution.py:113
  7.9 113.3 %all-gather.6.cloned.1.call-start = ((), (), s32[]{:S(2)}) async-start(), calls=%async_computation.1 | async-start | bytes 8912896 | tf_op jit(solution)/shard_map/all_gather | solution.py:60
  8.6 277.7 %reduce-scatter.2.cloned.1.call-start = ((), (), s32[]{:S(2)}) async-start(), calls=%async_computation.2 | async-start | bytes 2228224 | tf_op jit(solution)/shard_map/reduce_scatter | solution.py:109
  9.4 73.2 %collective-permute-start = (bf16[3,2,512]{2,1,0:T(2,128)(2,1)S(1)}, bf16[3,2,512]{2,1,0:T(2,128)(2,1)S(1)}, u32[]{:S(2)}, u32[]{:S(2)}) collective-permute-start(bf16[3,2,512]{2,1,0:T(2,128)(2,1)S(1)} %pad_maximum_fusion.2), channel_id=1, source_target_pairs={{0,16},{16,32},{32,48},{48,64},{64,80},{80,96},{96,112},{112,128},... | collective-permute-start | bytes 18440 | tf_op jit(solution)/shard_map/ppermute | solution.py:12
  18.5 64.2 %copy-start = (bf16[128,512]{1,0:T(8,128)(2,1)S(1)}, bf16[128,512]{1,0:T(8,128)(2,1)}, u32[]{:S(2)}) copy-start(bf16[128,512]{1,0:T(8,128)(2,1)} %param.15) | copy-start | bytes 393220
  18.5 64.2 %copy-start.1 = (bf16[128,512]{1,0:T(8,128)(2,1)S(1)}, bf16[128,512]{1,0:T(8,128)(2,1)}, u32[]{:S(2)}) copy-start(bf16[128,512]{1,0:T(8,128)(2,1)} %param.14) | copy-start | bytes 393220
  18.5 64.2 %copy-start.2 = (bf16[128,512]{1,0:T(8,128)(2,1)S(1)}, bf16[128,512]{1,0:T(8,128)(2,1)}, u32[]{:S(2)}) copy-start(bf16[128,512]{1,0:T(8,128)(2,1)} %param.13) | copy-start | bytes 393220
  128.1 3.2 %copy-start.3 = (f32[16,512]{1,0:T(8,128)S(1)}, f32[16,512]{1,0:T(8,128)}, u32[]{:S(2)}) copy-start(f32[16,512]{1,0:T(8,128)} %param.17) | copy-start | bytes 98308
  180.4 20.7 %copy-start.4 = (f32[512]{0:T(512)S(1)}, f32[512]{0:T(512)}, u32[]{:S(2)}) copy-start(f32[512]{0:T(512)} %param.19) | copy-start | bytes 6148
  207.4 5.0 %collective-permute-start.1 = (f32[3,2,512]{2,1,0:T(2,128)S(1)}, f32[3,2,512]{2,1,0:T(2,128)S(1)}, u32[]{:S(2)}, u32[]{:S(2)}) collective-permute-start(f32[3,2,512]{2,1,0:T(2,128)S(1)} %slice.75), channel_id=1, source_target_pairs={{16,0},{32,16},{48,32},{64,48},{80,64},{96,80},{112,96},{128,112},... | collective-permute-start | bytes 36872 | tf_op jit(solution)/shard_map/ppermute | solution.py:12
Sparse Core Ops, SparseCore 0:
  10.4 54.0 all-gather.7
  66.3 54.7 all-gather.5
  207.4 78.8 reduce-scatter.1
where the time goes:
time: 295 us; the launch traced here: 293 us
  waiting for transfers between devices  115 us (39%)
  local copies, waits for them, and re-layouts  66 us (22%)
  blocking collectives  48.1 us (16%)
  other arithmetic  29.7 us (10%)
  between operations  14 us (5%)
  matrix products  12.9 us (4%)
  starting transfers between devices  6.25 us (2%)
    reduce_scatter x1, waiting for transfers between devices, per_device(): lax.psum_scatter(partial_value.astype(jnp.bfloat16), 'ch', scatter_dimens...  72.8 us
    gather x1, local copies, waits for them, and re-layouts, per_device(): toeplitz = jnp.take(filter_padded, lag_index, axis=0)  64.1 us
    all_gather x3, blocking collectives, entering(): lax.all_gather(a.astype(kind), axis)  48.1 us
    all_gather x1, waiting for transfers between devices, per_device(): columns = lax.all_gather(out_weight, 'seq', axis=1, tiled=True)  38.1 us
    dot_general x1, other arithmetic, local_pass(): intra = jnp.einsum('ijc,bjc->bic', toeplitz, blocks, precision=highest)  18 us
    dot_general x1, matrix products, per_device(): lax.dot_general(lax.all_gather(grad_out, 'ch', axis=1, tiled=True), colum...  6.94 us
    ppermute x2, starting transfers between devices, from_behind(): return lax.ppermute(block, axis, route)  6.13 us
    dot_general x1, matrix products, per_device(): partial_value = jnp.dot(mixer, columns, preferred_element_type=jnp.float32)  5.99 us
  transfers between devices with their start and end apart: 5, of which 3 were waited for; matrix products, arithmetic and copies ran while one was open for 24% of the time, Pallas kernels for 0%

commit v1 on v0

v1 whole, which is shorter than its diff:
```python
import jax
import jax.numpy as jnp
from jax import lax
from jax.sharding import PartitionSpec as P


def from_behind(block, axis, distance):
    devices = range(lax.axis_size(axis))
    route = [(i - distance, i) for i in devices if i - distance in devices]
    return lax.ppermute(block, axis, route)


def per_device(query, key, value, short_taps, decay_rate, residue, skip_gain, out_weight, grad_out):
    tok_rows, chan_width = query.shape
    tap_count = short_taps.shape[0]
    mode_count = decay_rate.shape[0]
    highest = lax.Precision.HIGHEST
    count = lax.axis_size("seq")
    place = lax.axis_index("seq")

    columns = lax.all_gather(out_weight, "seq", axis=1, tiled=True)
    grad_full = lax.all_gather(grad_out, "ch", axis=1, tiled=True)

    streams = jnp.stack([query, key, value])
    before = from_behind(streams[:, tok_rows - (tap_count - 1) :, :], "seq", 1)
    extended = jnp.concatenate([before, streams], axis=1).astype(jnp.float32)
    featured = jnp.zeros((3, tok_rows, chan_width), jnp.float32)
    for tap_index in range(tap_count):
        begin = tap_count - 1 - tap_index
        featured = (
            featured + short_taps[tap_index][:, None, :] * extended[:, begin : begin + tok_rows, :]
        )
    q_short = featured[0]
    k_short = featured[1]
    v_short = featured[2]
    gated = k_short * v_short

    mode_scale = residue * jnp.sqrt(-jnp.expm1(-2.0 * decay_rate))
    offsets = jnp.arange(tok_rows).astype(jnp.float32)
    shrink = jnp.exp(-decay_rate[None, :, :] * offsets[:, None, None])
    grow = jnp.exp(decay_rate[None, :, :] * offsets[:, None, None])
    scaled_shrink = mode_scale[None] * shrink
    scaled_grow = mode_scale[None] * grow
    one_step = jnp.exp(-decay_rate)
    block_decay = jnp.exp(-decay_rate * tok_rows)
    rows = jnp.arange(tok_rows)
    lower = (rows[:, None] >= rows[None, :]).astype(jnp.float32)
    upper = (rows[:, None] <= rows[None, :]).astype(jnp.float32)

    def prefix(tri, weights, signal):
        spread = (weights * signal[:, None, :]).reshape(tok_rows, mode_count * chan_width)
        summed = jnp.dot(tri, spread, precision=highest, preferred_element_type=jnp.float32)
        return summed.reshape(tok_rows, mode_count, chan_width)

    fwd_sums = prefix(lower, grow, gated)
    fwd_final = shrink[tok_rows - 1] * fwd_sums[tok_rows - 1]

    grad_mixer = lax.dot_general(
        grad_full, columns, (((1,), (1,)), ((), ())), preferred_element_type=jnp.float32
    )
    grad_long = grad_mixer * q_short
    bwd_sums = prefix(upper, shrink, grad_long)
    bwd_final = bwd_sums[0]

    finals = jnp.stack([fwd_final, bwd_final]).astype(jnp.bfloat16)
    gathered = lax.all_gather(finals, "seq").astype(jnp.float32)
    source = jnp.arange(count)
    fwd_gap = place - 1 - source
    bwd_gap = source - place - 1
    fwd_weight = jnp.where(
        (fwd_gap >= 0)[:, None, None],
        jnp.exp(-decay_rate[None] * (tok_rows * jnp.maximum(fwd_gap, 0)).astype(jnp.float32)[:, None, None]),
        0.0,
    )
    bwd_weight = jnp.where(
        (bwd_gap >= 0)[:, None, None],
        jnp.exp(-decay_rate[None] * (tok_rows * jnp.maximum(bwd_gap, 0)).astype(jnp.float32)[:, None, None]),
        0.0,
    )
    fwd_entry = jnp.sum(fwd_weight * gathered[:, 0], axis=0) * one_step
    bwd_entry = jnp.sum(bwd_weight * gathered[:, 1], axis=0) * block_decay

    long_out = (
        jnp.sum(scaled_shrink * (fwd_sums + fwd_entry[None]), axis=1) + skip_gain[None, :] * gated
    )
    mixer = (q_short * long_out).astype(jnp.bfloat16)
    partial_value = jnp.dot(mixer, columns, preferred_element_type=jnp.float32)
    mixed = lax.psum_scatter(
        partial_value.astype(jnp.bfloat16), "ch", scatter_dimension=1, tiled=True
    )

    grad_qshort = grad_mixer * long_out
    grad_gated = (
        jnp.sum(scaled_grow * (bwd_sums + bwd_entry[None]), axis=1) + skip_gain[None, :] * grad_long
    )
    grad_stack = jnp.stack([grad_qshort, grad_gated * v_short, grad_gated * k_short])
    after = from_behind(grad_stack[:, : tap_count - 1, :], "seq", -1)
    extended_back = jnp.concatenate([grad_stack, after], axis=1)
    grads = jnp.zeros((3, tok_rows, chan_width), jnp.float32)
    for tap_index in range(tap_count):
        grads = (
            grads
            + short_taps[tap_index][:, None, :]
            * extended_back[:, tap_index : tap_index + tok_rows, :]
        )
    grads = grads.astype(jnp.bfloat16)
    return (mixed, grads[0], grads[1], grads[2])


def solution(mesh):
    in_specs = (
        P("seq", "ch"),
        P("seq", "ch"),
        P("seq", "ch"),
        P(None, None, "ch"),
        P(None, "ch"),
        P(None, "ch"),
        P("ch"),
        P("ch", "seq"),
        P("seq", "ch"),
    )
    out_specs = (P("seq", "ch"), P("seq", "ch"), P("seq", "ch"), P("seq", "ch"))
    return jax.shard_map(
        per_device, mesh=mesh, in_specs=in_specs, out_specs=out_specs, check_vma=False
    )
```

time: 295 us -> 272 us (0.922)
  waiting for transfers between devices: 115 us -> 180 us
  local copies, waits for them, and re-layouts: 66 us -> 26.7 us
  blocking collectives: 48.1 us -> 17.4 us
  other arithmetic: 29.7 us -> 10.1 us
    gather x1 -> x0, local copies, waits for them, and re-layouts: 64.1 us -> none  [per_device(): toeplitz = jnp.take(filter_padded, lag_index, axis=0)]
    all_gather x1, waiting for transfers between devices: 0.02 us -> 46.3 us  [per_device(): grad_full = lax.all_gather(grad_out, 'ch', axis=1, tiled=True)]
    all_gather x3 -> x1, blocking collectives: 48.1 us -> 17.4 us  [per_device(): gathered = lax.all_gather(finals, 'seq').astype(jnp.float32)]
    unnamed x10 -> x28, local copies, waits for them, and re-layouts: 0.03 us -> 24 us
    dot_general x3 -> x0, other arithmetic: 23.6 us -> none  [the longest x1 18 us: local_pass(): intra = jnp.einsum('ijc,bjc->bic', toeplitz, blocks, precision=highest)]
    all_gather x1, waiting for transfers between devices: 38.1 us -> 56.7 us  [per_device(): columns = lax.all_gather(out_weight, 'seq', axis=1, tiled=True)]
    dot_general x1 -> x3, matrix products: 6.94 us -> 13 us  [the longest x1 6.97 us: per_device(): lax.dot_general(grad_full, columns, (((1,), (1,)), ((), ())), preferred_e...]
    reduce_sum x0 -> x2, other arithmetic: none -> 4.12 us  [the longest x1 3.81 us: per_device(): jnp.sum(scaled_grow * (bwd_sums + bwd_entry[None]), axis=1)]
  transfers between devices with their start and end apart: 5 -> 5, of which waited for: 3 -> 4; matrix products, arithmetic and copies ran while one was open for 24% -> 2% of each run, Pallas kernels for 0% -> 0%
where the time goes in v1:
time: 272 us; the launch traced here: 270 us
  waiting for transfers between devices  180 us (66%)
  local copies, waits for them, and re-layouts  26.7 us (10%)
  blocking collectives  17.4 us (6%)
  matrix products  15.6 us (6%)
  between operations  14.1 us (5%)
  other arithmetic  10.1 us (4%)
  starting transfers between devices  6.29 us (2%)
    reduce_scatter x1, waiting for transfers between devices, per_device(): lax.psum_scatter(partial_value.astype(jnp.bfloat16), 'ch', scatter_dimens...  72.5 us
    all_gather x1, waiting for transfers between devices, per_device(): columns = lax.all_gather(out_weight, 'seq', axis=1, tiled=True)  56.7 us
    all_gather x1, waiting for transfers between devices, per_device(): grad_full = lax.all_gather(grad_out, 'ch', axis=1, tiled=True)  46.3 us
    unnamed x28, local copies, waits for them, and re-layouts  24 us
    all_gather x1, blocking collectives, per_device(): gathered = lax.all_gather(finals, 'seq').astype(jnp.float32)  17.4 us
    dot_general x1, matrix products, per_device(): lax.dot_general(grad_full, columns, (((1,), (1,)), ((), ())), preferred_e...  6.97 us
    ppermute x2, starting transfers between devices, from_behind(): return lax.ppermute(block, axis, route)  6.17 us
    dot_general x2, matrix products, prefix(): jnp.dot(tri, spread, precision=highest, preferred_element_type=jnp.float32)  6.02 us
  transfers between devices with their start and end apart: 5, of which 4 were waited for; matrix products, arithmetic and copies ran while one was open for 2% of the time, Pallas kernels for 0%

profile of v1, /device:TPU:65, one launch (start us, length us, event | category | flops | bytes accessed | tf_op | source)
XLA Modules:
  0.0 270.1 jit_solution(8991568533417485764)
XLA Ops:
  8.7 0.7 pad_maximum_fusion.3
  9.5 4.1 %collective-permute-start = (bf16[3,2,512]{2,1,0:T(2,128)(2,1)S(1)}, bf16[3,2,512]{2,1,0:T(2,128)(2,1)S(1)}, u32[]{:S(2)}, u32[]{:S(2)}) collective-permute-start(bf16[3,2,512]{2,1,0:T(2,128)(2,1)S(1)} %pad_maximum_fusion.3), channel_id=1, source_target_pairs={{0,16},{16,32},{32,48},{48,64},{64,80},{80,96},{96,112},{112,128},... | collective-permute-start | bytes 18440 | tf_op jit(solution)/shard_map/ppermute | solution.py:10
  13.6 0.7 slice_bitcast_fusion.10
  14.4 0.8 fusion.32
  15.1 2.6 multiply_exponential_fusion
  18.2 46.3 %all-gather.3.cloned.1.call-done = bf16[128,8192]{1,0:T(8,128)(2,1)} async-done(((bf16[128,512]{1,0:T(8,128)(2,1)}), bf16[128,8192]{1,0:T(8,128)(2,1)}) %all-gather.3.cloned.1.call-update) | async-done | bytes 2097168 | tf_op jit(solution)/shard_map/all_gather | solution.py:22
  64.5 56.7 %all-gather.5.cloned.1.call-done = bf16[512,8192]{1,0:T(8,128)(2,1)} async-done(((bf16[512,512]{1,0:T(8,128)(2,1)}), bf16[512,8192]{1,0:T(8,128)(2,1)}) %all-gather.5.cloned.1.call-update) | async-done | bytes 8388624 | tf_op jit(solution)/shard_map/all_gather | solution.py:21
  121.2 7.0 %fusion.26 = (f32[128,512]{1,0:T(8,128)S(1)}, f32[128,512]{1,0:T(8,128)S(1)}, f32[128,512]{1,0:T(8,128)S(1)}) fusion(f32[3,128,512]{2,1,0:T(8,128)S(1)} %fusion.19, bf16[128,8192]{1,0:T(8,128)(2,1)} %all-gather.3.cloned.1.call-done, bf16[512,8192]{1,0:T(8,128)(2,1)} %all-gather.5.cloned.1.call-done), kind=kOutput, calls=%fused_computation.49 | convolution fusion | flops 1073872896 | bytes 12058624 | tf_op jit(solution)/shard_map/dot_general | solution.py:58
  128.7 3.4 %copy.20 = f32[16,8,16,512]{3,1,2,0:T(8,128)S(1)} copy(f32[16,8,16,512]{3,2,1,0:T(8,128)S(1)} %bitcast.88) | data formatting | bytes 8388608
  132.1 3.0 %fusion.4 = f32[128,8192]{1,0:T(8,128)S(1)} fusion(f32[128,8192]{1,0:T(8,128)S(1)} %bitcast.86, f32[8192]{0:T(1024)S(1)} %bitcast.98, f32[128]{0:T(128)S(1)} %iota_convert_fusion), kind=kOutput, calls=%fused_computation.7 | convolution fusion | flops 1612726272 | bytes 8421888 | tf_op jit(solution)/shard_map/dot_general | solution.py:52
  135.2 1.9 copy-done
  137.2 7.5 %copy.21 = f32[16,8,16,512]{3,2,1,0:T(8,128)} copy(f32[16,8,16,512]{3,1,2,0:T(8,128)} %bitcast.84) | data formatting | bytes 8388608
  145.3 3.4 %copy.17 = f32[16,8,16,512]{3,1,2,0:T(8,128)S(1)} copy(f32[16,8,16,512]{3,2,1,0:T(8,128)S(1)} %bitcast.89) | data formatting | bytes 8388608
  148.7 3.0 %fusion.8 = f32[128,8192]{1,0:T(8,128)S(1)} fusion(f32[128,8192]{1,0:T(8,128)S(1)} %bitcast.87, f32[128]{0:T(128)S(1)} %iota_convert_fusion, f32[8192]{0:T(1024)S(1)} %bitcast.97), kind=kOutput, calls=%fused_computation.11 | convolution fusion | flops 1612726272 | bytes 8421888 | tf_op jit(solution)/shard_map/dot_general | solution.py:52
  151.8 1.9 copy-done.1
  153.8 5.6 %copy.18 = f32[16,8,16,512]{3,2,1,0:T(8,128)S(1)} copy(f32[16,8,16,512]{3,1,2,0:T(8,128)} %bitcast.85) | data formatting | bytes 8388608
  159.5 0.8 fusion.29
  160.2 17.4 %all_gather.12 = bf16[16,2,16,512]{3,2,1,0:T(8,128)(2,1)S(1)} all-gather(bf16[1,2,16,512]{3,2,1,0:T(8,128)(2,1)S(1)} %pad_maximum_fusion.2), channel_id=1, replica_groups=mesh['seq'=16,'ch'=16] {'seq'}, dimensions={0}, use_global_device_ids=true | all-gather | bytes 557056 | tf_op jit(solution)/shard_map/all_gather | solution.py:66
  178.2 3.8 %fusion.1 = (f32[128,512]{1,0:T(8,128)S(1)}, f32[128,512]{1,0:T(8,128)S(1)}) fusion(f32[16,8,16,512]{3,2,1,0:T(8,128)S(1)} %copy-done.2, f32[16,512]{1,0:T(8,128)S(1)} %get-tuple-element.16, f32[16,512]{1,0:T(8,128)S(1)} %copy-done.3, f32[128]{0:T(128)S(1)} %iota_convert_fusion, f32[16,512]{1,0:T(8,128)S(1)} %get-tuple-element.17, ...), kind=kLoop, calls=%fused_computation.3 | loop fusion | flops 10354688 | bytes 9077248 | tf_op jit(solution)/shard_map/reduce_sum | solution.py:94
  182.1 2.6 convolution_convert_fusion
  185.0 2.1 collective-permute-start.1
  187.1 2.9 %collective-permute-done.1 = f32[3,2,512]{2,1,0:T(2,128)S(1)} collective-permute-done((f32[3,2,512]{2,1,0:T(2,128)S(1)}, f32[3,2,512]{2,1,0:T(2,128)S(1)}, u32[]{:S(2)}, u32[]{:S(2)}) %collective-permute-start.1) | collective-permute-done | bytes 12320 | tf_op jit(solution)/shard_map/ppermute | solution.py:10
  190.3 0.8 slice_bitcast_fusion.5
  191.1 72.5 %reduce-scatter.2.cloned.1.call-done = bf16[128,512]{1,0:T(8,128)(2,1)} async-done(((bf16[128,8192]{1,0:T(8,128)(2,1)}), bf16[128,512]{1,0:T(8,128)(2,1)}) %reduce-scatter.2.cloned.1.call-update) | async-done | bytes 131088 | tf_op jit(solution)/shard_map/reduce_scatter | solution.py:88
  (50 shorter events, 4.3 us)
Async XLA Ops:
  7.2 10.6 %copy-start.4 = (bf16[128,512]{1,0:T(8,128)(2,1)S(1)}, bf16[128,512]{1,0:T(8,128)(2,1)}, u32[]{:S(2)}) copy-start(bf16[128,512]{1,0:T(8,128)(2,1)} %param.11) | copy-start | bytes 393220
  7.2 10.6 %copy-start.5 = (bf16[128,512]{1,0:T(8,128)(2,1)S(1)}, bf16[128,512]{1,0:T(8,128)(2,1)}, u32[]{:S(2)}) copy-start(bf16[128,512]{1,0:T(8,128)(2,1)} %param.10) | copy-start | bytes 393220
  7.2 10.6 %copy-start.6 = (bf16[128,512]{1,0:T(8,128)(2,1)S(1)}, bf16[128,512]{1,0:T(8,128)(2,1)}, u32[]{:S(2)}) copy-start(bf16[128,512]{1,0:T(8,128)(2,1)} %param.9) | copy-start | bytes 393220
  7.2 10.5 %copy-start.3 = (f32[16,512]{1,0:T(8,128)S(1)}, f32[16,512]{1,0:T(8,128)}, u32[]{:S(2)}) copy-start(f32[16,512]{1,0:T(8,128)} %param.13) | copy-start | bytes 98308
  7.2 57.3 %all-gather.3.cloned.1.call-start = ((), (), s32[]{:S(2)}) async-start(), calls=%async_computation.1 | async-start | bytes 2228224 | tf_op jit(solution)/shard_map/all_gather | solution.py:22
  7.9 113.3 %all-gather.5.cloned.1.call-start = ((), (), s32[]{:S(2)}) async-start(), calls=%async_computation.2 | async-start | bytes 8912896 | tf_op jit(solution)/shard_map/all_gather | solution.py:21
  8.7 254.9 %reduce-scatter.2.cloned.1.call-start = ((), (), s32[]{:S(2)}) async-start(), calls=%async_computation.3 | async-start | bytes 2228224 | tf_op jit(solution)/shard_map/reduce_scatter | solution.py:88
  9.5 8.3 %collective-permute-start = (bf16[3,2,512]{2,1,0:T(2,128)(2,1)S(1)}, bf16[3,2,512]{2,1,0:T(2,128)(2,1)S(1)}, u32[]{:S(2)}, u32[]{:S(2)}) collective-permute-start(bf16[3,2,512]{2,1,0:T(2,128)(2,1)S(1)} %pad_maximum_fusion.3), channel_id=1, source_target_pairs={{0,16},{16,32},{32,48},{48,64},{64,80},{80,96},{96,112},{112,128},... | collective-permute-start | bytes 18440 | tf_op jit(solution)/shard_map/ppermute | solution.py:10
  135.2 1.9 copy-start
  151.7 1.9 copy-start.1
  153.8 24.3 %copy-start.8 = (f32[16,512]{1,0:T(8,128)S(1)}, f32[16,512]{1,0:T(8,128)}, u32[]{:S(2)}) copy-start(f32[16,512]{1,0:T(8,128)} %param.14) | copy-start | bytes 98308
  153.8 24.4 %copy-start.2 = (f32[16,8,16,512]{3,2,1,0:T(8,128)S(1)}, f32[16,8,16,512]{3,2,1,0:T(8,128)}, u32[]{:S(2)}) copy-start(f32[16,8,16,512]{3,2,1,0:T(8,128)} %copy.21) | copy-start | bytes 12582916
  153.8 28.2 %slice-start = ((s8[8388608]{0:T(1024)(128)(4,1)}), s8[4194304]{0:T(1024)(128)(4,1)S(1)}, s32[]{:S(2)}) async-start(s8[8388608]{0:T(1024)(128)(4,1)} %bitcast.82), calls=%async_computation.4 | async-start | bytes 8388608
  177.7 4.4 %slice-start.1 = ((s8[8388608]{0:T(1024)(128)(4,1)}), s8[4194304]{0:T(1024)(128)(4,1)S(1)}, s32[]{:S(2)}) async-start(s8[8388608]{0:T(1024)(128)(4,1)} %bitcast.82), calls=%async_computation.5 | async-start | bytes 8388608
  178.2 3.9 %copy-start.7 = (f32[512]{0:T(512)S(1)}, f32[512]{0:T(512)}, u32[]{:S(2)}) copy-start(f32[512]{0:T(512)} %param.15) | copy-start | bytes 6148
  185.0 5.0 %collective-permute-start.1 = (f32[3,2,512]{2,1,0:T(2,128)S(1)}, f32[3,2,512]{2,1,0:T(2,128)S(1)}, u32[]{:S(2)}, u32[]{:S(2)}) collective-permute-start(f32[3,2,512]{2,1,0:T(2,128)S(1)} %slice.101), channel_id=1, source_target_pairs={{16,0},{32,16},{48,32},{64,48},{80,64},{96,80},{112,96},{128,112},... | collective-permute-start | bytes 36872 | tf_op jit(solution)/shard_map/ppermute | solution.py:10
Sparse Core Ops, SparseCore 0:
  10.4 54.0 all-gather.2
  66.4 54.7 all-gather.4
  184.8 78.6 reduce-scatter.1

commit v2 on v1

--- a/solution.py
+++ b/solution.py
@@ -18,8 +18,15 @@
     count = lax.axis_size("seq")
     place = lax.axis_index("seq")
 
-    columns = lax.all_gather(out_weight, "seq", axis=1, tiled=True)
+    core = place % 2
+    half = count // 2
+    groups = [[side + 2 * step for step in range(half)] for side in range(2)]
+    mine = lax.all_gather(out_weight, "seq", axis_index_groups=groups)
+    other = lax.ppermute(mine, "seq", [(i, i ^ 1) for i in range(count)])
     grad_full = lax.all_gather(grad_out, "ch", axis=1, tiled=True)
+    grad_split = grad_full.reshape(tok_rows, half, 2, chan_width)
+    grad_mine = lax.dynamic_index_in_dim(grad_split, core, 2, False)
+    grad_other = lax.dynamic_index_in_dim(grad_split, 1 - core, 2, False)
 
     streams = jnp.stack([query, key, value])
     before = from_behind(streams[:, tok_rows - (tap_count - 1) :, :], "seq", 1)
@@ -55,39 +62,44 @@
     fwd_sums = prefix(lower, grow, gated)
     fwd_final = shrink[tok_rows - 1] * fwd_sums[tok_rows - 1]
 
-    grad_mixer = lax.dot_general(
-        grad_full, columns, (((1,), (1,)), ((), ())), preferred_element_type=jnp.float32
-    )
+    grad_mixer = jnp.einsum(
+        "tzc,zrc->tr", grad_mine, mine, preferred_element_type=jnp.float32
+    ) + jnp.einsum("tzc,zrc->tr", grad_other, other, preferred_element_type=jnp.float32)
     grad_long = grad_mixer * q_short
     bwd_sums = prefix(upper, shrink, grad_long)
     bwd_final = bwd_sums[0]
 
-    finals = jnp.stack([fwd_final, bwd_final]).astype(jnp.bfloat16)
-    gathered = lax.all_gather(finals, "seq").astype(jnp.float32)
-    source = jnp.arange(count)
-    fwd_gap = place - 1 - source
-    bwd_gap = source - place - 1
-    fwd_weight = jnp.where(
-        (fwd_gap >= 0)[:, None, None],
-        jnp.exp(-decay_rate[None] * (tok_rows * jnp.maximum(fwd_gap, 0)).astype(jnp.float32)[:, None, None]),
-        0.0,
-    )
-    bwd_weight = jnp.where(
-        (bwd_gap >= 0)[:, None, None],
-        jnp.exp(-decay_rate[None] * (tok_rows * jnp.maximum(bwd_gap, 0)).astype(jnp.float32)[:, None, None]),
-        0.0,
-    )
-    fwd_entry = jnp.sum(fwd_weight * gathered[:, 0], axis=0) * one_step
-    bwd_entry = jnp.sum(bwd_weight * gathered[:, 1], axis=0) * block_decay
+    def shift(block, distance):
+        route = [(i, i + distance) for i in range(count) if 0 <= i + distance < count]
+        return lax.ppermute(block, "seq", route)
+
+    def entering(final, direction):
+        state = shift(final, direction)
+        distance = 1
+        while distance < count:
+            jump = jnp.exp(-decay_rate * float(tok_rows * distance))
+            state = state + jump * shift(state, direction * distance)
+            distance *= 2
+        return state
+
+    fwd_entry = entering(fwd_final, 1) * one_step
+    bwd_entry = entering(bwd_final, -1) * block_decay
 
     long_out = (
         jnp.sum(scaled_shrink * (fwd_sums + fwd_entry[None]), axis=1) + skip_gain[None, :] * gated
     )
     mixer = (q_short * long_out).astype(jnp.bfloat16)
-    partial_value = jnp.dot(mixer, columns, preferred_element_type=jnp.float32)
-    mixed = lax.psum_scatter(
-        partial_value.astype(jnp.bfloat16), "ch", scatter_dimension=1, tiled=True
-    )
+    part_mine = jnp.einsum("tr,zrc->ztc", mixer, mine, preferred_element_type=jnp.float32)
+    part_other = jnp.einsum("tr,zrc->ztc", mixer, other, preferred_element_type=jnp.float32)
+    part_mine = part_mine.astype(jnp.bfloat16)
+    part_other = part_other.astype(jnp.bfloat16)
+    parts = jnp.where(
+        core == 0,
+        jnp.stack([part_mine, part_other], axis=1),
+        jnp.stack([part_other, part_mine], axis=1),
+    ).reshape(count, tok_rows, chan_width)
+    received = lax.all_to_all(parts, "ch", 0, 0, tiled=True)
+    mixed = jnp.sum(received.astype(jnp.float32), axis=0).astype(jnp.bfloat16)
 
     grad_qshort = grad_mixer * long_out
     grad_gated = (

time: 272 us -> 277 us (1.018)
  the two profiles are of different devices: /device:TPU:65 before, /device:TPU:161 now
where the time goes in v2:
time: 277 us; the launch traced here: 274 us
  waiting for transfers between devices  147 us (53%)
  starting transfers between devices  53.3 us (19%)
  local copies, waits for them, and re-layouts  31.8 us (11%)
  matrix products  15.4 us (6%)
  between operations  14.8 us (5%)
  other arithmetic  11.1 us (4%)
    all_gather x1, waiting for transfers between devices, per_device(): mine = lax.all_gather(out_weight, 'seq', axis_index_groups=groups)  55.2 us
    all_gather x1, waiting for transfers between devices, per_device(): grad_full = lax.all_gather(grad_out, 'ch', axis=1, tiled=True)  47.1 us
    ppermute x10, starting transfers between devices, shift(): return lax.ppermute(block, 'seq', route)  43.7 us
    all_to_all x1, waiting for transfers between devices, per_device(): received = lax.all_to_all(parts, 'ch', 0, 0, tiled=True)  27.9 us
    unnamed x30, local copies, waits for them, and re-layouts  19.7 us
    ppermute x10, waiting for transfers between devices, shift(): return lax.ppermute(block, 'seq', route)  12.1 us
    dot_general x2, matrix products, prefix(): jnp.dot(tri, spread, precision=highest, preferred_element_type=jnp.float32)  6.19 us
  transfers between devices with their start and end apart: 16, of which 12 were waited for; matrix products, arithmetic and copies ran while one was open for 10% of the time, Pallas kernels for 0%

profile of v2, /device:TPU:161, one launch (start us, length us, event | category | flops | bytes accessed | tf_op | source)
XLA Modules:
  0.0 273.7 jit_solution(9001503624924707344)
XLA Ops:
  8.7 55.2 %all-gather.6.cloned.1.call-done = bf16[4096,512]{1,0:T(8,128)(2,1)} async-done(((bf16[512,512]{1,0:T(8,128)(2,1)}), bf16[4096,512]{1,0:T(8,128)(2,1)}) %all-gather.6.cloned.1.call-update) | async-done | bytes 4194320 | tf_op jit(solution)/shard_map/all_gather | solution.py:24
  71.6 47.1 %all-gather.4.cloned.1.call-done = bf16[128,8192]{1,0:T(8,128)(2,1)} async-done(((bf16[128,512]{1,0:T(8,128)(2,1)}), bf16[128,8192]{1,0:T(8,128)(2,1)}) %all-gather.4.cloned.1.call-update) | async-done | bytes 2097168 | tf_op jit(solution)/shard_map/all_gather | solution.py:26
  118.7 3.8 %reshape.58 = bf16[128,8,2,512]{3,2,1,0:T(2,128)(2,1)S(1)} reshape(bf16[128,8192]{1,0:T(8,128)(2,1)} %all-gather.4.cloned.1.call-done) | data formatting | bytes 4194304 | tf_op jit(solution)/shard_map/reshape | solution.py:27
  122.5 4.9 %constant_dynamic-slice_fusion = (bf16[128,8,1,512]{3,2,1,0:T(2,128)(2,1)S(1)}, bf16[128,8,1,512]{3,2,1,0:T(2,128)(2,1)S(1)}) fusion(bf16[128,8,2,512]{3,2,1,0:T(2,128)(2,1)S(1)} %reshape.58, s32[]{:T(128)S(6)} %select_n.31, s32[]{:T(128)S(6)} %select_n.30), kind=kLoop, calls=%fused_computation.82 | loop fusion | bytes 4194312 | tf_op jit(solution)/shard_map/jit(dynamic_index_in_dim)/dynamic_slice | solution.py:29
  129.0 3.9 %fusion.25 = (f32[128,512]{1,0:T(8,128)S(1)}, f32[128,512]{1,0:T(8,128)S(1)}, f32[128,512]{1,0:T(8,128)S(1)}) fusion(f32[3,128,512]{2,1,0:T(8,128)S(1)} %fusion.22, f32[128,512]{1,0:T(8,128)S(1)} %convolution_bitcast_fusion.1, bf16[8,512,512]{2,1,0:T(8,128)(2,1)} %collective-permute-done.6, bf16[128,8,1,512]{3,2,1,0:T(2,128)(2,1)S(1)} %get-tuple-element.6), kind=kOutput, calls=%fused_computation.52 | convolution fusion | flops 537067520 | bytes 7077888 | tf_op jit(solution)/shard_map/tzc,zrc->tr/dot_general | solution.py:67
  133.4 3.4 %copy.21 = f32[16,8,16,512]{3,1,2,0:T(8,128)S(1)} copy(f32[16,8,16,512]{3,2,1,0:T(8,128)S(1)} %bitcast.107) | data formatting | bytes 8388608
  136.9 3.2 %fusion.8 = f32[128,8192]{1,0:T(8,128)S(1)} fusion(f32[128,8192]{1,0:T(8,128)S(1)} %bitcast.106, f32[128]{0:T(128)S(1)} %iota_convert_fusion, f32[8192]{0:T(1024)S(1)} %bitcast.117), kind=kOutput, calls=%fused_computation.10 | convolution fusion | flops 1612726272 | bytes 8421888 | tf_op jit(solution)/shard_map/dot_general | solution.py:59
  142.8 3.7 %collective-permute-start.1 = (f32[16,512]{1,0:T(8,128)S(1)}, f32[16,512]{1,0:T(8,128)S(1)}, u32[]{:S(2)}, u32[]{:S(2)}) collective-permute-start(f32[16,512]{1,0:T(8,128)S(1)} %fusion.27), channel_id=1, source_target_pairs={{0,16},{16,32},{32,48},{48,64},{64,80},{80,96},{96,112},{112,128},... | collective-permute-start | bytes 98312 | tf_op jit(solution)/shard_map/ppermute | solution.py:74
  147.6 4.2 %collective-permute-start.2 = (f32[16,512]{1,0:T(8,128)S(1)}, f32[16,512]{1,0:T(8,128)S(1)}, u32[]{:S(2)}, u32[]{:S(2)}) collective-permute-start(f32[16,512]{1,0:T(8,128)S(1)} %collective-permute-done.1), channel_id=1, source_target_pairs={{0,16},{16,32},{32,48},{48,64},{64,80},{80,96},{96,112},{112,128},... | collective-permute-start | bytes 98312 | tf_op jit(solution)/shard_map/ppermute | solution.py:74
  155.1 2.6 collective-permute-done.3
  160.2 3.4 %copy.24 = f32[16,8,16,512]{3,1,2,0:T(8,128)S(1)} copy(f32[16,8,16,512]{3,2,1,0:T(8,128)S(1)} %bitcast.108) | data formatting | bytes 8388608
  165.0 3.0 %fusion.4 = f32[128,8192]{1,0:T(8,128)S(1)} fusion(f32[128,8192]{1,0:T(8,128)S(1)} %bitcast.105, f32[8192]{0:T(1024)S(1)} %bitcast.118, f32[128]{0:T(128)S(1)} %iota_convert_fusion), kind=kOutput, calls=%fused_computation.6 | convolution fusion | flops 1612726272 | bytes 8421888 | tf_op jit(solution)/shard_map/dot_general | solution.py:59
  170.1 7.3 %collective-permute-start.7 = (f32[16,512]{1,0:T(8,128)S(1)}, f32[16,512]{1,0:T(8,128)S(1)}, u32[]{:S(2)}, u32[]{:S(2)}) collective-permute-start(f32[16,512]{1,0:T(8,128)S(1)} %squeeze.41), channel_id=1, source_target_pairs={{16,0},{32,16},{48,32},{64,48},{80,64},{96,80},{112,96},{128,112},... | collective-permute-start | bytes 98312 | tf_op jit(solution)/shard_map/ppermute | solution.py:74
  181.1 3.3 %collective-permute-done.8 = f32[16,512]{1,0:T(8,128)S(1)} collective-permute-done((f32[16,512]{1,0:T(8,128)S(1)}, f32[16,512]{1,0:T(8,128)S(1)}, u32[]{:S(2)}, u32[]{:S(2)}) %collective-permute-start.8) | collective-permute-done | bytes 32800 | tf_op jit(solution)/shard_map/ppermute | solution.py:74
  184.4 3.9 %collective-permute-start.9 = (f32[16,512]{1,0:T(8,128)S(1)}, f32[16,512]{1,0:T(8,128)S(1)}, u32[]{:S(2)}, u32[]{:S(2)}) collective-permute-start(f32[16,512]{1,0:T(8,128)S(1)} %multiply_add_fusion.4), channel_id=1, source_target_pairs={{32,0},{48,16},{64,32},{80,48},{96,64},{112,80},{128,96},{144,112}... | collective-permute-start | bytes 98312 | tf_op jit(solution)/shard_map/ppermute | solution.py:74
  189.4 9.1 %collective-permute-start.10 = (f32[16,512]{1,0:T(8,128)S(1)}, f32[16,512]{1,0:T(8,128)S(1)}, u32[]{:S(2)}, u32[]{:S(2)}) collective-permute-start(f32[16,512]{1,0:T(8,128)S(1)} %multiply_add_fusion.3), channel_id=1, source_target_pairs={{64,0},{80,16},{96,32},{112,48},{128,64},{144,80},{160,96},{176,11... | collective-permute-start | bytes 98312 | tf_op jit(solution)/shard_map/ppermute | solution.py:74
  199.8 8.1 %collective-permute-start.11 = (f32[16,512]{1,0:T(8,128)S(1)}, f32[16,512]{1,0:T(8,128)S(1)}, u32[]{:S(2)}, u32[]{:S(2)}) collective-permute-start(f32[16,512]{1,0:T(8,128)S(1)} %multiply_add_fusion.2), channel_id=1, source_target_pairs={{128,0},{144,16},{160,32},{176,48},{192,64},{208,80},{224,96},{240... | collective-permute-start | bytes 98312 | tf_op jit(solution)/shard_map/ppermute | solution.py:74
  208.0 5.6 %copy.22 = f32[16,8,16,512]{3,2,1,0:T(8,128)S(1)} copy(f32[16,8,16,512]{3,1,2,0:T(8,128)} %bitcast.100) | data formatting | bytes 8388608
  213.6 3.3 %copy.25 = f32[16,8,16,512]{3,2,1,0:T(8,128)S(1)} copy(f32[16,8,16,512]{3,1,2,0:T(8,128)S(1)} %bitcast.101) | data formatting | bytes 8388608
  217.0 3.8 %fusion.1 = (f32[128,512]{1,0:T(8,128)S(1)}, f32[128,512]{1,0:T(8,128)S(1)}) fusion(f32[16,8,16,512]{3,2,1,0:T(8,128)S(1)} %copy.25, f32[16,512]{1,0:T(8,128)S(1)} %get-tuple-element.18, f32[16,512]{1,0:T(8,128)S(1)} %copy-done.5, f32[128]{0:T(128)S(1)} %iota_convert_fusion, f32[16,512]{1,0:T(8,128)S(1)} %get-tuple-element.19, ...), kind=kLoop, calls=%fused_computation.2 | loop fusion | flops 10354688 | bytes 9077248 | tf_op jit(solution)/shard_map/reduce_sum | solution.py:106
  221.8 2.9 %fusion.17 = bf16[8,1,128,512]{3,2,0,1:T(8,128)(2,1)S(1)} fusion(bf16[128,512,1]{1,0,2:T(8,128)(2,1)S(1)} %get-tuple-element.10, bf16[8,512,512]{2,1,0:T(8,128)(2,1)} %collective-permute-done.6), kind=kOutput, calls=%fused_computation.23 | convolution fusion | flops 537395200 | bytes 5373952 | tf_op jit(solution)/shard_map/tr,zrc->ztc/dot_general | solution.py:93
  226.6 4.7 %all-to-all-start = ((bf16[16,128,512]{2,1,0:T(8,128)(2,1)}), bf16[16,128,512]{2,1,0:T(8,128)(2,1)S(1)}, u32[]{:S(2)}, u32[]{:S(2)}) async-start(bf16[16,128,512]{2,1,0:T(8,128)(2,1)} %bitcast.109), calls=%async_computation | async-start | bytes 4194304 | tf_op jit(solution)/shard_map/all_to_all | solution.py:101
  233.3 3.4 %collective-permute-done.12 = f32[3,2,512]{2,1,0:T(2,128)S(1)} collective-permute-done((f32[3,2,512]{2,1,0:T(2,128)S(1)}, f32[3,2,512]{2,1,0:T(2,128)S(1)}, u32[]{:S(2)}, u32[]{:S(2)}) %collective-permute-start.12) | collective-permute-done | bytes 12320 | tf_op jit(solution)/shard_map/ppermute | solution.py:10
  237.7 27.9 %all-to-all-done = bf16[16,128,512]{2,1,0:T(8,128)(2,1)S(1)} async-done(((bf16[16,128,512]{2,1,0:T(8,128)(2,1)}), bf16[16,128,512]{2,1,0:T(8,128)(2,1)S(1)}, u32[]{:S(2)}, u32[]{:S(2)}) %all-to-all-start) | async-done | bytes 2097184 | tf_op jit(solution)/shard_map/all_to_all | solution.py:101
  (79 shorter events, 37.2 us)
Async XLA Ops:
  7.2 64.1 %copy-start.6 = (bf16[128,512]{1,0:T(8,128)(2,1)S(1)}, bf16[128,512]{1,0:T(8,128)(2,1)}, u32[]{:S(2)}) copy-start(bf16[128,512]{1,0:T(8,128)(2,1)} %param.11) | copy-start | bytes 393220
  7.2 64.1 %copy-start.7 = (bf16[128,512]{1,0:T(8,128)(2,1)S(1)}, bf16[128,512]{1,0:T(8,128)(2,1)}, u32[]{:S(2)}) copy-start(bf16[128,512]{1,0:T(8,128)(2,1)} %param.10) | copy-start | bytes 393220
  7.2 64.1 %copy-start.8 = (bf16[128,512]{1,0:T(8,128)(2,1)S(1)}, bf16[128,512]{1,0:T(8,128)(2,1)}, u32[]{:S(2)}) copy-start(bf16[128,512]{1,0:T(8,128)(2,1)} %param.9) | copy-start | bytes 393220
  7.2 63.7 %copy-start.5 = (f32[16,512]{1,0:T(8,128)S(1)}, f32[16,512]{1,0:T(8,128)}, u32[]{:S(2)}) copy-start(f32[16,512]{1,0:T(8,128)} %param.13) | copy-start | bytes 98308
  7.2 63.7 %copy-start.10 = (f32[3,3,512]{2,1,0:T(4,128)S(1)}, f32[3,3,512]{2,1,0:T(4,128)}, u32[]{:S(2)}) copy-start(f32[3,3,512]{2,1,0:T(4,128)} %param.12) | copy-start | bytes 55300
  7.2 56.7 %all-gather.6.cloned.1.call-start = ((), (), s32[]{:S(2)}) async-start(), calls=%async_computation.2 | async-start | bytes 4718592 | tf_op jit(solution)/shard_map/all_gather | solution.py:24
  8.0 110.7 %all-gather.4.cloned.1.call-start = ((), (), s32[]{:S(2)}) async-start(), calls=%async_computation.1 | async-start | bytes 2228224 | tf_op jit(solution)/shard_map/all_gather | solution.py:26
  63.9 65.0 %collective-permute-start.6 = (bf16[8,512,512]{2,1,0:T(8,128)(2,1)}, bf16[8,512,512]{2,1,0:T(8,128)(2,1)}, u32[]{:S(2)}, u32[]{:S(2)}) collective-permute-start(bf16[8,512,512]{2,1,0:T(8,128)(2,1)} %bitcast.102), channel_id=1, source_target_pairs={{0,16},{16,0},{32,48},{48,32},{64,80},{80,64},{96,112},{112,96},{1... | collective-permute-start | bytes 12582920 | tf_op jit(solution)/shard_map/ppermute | solution.py:25
  65.3 5.9 %collective-permute-start = (bf16[3,2,512]{2,1,0:T(2,128)(2,1)S(1)}, bf16[3,2,512]{2,1,0:T(2,128)(2,1)S(1)}, u32[]{:S(2)}, u32[]{:S(2)}) collective-permute-start(bf16[3,2,512]{2,1,0:T(2,128)(2,1)S(1)} %pad_maximum_fusion.2), channel_id=1, source_target_pairs={{0,16},{16,32},{32,48},{48,64},{64,80},{80,96},{96,112},{112,128},... | collective-permute-start | bytes 18440 | tf_op jit(solution)/shard_map/ppermute | solution.py:10
  122.5 4.9 %copy-start.3 = (bf16[4096,512]{1,0:T(8,128)(2,1)S(1)}, bf16[4096,512]{1,0:T(8,128)(2,1)}, u32[]{:S(2)}) copy-start(bf16[4096,512]{1,0:T(8,128)(2,1)} %all-gather.6.cloned.1.call-done) | copy-start | bytes 12582916
  142.8 4.7 %collective-permute-start.1 = (f32[16,512]{1,0:T(8,128)S(1)}, f32[16,512]{1,0:T(8,128)S(1)}, u32[]{:S(2)}, u32[]{:S(2)}) collective-permute-start(f32[16,512]{1,0:T(8,128)S(1)} %fusion.27), channel_id=1, source_target_pairs={{0,16},{16,32},{32,48},{48,64},{64,80},{80,96},{96,112},{112,128},... | collective-permute-start | bytes 98312 | tf_op jit(solution)/shard_map/ppermute | solution.py:74
  147.6 5.2 %collective-permute-start.2 = (f32[16,512]{1,0:T(8,128)S(1)}, f32[16,512]{1,0:T(8,128)S(1)}, u32[]{:S(2)}, u32[]{:S(2)}) collective-permute-start(f32[16,512]{1,0:T(8,128)S(1)} %collective-permute-done.1), channel_id=1, source_target_pairs={{0,16},{16,32},{32,48},{48,64},{64,80},{80,96},{96,112},{112,128},... | collective-permute-start | bytes 98312 | tf_op jit(solution)/shard_map/ppermute | solution.py:74
  152.8 4.9 %collective-permute-start.3 = (f32[16,512]{1,0:T(8,128)S(1)}, f32[16,512]{1,0:T(8,128)S(1)}, u32[]{:S(2)}, u32[]{:S(2)}) collective-permute-start(f32[16,512]{1,0:T(8,128)S(1)} %multiply_add_fusion.7), channel_id=1, source_target_pairs={{0,32},{16,48},{32,64},{48,80},{64,96},{80,112},{96,128},{112,144}... | collective-permute-start | bytes 98312 | tf_op jit(solution)/shard_map/ppermute | solution.py:74
  157.8 7.3 %collective-permute-start.4 = (f32[16,512]{1,0:T(8,128)S(1)}, f32[16,512]{1,0:T(8,128)S(1)}, u32[]{:S(2)}, u32[]{:S(2)}) collective-permute-start(f32[16,512]{1,0:T(8,128)S(1)} %multiply_add_fusion.6), channel_id=1, source_target_pairs={{0,64},{16,80},{32,96},{48,112},{64,128},{80,144},{96,160},{112,17... | collective-permute-start | bytes 98312 | tf_op jit(solution)/shard_map/ppermute | solution.py:74
  170.1 9.0 %collective-permute-start.7 = (f32[16,512]{1,0:T(8,128)S(1)}, f32[16,512]{1,0:T(8,128)S(1)}, u32[]{:S(2)}, u32[]{:S(2)}) collective-permute-start(f32[16,512]{1,0:T(8,128)S(1)} %squeeze.41), channel_id=1, source_target_pairs={{16,0},{32,16},{48,32},{64,48},{80,64},{96,80},{112,96},{128,112},... | collective-permute-start | bytes 98312 | tf_op jit(solution)/shard_map/ppermute | solution.py:74
  179.2 5.2 %collective-permute-start.8 = (f32[16,512]{1,0:T(8,128)S(1)}, f32[16,512]{1,0:T(8,128)S(1)}, u32[]{:S(2)}, u32[]{:S(2)}) collective-permute-start(f32[16,512]{1,0:T(8,128)S(1)} %collective-permute-done.7), channel_id=1, source_target_pairs={{16,0},{32,16},{48,32},{64,48},{80,64},{96,80},{112,96},{128,112},... | collective-permute-start | bytes 98312 | tf_op jit(solution)/shard_map/ppermute | solution.py:74
  184.4 4.9 %collective-permute-start.9 = (f32[16,512]{1,0:T(8,128)S(1)}, f32[16,512]{1,0:T(8,128)S(1)}, u32[]{:S(2)}, u32[]{:S(2)}) collective-permute-start(f32[16,512]{1,0:T(8,128)S(1)} %multiply_add_fusion.4), channel_id=1, source_target_pairs={{32,0},{48,16},{64,32},{80,48},{96,64},{112,80},{128,96},{144,112}... | collective-permute-start | bytes 98312 | tf_op jit(solution)/shard_map/ppermute | solution.py:74
  189.4 10.4 %collective-permute-start.10 = (f32[16,512]{1,0:T(8,128)S(1)}, f32[16,512]{1,0:T(8,128)S(1)}, u32[]{:S(2)}, u32[]{:S(2)}) collective-permute-start(f32[16,512]{1,0:T(8,128)S(1)} %multiply_add_fusion.3), channel_id=1, source_target_pairs={{64,0},{80,16},{96,32},{112,48},{128,64},{144,80},{160,96},{176,11... | collective-permute-start | bytes 98312 | tf_op jit(solution)/shard_map/ppermute | solution.py:74
  198.5 18.4 %collective-permute-start.5 = (f32[16,512]{1,0:T(8,128)S(1)}, f32[16,512]{1,0:T(8,128)S(1)}, u32[]{:S(2)}, u32[]{:S(2)}) collective-permute-start(f32[16,512]{1,0:T(8,128)S(1)} %get-tuple-element.20), channel_id=1, source_target_pairs={{0,128},{16,144},{32,160},{48,176},{64,192},{80,208},{96,224},{112... | collective-permute-start | bytes 98312 | tf_op jit(solution)/shard_map/ppermute | solution.py:74
  199.8 17.0 %collective-permute-start.11 = (f32[16,512]{1,0:T(8,128)S(1)}, f32[16,512]{1,0:T(8,128)S(1)}, u32[]{:S(2)}, u32[]{:S(2)}) collective-permute-start(f32[16,512]{1,0:T(8,128)S(1)} %multiply_add_fusion.2), channel_id=1, source_target_pairs={{128,0},{144,16},{160,32},{176,48},{192,64},{208,80},{224,96},{240... | collective-permute-start | bytes 98312 | tf_op jit(solution)/shard_map/ppermute | solution.py:74
  207.9 5.6 %copy-start.2 = (f32[128,8192]{1,0:T(8,128)S(1)}, f32[128,8192]{1,0:T(8,128)}, u32[]{:S(2)}) copy-start(f32[128,8192]{1,0:T(8,128)} %copy-done.1) | copy-start | bytes 12582916
  216.9 4.1 %copy-start.4 = (bf16[4096,512]{1,0:T(8,128)(2,1)S(1)}, bf16[4096,512]{1,0:T(8,128)(2,1)}, u32[]{:S(2)}) copy-start(bf16[4096,512]{1,0:T(8,128)(2,1)} %all-gather.6.cloned.1.call-done) | copy-start | bytes 12582916
  226.6 39.1 %all-to-all-start = ((bf16[16,128,512]{2,1,0:T(8,128)(2,1)}), bf16[16,128,512]{2,1,0:T(8,128)(2,1)S(1)}, u32[]{:S(2)}, u32[]{:S(2)}) async-start(bf16[16,128,512]{2,1,0:T(8,128)(2,1)} %bitcast.109), calls=%async_computation | async-start | bytes 4194304 | tf_op jit(solution)/shard_map/all_to_all | solution.py:101
  231.3 5.3 %collective-permute-start.12 = (f32[3,2,512]{2,1,0:T(2,128)S(1)}, f32[3,2,512]{2,1,0:T(2,128)S(1)}, u32[]{:S(2)}, u32[]{:S(2)}) collective-permute-start(f32[3,2,512]{2,1,0:T(2,128)S(1)} %slice.90), channel_id=1, source_target_pairs={{16,0},{32,16},{48,32},{64,48},{80,64},{96,80},{112,96},{128,112},... | collective-permute-start | bytes 36872 | tf_op jit(solution)/shard_map/ppermute | solution.py:10
  (4 other events, 11.1 us)
Sparse Core Ops, SparseCore 0:
  9.8 54.0 all-gather.5
  66.3 52.3 all-gather.3

commit v3 on v2

v3 whole, which is shorter than its diff:
```python
import jax
import jax.numpy as jnp
from jax import lax
from jax.sharding import PartitionSpec as P


def per_device(query, key, value, short_taps, decay_rate, residue, skip_gain, out_weight, grad_out):
    tok_rows, chan_width = query.shape
    tap_count = short_taps.shape[0]
    mode_count = decay_rate.shape[0]
    highest = lax.Precision.HIGHEST
    count = lax.axis_size("seq")
    lanes = lax.axis_size("ch")
    place = lax.axis_index("seq")
    core = place % 2
    half = count // 2

    def shift(block, distance):
        route = [(i, i + distance) for i in range(count) if 0 <= i + distance < count]
        return lax.ppermute(block, "seq", route)

    def transpose(block):
        route = [(j * lanes + k, k * lanes + j) for j in range(count) for k in range(lanes)]
        return lax.ppermute(block, ("seq", "ch"), route)

    grad_cols = lax.all_gather(transpose(grad_out), "ch", axis=0, tiled=True)

    streams = jnp.stack([query, key, value])
    before = shift(streams[:, tok_rows - (tap_count - 1) :, :], 1)
    extended = jnp.concatenate([before, streams], axis=1).astype(jnp.float32)
    featured = jnp.zeros((3, tok_rows, chan_width), jnp.float32)
    for tap_index in range(tap_count):
        begin = tap_count - 1 - tap_index
        featured = (
            featured + short_taps[tap_index][:, None, :] * extended[:, begin : begin + tok_rows, :]
        )
    q_short = featured[0]
    k_short = featured[1]
    v_short = featured[2]
    gated = k_short * v_short

    mode_scale = residue * jnp.sqrt(-jnp.expm1(-2.0 * decay_rate))
    offsets = jnp.arange(tok_rows).astype(jnp.float32)
    shrink = jnp.exp(-decay_rate[None, :, :] * offsets[:, None, None])
    grow = jnp.exp(decay_rate[None, :, :] * offsets[:, None, None])
    one_step = jnp.exp(-decay_rate)
    block_decay = jnp.exp(-decay_rate * tok_rows)
    rows = jnp.arange(tok_rows)
    lower = (rows[:, None] >= rows[None, :]).astype(jnp.float32)
    upper = (rows[:, None] <= rows[None, :]).astype(jnp.float32)

    def prefix(tri, weights, signal):
        spread = (weights * signal[:, None, :]).reshape(tok_rows, mode_count * chan_width)
        summed = jnp.dot(tri, spread, precision=highest, preferred_element_type=jnp.float32)
        return summed.reshape(tok_rows, mode_count, chan_width)

    def entering(final, direction):
        state = shift(final, direction)
        distance = 1
        while distance < count:
            jump = jnp.exp(-decay_rate * float(tok_rows * distance))
            state = state + jump * shift(state, direction * distance)
            distance *= 2
        return state

    fwd_sums = prefix(lower, grow, gated)
    fwd_entry = entering(shrink[tok_rows - 1] * fwd_sums[tok_rows - 1], 1) * one_step
    long_out = (
        jnp.sum((mode_scale[None] * shrink) * (fwd_sums + fwd_entry[None]), axis=1)
        + skip_gain[None, :] * gated
    )
    mixer = (q_short * long_out).astype(jnp.bfloat16)

    groups = [[side + 2 * step for step in range(half)] for side in range(2)]
    mine = lax.all_gather(mixer, "seq", axis_index_groups=groups)
    other = lax.ppermute(mine, "seq", [(i, i ^ 1) for i in range(count)])
    part_mine = jnp.einsum("ztr,rc->ztc", mine, out_weight, preferred_element_type=jnp.float32)
    part_other = jnp.einsum("ztr,rc->ztc", other, out_weight, preferred_element_type=jnp.float32)
    part_mine = part_mine.astype(jnp.bfloat16)
    part_other = part_other.astype(jnp.bfloat16)
    parts = jnp.where(
        core == 0,
        jnp.stack([part_mine, part_other], axis=1),
        jnp.stack([part_other, part_mine], axis=1),
    ).reshape(count, tok_rows, chan_width)
    received = lax.all_to_all(parts, "ch", 0, 0, tiled=True)
    mixed = transpose(jnp.sum(received.astype(jnp.float32), axis=0).astype(jnp.bfloat16))

    partial_grad = lax.dot_general(
        grad_cols, out_weight, (((1,), (1,)), ((), ())), preferred_element_type=jnp.float32
    )
    partial_grad = partial_grad.astype(jnp.bfloat16).reshape(count, tok_rows, chan_width)
    grad_parts = lax.all_to_all(partial_grad, "seq", 0, 0, tiled=True)
    grad_mixer = jnp.sum(grad_parts.astype(jnp.float32), axis=0)

    grad_qshort = grad_mixer * long_out
    grad_long = grad_mixer * q_short
    bwd_sums = prefix(upper, shrink, grad_long)
    bwd_entry = entering(bwd_sums[0], -1) * block_decay
    grad_gated = (
        jnp.sum((mode_scale[None] * grow) * (bwd_sums + bwd_entry[None]), axis=1)
        + skip_gain[None, :] * grad_long
    )
    grad_stack = jnp.stack([grad_qshort, grad_gated * v_short, grad_gated * k_short])
    after = shift(grad_stack[:, : tap_count - 1, :], -1)
    extended_back = jnp.concatenate([grad_stack, after], axis=1)
    grads = jnp.zeros((3, tok_rows, chan_width), jnp.float32)
    for tap_index in range(tap_count):
        grads = (
            grads
            + short_taps[tap_index][:, None, :]
            * extended_back[:, tap_index : tap_index + tok_rows, :]
        )
    grads = grads.astype(jnp.bfloat16)
    return (mixed, grads[0], grads[1], grads[2])


def solution(mesh):
    in_specs = (
        P("seq", "ch"),
        P("seq", "ch"),
        P("seq", "ch"),
        P(None, None, "ch"),
        P(None, "ch"),
        P(None, "ch"),
        P("ch"),
        P("ch", "seq"),
        P("seq", "ch"),
    )
    out_specs = (P("seq", "ch"), P("seq", "ch"), P("seq", "ch"), P("seq", "ch"))
    return jax.shard_map(
        per_device, mesh=mesh, in_specs=in_specs, out_specs=out_specs, check_vma=False
    )
```

time: 277 us -> 342 us (1.23)
  the two profiles are of different devices: /device:TPU:161 before, /device:TPU:65 now
where the time goes in v3:
time: 342 us; the launch traced here: 337 us
  waiting for transfers between devices  197 us (58%)
  starting transfers between devices  73.7 us (22%)
  local copies, waits for them, and re-layouts  25.3 us (7%)
  between operations  14.7 us (4%)
  other arithmetic  13.4 us (4%)
  matrix products  12.9 us (4%)
    all_gather x1, waiting for transfers between devices, per_device(): grad_cols = lax.all_gather(transpose(grad_out), 'ch', axis=0, tiled=True)  61.2 us
    ppermute x12, waiting for transfers between devices, shift(): return lax.ppermute(block, 'seq', route)  56.8 us
    ppermute x12, starting transfers between devices, shift(): return lax.ppermute(block, 'seq', route)  47.6 us
    all_gather x1, waiting for transfers between devices, per_device(): mine = lax.all_gather(mixer, 'seq', axis_index_groups=groups)  35.4 us
    all_to_all x1, waiting for transfers between devices, per_device(): received = lax.all_to_all(parts, 'ch', 0, 0, tiled=True)  22.3 us
    unnamed x47, local copies, waits for them, and re-layouts  21.8 us
    ppermute x2, waiting for transfers between devices, transpose(): return lax.ppermute(block, ('seq', 'ch'), route)  20.7 us
    all_to_all x1, starting transfers between devices, per_device(): grad_parts = lax.all_to_all(partial_grad, 'seq', 0, 0, tiled=True)  8.69 us
  transfers between devices with their start and end apart: 19, of which 15 were waited for; matrix products, arithmetic and copies ran while one was open for 8% of the time, Pallas kernels for 0%

profile of v3, /device:TPU:65, one launch (start us, length us, event | category | flops | bytes accessed | tf_op | source)
XLA Modules:
  0.0 336.9 jit_solution(16510468369814847159)
XLA Ops:
  7.2 3.9 %collective-permute-start.8 = (bf16[128,512]{1,0:T(8,128)(2,1)}, bf16[128,512]{1,0:T(8,128)(2,1)S(1)}, u32[]{:S(2)}, u32[]{:S(2)}) collective-permute-start(bf16[128,512]{1,0:T(8,128)(2,1)} %param.17), channel_id=1, source_target_pairs={{0,0},{1,16},{2,32},{3,48},{4,64},{5,80},{6,96},{7,112},{8,128},{9... | collective-permute-start | bytes 393224 | tf_op jit(solution)/shard_map/ppermute | solution.py:24
  11.1 6.6 %collective-permute-done.8 = bf16[128,512]{1,0:T(8,128)(2,1)S(1)} collective-permute-done((bf16[128,512]{1,0:T(8,128)(2,1)}, bf16[128,512]{1,0:T(8,128)(2,1)S(1)}, u32[]{:S(2)}, u32[]{:S(2)}) %collective-permute-start.8) | collective-permute-done | bytes 131104 | tf_op jit(solution)/shard_map/ppermute | solution.py:24
  18.4 61.2 %all-gather.5.cloned.1.call-done = bf16[2048,512]{1,0:T(8,128)(2,1)} async-done(((bf16[128,512]{1,0:T(8,128)(2,1)}), bf16[2048,512]{1,0:T(8,128)(2,1)}) %all-gather.5.cloned.1.call-update) | async-done | bytes 2097168 | tf_op jit(solution)/shard_map/all_gather | solution.py:26
  79.6 4.2 %convolution_convert_fusion = bf16[2048,512]{1,0:T(8,128)(2,1)} fusion(bf16[2048,512]{1,0:T(8,128)(2,1)} %all-gather.5.cloned.1.call-done, bf16[512,512]{1,0:T(8,128)(2,1)S(1)} %copy-done), kind=kOutput, calls=%fused_computation.16 | convolution fusion | flops 1074790400 | bytes 4718592 | tf_op jit(solution)/shard_map/dot_general | solution.py:89
  83.9 8.7 %all-to-all-start.1 = ((bf16[16,128,512]{2,1,0:T(8,128)(2,1)}), bf16[16,128,512]{2,1,0:T(8,128)(2,1)S(1)}, u32[]{:S(2)}, u32[]{:S(2)}) async-start(bf16[16,128,512]{2,1,0:T(8,128)(2,1)} %bitcast.86), calls=%async_computation.1 | async-start | bytes 4194304 | tf_op jit(solution)/shard_map/all_to_all | solution.py:93
  98.7 39.2 %collective-permute-done = bf16[3,2,512]{2,1,0:T(2,128)(2,1)S(1)} collective-permute-done((bf16[3,2,512]{2,1,0:T(2,128)(2,1)S(1)}, bf16[3,2,512]{2,1,0:T(2,128)(2,1)S(1)}, u32[]{:S(2)}, u32[]{:S(2)}) %collective-permute-start) | collective-permute-done | bytes 6176 | tf_op jit(solution)/shard_map/ppermute | solution.py:20
  138.9 3.4 %copy.16 = f32[16,8,16,512]{3,1,2,0:T(8,128)S(1)} copy(f32[16,8,16,512]{3,2,1,0:T(8,128)S(1)} %bitcast.82) | data formatting | bytes 8388608
  148.2 4.4 %collective-permute-start.1 = (f32[16,512]{1,0:T(8,128)S(1)}, f32[16,512]{1,0:T(8,128)S(1)}, u32[]{:S(2)}, u32[]{:S(2)}) collective-permute-start(f32[16,512]{1,0:T(8,128)S(1)} %fusion.26), channel_id=1, source_target_pairs={{0,16},{16,32},{32,48},{48,64},{64,80},{80,96},{96,112},{112,128},... | collective-permute-start | bytes 98312 | tf_op jit(solution)/shard_map/ppermute | solution.py:20
  153.6 4.2 %collective-permute-start.2 = (f32[16,512]{1,0:T(8,128)S(1)}, f32[16,512]{1,0:T(8,128)S(1)}, u32[]{:S(2)}, u32[]{:S(2)}) collective-permute-start(f32[16,512]{1,0:T(8,128)S(1)} %collective-permute-done.1), channel_id=1, source_target_pairs={{0,16},{16,32},{32,48},{48,64},{64,80},{80,96},{96,112},{112,128},... | collective-permute-start | bytes 98312 | tf_op jit(solution)/shard_map/ppermute | solution.py:20
  158.8 5.8 %collective-permute-start.3 = (f32[16,512]{1,0:T(8,128)S(1)}, f32[16,512]{1,0:T(8,128)S(1)}, u32[]{:S(2)}, u32[]{:S(2)}) collective-permute-start(f32[16,512]{1,0:T(8,128)S(1)} %multiply_add_fusion.5), channel_id=1, source_target_pairs={{0,32},{16,48},{32,64},{48,80},{64,96},{80,112},{96,128},{112,144}... | collective-permute-start | bytes 98312 | tf_op jit(solution)/shard_map/ppermute | solution.py:20
  165.7 4.8 %collective-permute-start.4 = (f32[16,512]{1,0:T(8,128)S(1)}, f32[16,512]{1,0:T(8,128)S(1)}, u32[]{:S(2)}, u32[]{:S(2)}) collective-permute-start(f32[16,512]{1,0:T(8,128)S(1)} %multiply_add_fusion.4), channel_id=1, source_target_pairs={{0,64},{16,80},{32,96},{48,112},{64,128},{80,144},{96,160},{112,17... | collective-permute-start | bytes 98312 | tf_op jit(solution)/shard_map/ppermute | solution.py:20
  172.9 3.4 %copy.19 = f32[16,8,16,512]{3,1,2,0:T(8,128)S(1)} copy(f32[16,8,16,512]{3,2,1,0:T(8,128)S(1)} %bitcast.83) | data formatting | bytes 8388608
  181.5 7.5 %collective-permute-start.9 = (f32[16,512]{1,0:T(8,128)S(1)}, f32[16,512]{1,0:T(8,128)S(1)}, u32[]{:S(2)}, u32[]{:S(2)}) collective-permute-start(f32[16,512]{1,0:T(8,128)S(1)} %squeeze.26), channel_id=1, source_target_pairs={{16,0},{32,16},{48,32},{64,48},{80,64},{96,80},{112,96},{128,112},... | collective-permute-start | bytes 98312 | tf_op jit(solution)/shard_map/ppermute | solution.py:20
  195.7 3.4 %collective-permute-start.11 = (f32[16,512]{1,0:T(8,128)S(1)}, f32[16,512]{1,0:T(8,128)S(1)}, u32[]{:S(2)}, u32[]{:S(2)}) collective-permute-start(f32[16,512]{1,0:T(8,128)S(1)} %multiply_add_fusion.2), channel_id=1, source_target_pairs={{32,0},{48,16},{64,32},{80,48},{96,64},{112,80},{128,96},{144,112}... | collective-permute-start | bytes 98312 | tf_op jit(solution)/shard_map/ppermute | solution.py:20
  199.2 5.5 %collective-permute-done.11 = f32[16,512]{1,0:T(8,128)S(1)} collective-permute-done((f32[16,512]{1,0:T(8,128)S(1)}, f32[16,512]{1,0:T(8,128)S(1)}, u32[]{:S(2)}, u32[]{:S(2)}) %collective-permute-start.11) | collective-permute-done | bytes 32800 | tf_op jit(solution)/shard_map/ppermute | solution.py:20
  206.6 6.1 %collective-permute-start.5 = (f32[16,512]{1,0:T(8,128)S(1)}, f32[16,512]{1,0:T(8,128)S(1)}, u32[]{:S(2)}, u32[]{:S(2)}) collective-permute-start(f32[16,512]{1,0:T(8,128)S(1)} %get-tuple-element.18), channel_id=1, source_target_pairs={{0,128},{16,144},{32,160},{48,176},{64,192},{80,208},{96,224},{112... | collective-permute-start | bytes 98312 | tf_op jit(solution)/shard_map/ppermute | solution.py:20
  214.2 5.6 %copy.17 = f32[16,8,16,512]{3,2,1,0:T(8,128)S(1)} copy(f32[16,8,16,512]{3,1,2,0:T(8,128)} %bitcast.78) | data formatting | bytes 8388608
  223.2 3.8 %fusion.1 = (f32[128,512]{1,0:T(8,128)S(1)}, f32[128,512]{1,0:T(8,128)S(1)}) fusion(f32[16,8,16,512]{3,2,1,0:T(8,128)S(1)} %copy.20, f32[16,512]{1,0:T(8,128)S(1)} %get-tuple-element.16, f32[16,512]{1,0:T(8,128)S(1)} %copy-done.6, f32[128]{0:T(128)S(1)} %copy-done.18, f32[16,512]{1,0:T(8,128)S(1)} %get-tuple-element.17, f32[16,512]{1,0:T(8,128)S(1)} %get-tuple-element.15, ...), kind=kLoop, calls=%fused_computation.2 | loop fusion | flops 10354688 | bytes 9077248 | tf_op jit(solution)/shard_map/reduce_sum | solution.py:101
  228.2 35.4 %all-gather.3.cloned.1.call-done = bf16[8,128,512]{2,1,0:T(8,128)(2,1)} async-done(((bf16[1,128,512]{2,1,0:T(8,128)(2,1)}), bf16[8,128,512]{2,1,0:T(8,128)(2,1)}) %all-gather.3.cloned.1.call-update) | async-done | bytes 1048592 | tf_op jit(solution)/shard_map/all_gather | solution.py:75
  263.6 4.8 %collective-permute-start.6 = (bf16[8,128,512]{2,1,0:T(8,128)(2,1)}, bf16[8,128,512]{2,1,0:T(8,128)(2,1)S(1)}, u32[]{:S(2)}, u32[]{:S(2)}) collective-permute-start(bf16[8,128,512]{2,1,0:T(8,128)(2,1)} %all-gather.3.cloned.1.call-done), channel_id=1, source_target_pairs={{0,16},{16,0},{32,48},{48,32},{64,80},{80,64},{96,112},{112,96},{1... | collective-permute-start | bytes 3145736 | tf_op jit(solution)/shard_map/ppermute | solution.py:76
  273.6 6.7 %all-to-all-start = ((bf16[16,128,512]{2,1,0:T(8,128)(2,1)}), bf16[16,128,512]{2,1,0:T(8,128)(2,1)S(1)}, u32[]{:S(2)}, u32[]{:S(2)}) async-start(bf16[16,128,512]{2,1,0:T(8,128)(2,1)} %bitcast.84), calls=%async_computation | async-start | bytes 4194304 | tf_op jit(solution)/shard_map/all_to_all | solution.py:86
  285.0 3.6 %collective-permute-done.14 = f32[3,2,512]{2,1,0:T(2,128)S(1)} collective-permute-done((f32[3,2,512]{2,1,0:T(2,128)S(1)}, f32[3,2,512]{2,1,0:T(2,128)S(1)}, u32[]{:S(2)}, u32[]{:S(2)}) %collective-permute-start.14) | collective-permute-done | bytes 12320 | tf_op jit(solution)/shard_map/ppermute | solution.py:20
  290.0 22.3 %all-to-all-done = bf16[16,128,512]{2,1,0:T(8,128)(2,1)S(1)} async-done(((bf16[16,128,512]{2,1,0:T(8,128)(2,1)}), bf16[16,128,512]{2,1,0:T(8,128)(2,1)S(1)}, u32[]{:S(2)}, u32[]{:S(2)}) %all-to-all-start) | async-done | bytes 2097184 | tf_op jit(solution)/shard_map/all_to_all | solution.py:86
  315.2 14.1 %collective-permute-done.7 = bf16[128,512]{1,0:T(8,128)(2,1)S(1)} collective-permute-done((bf16[128,512]{1,0:T(8,128)(2,1)S(1)}, bf16[128,512]{1,0:T(8,128)(2,1)S(1)}, u32[]{:S(2)}, u32[]{:S(2)}) %collective-permute-start.7) | collective-permute-done | bytes 131104 | tf_op jit(solution)/shard_map/ppermute | solution.py:24
  (103 shorter events, 53.5 us)
Async XLA Ops:
  7.2 72.5 %copy-start = (bf16[512,512]{1,0:T(8,128)(2,1)S(1)}, bf16[512,512]{1,0:T(8,128)(2,1)}, u32[]{:S(2)}) copy-start(bf16[512,512]{1,0:T(8,128)(2,1)} %param.16) | copy-start | bytes 1572868
  7.2 72.5 %all-gather.5.cloned.1.call-start = ((), (), s32[]{:S(2)}) async-start(), calls=%async_computation.3 | async-start | bytes 2228224 | tf_op jit(solution)/shard_map/all_gather | solution.py:26
  7.2 10.5 %collective-permute-start.8 = (bf16[128,512]{1,0:T(8,128)(2,1)}, bf16[128,512]{1,0:T(8,128)(2,1)S(1)}, u32[]{:S(2)}, u32[]{:S(2)}) collective-permute-start(bf16[128,512]{1,0:T(8,128)(2,1)} %param.17), channel_id=1, source_target_pairs={{0,0},{1,16},{2,32},{3,48},{4,64},{5,80},{6,96},{7,112},{8,128},{9... | collective-permute-start | bytes 393224 | tf_op jit(solution)/shard_map/ppermute | solution.py:24
  83.9 14.8 %copy-start.16 = (f32[3,3,512]{2,1,0:T(4,128)S(1)}, f32[3,3,512]{2,1,0:T(4,128)}, u32[]{:S(2)}) copy-start(f32[3,3,512]{2,1,0:T(4,128)} %param.12) | copy-start | bytes 55300
  83.9 87.5 %all-to-all-start.1 = ((bf16[16,128,512]{2,1,0:T(8,128)(2,1)}), bf16[16,128,512]{2,1,0:T(8,128)(2,1)S(1)}, u32[]{:S(2)}, u32[]{:S(2)}) async-start(bf16[16,128,512]{2,1,0:T(8,128)(2,1)} %bitcast.86), calls=%async_computation.1 | async-start | bytes 4194304 | tf_op jit(solution)/shard_map/all_to_all | solution.py:93
  92.6 171.1 %all-gather.3.cloned.1.call-start = ((), (), s32[]{:S(2)}) async-start(), calls=%async_computation.2 | async-start | bytes 1179648 | tf_op jit(solution)/shard_map/all_gather | solution.py:75
  92.7 45.3 %collective-permute-start = (bf16[3,2,512]{2,1,0:T(2,128)(2,1)S(1)}, bf16[3,2,512]{2,1,0:T(2,128)(2,1)S(1)}, u32[]{:S(2)}, u32[]{:S(2)}) collective-permute-start(bf16[3,2,512]{2,1,0:T(2,128)(2,1)S(1)} %pad_maximum_fusion.2), channel_id=1, source_target_pairs={{0,16},{16,32},{32,48},{48,64},{64,80},{80,96},{96,112},{112,128},... | collective-permute-start | bytes 18440 | tf_op jit(solution)/shard_map/ppermute | solution.py:20
  96.1 46.3 %copy-start.17 = (f32[128]{0:T(128)}, f32[128]{0:T(128)S(1)}, u32[]{:S(2)}) copy-start(f32[128]{0:T(128)S(1)} %iota_convert_fusion) | copy-start | bytes 1540
  98.7 40.2 %copy-start.13 = (f32[3,512]{1,0:T(4,128)}, f32[3,512]{1,0:T(4,128)S(1)}, u32[]{:S(2)}) copy-start(f32[3,512]{1,0:T(4,128)S(1)} %get-tuple-element.22) | copy-start | bytes 18436
  148.2 5.4 %collective-permute-start.1 = (f32[16,512]{1,0:T(8,128)S(1)}, f32[16,512]{1,0:T(8,128)S(1)}, u32[]{:S(2)}, u32[]{:S(2)}) collective-permute-start(f32[16,512]{1,0:T(8,128)S(1)} %fusion.26), channel_id=1, source_target_pairs={{0,16},{16,32},{32,48},{48,64},{64,80},{80,96},{96,112},{112,128},... | collective-permute-start | bytes 98312 | tf_op jit(solution)/shard_map/ppermute | solution.py:20
  153.6 5.2 %collective-permute-start.2 = (f32[16,512]{1,0:T(8,128)S(1)}, f32[16,512]{1,0:T(8,128)S(1)}, u32[]{:S(2)}, u32[]{:S(2)}) collective-permute-start(f32[16,512]{1,0:T(8,128)S(1)} %collective-permute-done.1), channel_id=1, source_target_pairs={{0,16},{16,32},{32,48},{48,64},{64,80},{80,96},{96,112},{112,128},... | collective-permute-start | bytes 98312 | tf_op jit(solution)/shard_map/ppermute | solution.py:20
  158.8 6.8 %collective-permute-start.3 = (f32[16,512]{1,0:T(8,128)S(1)}, f32[16,512]{1,0:T(8,128)S(1)}, u32[]{:S(2)}, u32[]{:S(2)}) collective-permute-start(f32[16,512]{1,0:T(8,128)S(1)} %multiply_add_fusion.5), channel_id=1, source_target_pairs={{0,32},{16,48},{32,64},{48,80},{64,96},{80,112},{96,128},{112,144}... | collective-permute-start | bytes 98312 | tf_op jit(solution)/shard_map/ppermute | solution.py:20
  165.7 5.6 %collective-permute-start.4 = (f32[16,512]{1,0:T(8,128)S(1)}, f32[16,512]{1,0:T(8,128)S(1)}, u32[]{:S(2)}, u32[]{:S(2)}) collective-permute-start(f32[16,512]{1,0:T(8,128)S(1)} %multiply_add_fusion.4), channel_id=1, source_target_pairs={{0,64},{16,80},{32,96},{48,112},{64,128},{80,144},{96,160},{112,17... | collective-permute-start | bytes 98312 | tf_op jit(solution)/shard_map/ppermute | solution.py:20
  181.5 9.0 %collective-permute-start.9 = (f32[16,512]{1,0:T(8,128)S(1)}, f32[16,512]{1,0:T(8,128)S(1)}, u32[]{:S(2)}, u32[]{:S(2)}) collective-permute-start(f32[16,512]{1,0:T(8,128)S(1)} %squeeze.26), channel_id=1, source_target_pairs={{16,0},{32,16},{48,32},{64,48},{80,64},{96,80},{112,96},{128,112},... | collective-permute-start | bytes 98312 | tf_op jit(solution)/shard_map/ppermute | solution.py:20
  190.5 5.2 %collective-permute-start.10 = (f32[16,512]{1,0:T(8,128)S(1)}, f32[16,512]{1,0:T(8,128)S(1)}, u32[]{:S(2)}, u32[]{:S(2)}) collective-permute-start(f32[16,512]{1,0:T(8,128)S(1)} %collective-permute-done.9), channel_id=1, source_target_pairs={{16,0},{32,16},{48,32},{64,48},{80,64},{96,80},{112,96},{128,112},... | collective-permute-start | bytes 98312 | tf_op jit(solution)/shard_map/ppermute | solution.py:20
  195.7 8.9 %collective-permute-start.11 = (f32[16,512]{1,0:T(8,128)S(1)}, f32[16,512]{1,0:T(8,128)S(1)}, u32[]{:S(2)}, u32[]{:S(2)}) collective-permute-start(f32[16,512]{1,0:T(8,128)S(1)} %multiply_add_fusion.2), channel_id=1, source_target_pairs={{32,0},{48,16},{64,32},{80,48},{96,64},{112,80},{128,96},{144,112}... | collective-permute-start | bytes 98312 | tf_op jit(solution)/shard_map/ppermute | solution.py:20
  204.6 8.0 %collective-permute-start.12 = (f32[16,512]{1,0:T(8,128)S(1)}, f32[16,512]{1,0:T(8,128)S(1)}, u32[]{:S(2)}, u32[]{:S(2)}) collective-permute-start(f32[16,512]{1,0:T(8,128)S(1)} %multiply_add_fusion.1), channel_id=1, source_target_pairs={{64,0},{80,16},{96,32},{112,48},{128,64},{144,80},{160,96},{176,11... | collective-permute-start | bytes 98312 | tf_op jit(solution)/shard_map/ppermute | solution.py:20
  206.6 16.5 %collective-permute-start.5 = (f32[16,512]{1,0:T(8,128)S(1)}, f32[16,512]{1,0:T(8,128)S(1)}, u32[]{:S(2)}, u32[]{:S(2)}) collective-permute-start(f32[16,512]{1,0:T(8,128)S(1)} %get-tuple-element.18), channel_id=1, source_target_pairs={{0,128},{16,144},{32,160},{48,176},{64,192},{80,208},{96,224},{112... | collective-permute-start | bytes 98312 | tf_op jit(solution)/shard_map/ppermute | solution.py:20
  212.7 10.4 %collective-permute-start.13 = (f32[16,512]{1,0:T(8,128)S(1)}, f32[16,512]{1,0:T(8,128)S(1)}, u32[]{:S(2)}, u32[]{:S(2)}) collective-permute-start(f32[16,512]{1,0:T(8,128)S(1)} %multiply_add_fusion), channel_id=1, source_target_pairs={{128,0},{144,16},{160,32},{176,48},{192,64},{208,80},{224,96},{240... | collective-permute-start | bytes 98312 | tf_op jit(solution)/shard_map/ppermute | solution.py:20
  263.6 7.3 %collective-permute-start.6 = (bf16[8,128,512]{2,1,0:T(8,128)(2,1)}, bf16[8,128,512]{2,1,0:T(8,128)(2,1)S(1)}, u32[]{:S(2)}, u32[]{:S(2)}) collective-permute-start(bf16[8,128,512]{2,1,0:T(8,128)(2,1)} %all-gather.3.cloned.1.call-done), channel_id=1, source_target_pairs={{0,16},{16,0},{32,48},{48,32},{64,80},{80,64},{96,112},{112,96},{1... | collective-permute-start | bytes 3145736 | tf_op jit(solution)/shard_map/ppermute | solution.py:76
  273.6 16.1 %copy-start.14 = (f32[3,512]{1,0:T(4,128)S(1)}, f32[3,512]{1,0:T(4,128)}, u32[]{:S(2)}) copy-start(f32[3,512]{1,0:T(4,128)} %copy-done.13) | copy-start | bytes 18436
  273.6 38.7 %all-to-all-start = ((bf16[16,128,512]{2,1,0:T(8,128)(2,1)}), bf16[16,128,512]{2,1,0:T(8,128)(2,1)S(1)}, u32[]{:S(2)}, u32[]{:S(2)}) async-start(bf16[16,128,512]{2,1,0:T(8,128)(2,1)} %bitcast.84), calls=%async_computation | async-start | bytes 4194304 | tf_op jit(solution)/shard_map/all_to_all | solution.py:86
  282.4 6.2 %collective-permute-start.14 = (f32[3,2,512]{2,1,0:T(2,128)S(1)}, f32[3,2,512]{2,1,0:T(2,128)S(1)}, u32[]{:S(2)}, u32[]{:S(2)}) collective-permute-start(f32[3,2,512]{2,1,0:T(2,128)S(1)} %slice.90), channel_id=1, source_target_pairs={{16,0},{32,16},{48,32},{64,48},{80,64},{96,80},{112,96},{128,112},... | collective-permute-start | bytes 36872 | tf_op jit(solution)/shard_map/ppermute | solution.py:20
  312.6 16.8 %collective-permute-start.7 = (bf16[128,512]{1,0:T(8,128)(2,1)S(1)}, bf16[128,512]{1,0:T(8,128)(2,1)S(1)}, u32[]{:S(2)}, u32[]{:S(2)}) collective-permute-start(bf16[128,512]{1,0:T(8,128)(2,1)S(1)} %reduce_sum.47), channel_id=1, source_target_pairs={{0,0},{1,16},{2,32},{3,48},{4,64},{5,80},{6,96},{7,112},{8,128},{9... | collective-permute-start | bytes 393224 | tf_op jit(solution)/shard_map/ppermute | solution.py:24
  (15 other events, 82.8 us)
Sparse Core Ops, SparseCore 0:
  18.5 61.0 all-gather.4
  228.4 35.2 all-gather.2

commit v4 on v2

--- a/solution.py
+++ b/solution.py
@@ -1,7 +1,68 @@
+import functools
+
 import jax
 import jax.numpy as jnp
 from jax import lax
+from jax.experimental import pallas as pl
+from jax.experimental.pallas import tpu as pltpu
 from jax.sharding import PartitionSpec as P
+
+MESH = pl.DeviceIdType.MESH
+
+
+def exchange_kernel(count, final_ref, out_ref, slots, send_sems, recv_sems):
+    me = lax.axis_index("seq")
+    lane = lax.axis_index("ch")
+    barrier = pltpu.get_barrier_semaphore()
+    for peer in range(count):
+
+        @pl.when(me != peer)
+        def _():
+            pl.semaphore_signal(barrier, inc=1, device_id=(peer, lane), device_id_type=MESH)
+
+    pl.semaphore_wait(barrier, count - 1)
+
+    def link(peer, slot):
+        return pltpu.make_async_remote_copy(
+            src_ref=final_ref,
+            dst_ref=slots.at[slot],
+            send_sem=send_sems.at[peer],
+            recv_sem=recv_sems.at[slot],
+            device_id=(peer, lane),
+            device_id_type=MESH,
+        )
+
+    for peer in range(count):
+
+        @pl.when(me != peer)
+        def _():
+            link(peer, me).start()
+
+    slots[me] = final_ref[...]
+    for peer in range(count):
+
+        @pl.when(me != peer)
+        def _():
+            link(peer, me).wait_send()
+            link(peer, peer).wait_recv()
+
+    out_ref[...] = slots[...]
+
+
+def exchange(final, count):
+    shape = (count,) + final.shape
+    return pl.pallas_call(
+        functools.partial(exchange_kernel, count),
+        out_shape=jax.ShapeDtypeStruct(shape, final.dtype),
+        in_specs=[pl.BlockSpec(memory_space=pltpu.VMEM)],
+        out_specs=pl.BlockSpec(memory_space=pltpu.VMEM),
+        scratch_shapes=[
+            pltpu.VMEM(shape, final.dtype),
+            pltpu.SemaphoreType.DMA((count,)),
+            pltpu.SemaphoreType.DMA((count,)),
+        ],
+        compiler_params=pltpu.CompilerParams(collective_id=0, has_side_effects=True),
+    )(final)
 
 
 def from_behind(block, axis, distance):
@@ -23,8 +84,10 @@
     groups = [[side + 2 * step for step in range(half)] for side in range(2)]
     mine = lax.all_gather(out_weight, "seq", axis_index_groups=groups)
     other = lax.ppermute(mine, "seq", [(i, i ^ 1) for i in range(count)])
-    grad_full = lax.all_gather(grad_out, "ch", axis=1, tiled=True)
-    grad_split = grad_full.reshape(tok_rows, half, 2, chan_width)
+    lanes = lax.axis_size("ch")
+    grad_copies = jnp.broadcast_to(grad_out[None], (lanes,) + grad_out.shape)
+    grad_blocks = lax.all_to_all(grad_copies, "ch", 0, 0, tiled=True)
+    grad_split = jnp.transpose(grad_blocks, (1, 0, 2)).reshape(tok_rows, half, 2, chan_width)
     grad_mine = lax.dynamic_index_in_dim(grad_split, core, 2, False)
     grad_other = lax.dynamic_index_in_dim(grad_split, 1 - core, 2, False)
 
@@ -69,21 +132,18 @@
     bwd_sums = prefix(upper, shrink, grad_long)
     bwd_final = bwd_sums[0]
 
-    def shift(block, distance):
-        route = [(i, i + distance) for i in range(count) if 0 <= i + distance < count]
-        return lax.ppermute(block, "seq", route)
+    finals = jnp.stack([fwd_final, bwd_final])
+    gathered = exchange(finals, count)
+    source = jnp.arange(count)
+    fwd_gap = place - 1 - source
+    bwd_gap = source - place - 1
 
-    def entering(final, direction):
-        state = shift(final, direction)
-        distance = 1
-        while distance < count:
-            jump = jnp.exp(-decay_rate * float(tok_rows * distance))
-            state = state + jump * shift(state, direction * distance)
-            distance *= 2
-        return state
+    def weights(gap):
+        span = (tok_rows * jnp.maximum(gap, 0)).astype(jnp.float32)[:, None, None]
+        return jnp.where((gap >= 0)[:, None, None], jnp.exp(-decay_rate[None] * span), 0.0)
 
-    fwd_entry = entering(fwd_final, 1) * one_step
-    bwd_entry = entering(bwd_final, -1) * block_decay
+    fwd_entry = jnp.sum(weights(fwd_gap) * gathered[:, 0], axis=0) * one_step
+    bwd_entry = jnp.sum(weights(bwd_gap) * gathered[:, 1], axis=0) * block_decay
 
     long_out = (
         jnp.sum(scaled_shrink * (fwd_sums + fwd_entry[None]), axis=1) + skip_gain[None, :] * gated

time: 277 us -> 233 us (0.84)
  the two profiles are of different devices: /device:TPU:161 before, /device:TPU:65 now
where the time goes in v4:
time: 233 us
  waiting for transfers between devices  114 us (49%)
  Pallas kernels  33.4 us (14%)
  local copies, waits for them, and re-layouts  23.7 us (10%)
  matrix products  18 us (8%)
  starting transfers between devices  17.8 us (8%)
  between operations  14.6 us (6%)
  other arithmetic  11.2 us (5%)
    all_gather x1, waiting for transfers between devices, per_device(): mine = lax.all_gather(out_weight, 'seq', axis_index_groups=groups)  56.9 us
    pallas_call x1, Pallas kernels, exchange(): pl.pallas_call(functools.partial(exchange_kernel, count), out_shape=jax.S...  33.4 us
    all_to_all x1, waiting for transfers between devices, per_device(): received = lax.all_to_all(parts, 'ch', 0, 0, tiled=True)  27.6 us
    all_to_all x1, waiting for transfers between devices, per_device(): grad_blocks = lax.all_to_all(grad_copies, 'ch', 0, 0, tiled=True)  25.7 us
    unnamed x42, local copies, waits for them, and re-layouts  17.7 us
    all_to_all x1, starting transfers between devices, per_device(): grad_blocks = lax.all_to_all(grad_copies, 'ch', 0, 0, tiled=True)  6.53 us
    ppermute x2, starting transfers between devices, from_behind(): return lax.ppermute(block, axis, route)  6.48 us
    dot_general x2, matrix products, prefix(): jnp.dot(tri, spread, precision=highest, preferred_element_type=jnp.float32)  6.35 us
  transfers between devices with their start and end apart: 6, of which 4 were waited for; matrix products, arithmetic and copies ran while one was open for 4% of the time, Pallas kernels for 0%

profile of v4, /device:TPU:65, one launch (start us, length us, event | category | flops | bytes accessed | tf_op | source)
XLA Modules:
  0.0 232.8 jit_solution(4309295650636947996)
XLA Ops:
  8.0 56.9 %all-gather.3.cloned.1.call-done = bf16[4096,512]{1,0:T(8,128)(2,1)} async-done(((bf16[512,512]{1,0:T(8,128)(2,1)}), bf16[4096,512]{1,0:T(8,128)(2,1)}) %all-gather.3.cloned.1.call-update) | async-done | bytes 4194320 | tf_op jit(solution)/shard_map/all_gather | solution.py:85
  64.8 1.0 collective-permute-start.1
  65.8 2.4 %broadcast_in_dim.18 = bf16[16,128,512]{2,1,0:T(8,128)(2,1)} broadcast(bf16[128,512]{1,0:T(8,128)(2,1)} %param.17), dimensions={1,2} | broadcast | bytes 2228224 | tf_op jit(solution)/shard_map/broadcast_in_dim | solution.py:88
  68.3 6.5 %all-to-all-start = ((bf16[16,128,512]{2,1,0:T(8,128)(2,1)}), bf16[16,128,512]{2,1,0:T(8,128)(2,1)S(1)}, u32[]{:S(2)}, u32[]{:S(2)}) async-start(bf16[16,128,512]{2,1,0:T(8,128)(2,1)} %broadcast_in_dim.18), calls=%async_computation | async-start | bytes 4194304 | tf_op jit(solution)/shard_map/all_to_all | solution.py:89
  74.9 4.6 %collective-permute-start = (bf16[3,2,512]{2,1,0:T(2,128)(2,1)S(1)}, bf16[3,2,512]{2,1,0:T(2,128)(2,1)S(1)}, u32[]{:S(2)}, u32[]{:S(2)}) collective-permute-start(bf16[3,2,512]{2,1,0:T(2,128)(2,1)S(1)} %pad_maximum_fusion.3), channel_id=1, source_target_pairs={{0,16},{16,32},{32,48},{48,64},{64,80},{80,96},{96,112},{112,128},... | collective-permute-start | bytes 18440 | tf_op jit(solution)/shard_map/ppermute | solution.py:71
  79.5 2.6 %multiply_exponential_fusion = f32[128,16,512]{2,1,0:T(8,128)} fusion(f32[128]{0:T(128)S(1)} %iota_convert_fusion, f32[16,512]{1,0:T(8,128)S(1)} %get-tuple-element.20), kind=kLoop, calls=%fused_computation.14 | loop fusion | flops 1048576 | bytes 4227584 | tf_op jit(solution)/shard_map/exp | solution.py:110
  82.5 25.7 %all-to-all-done = bf16[16,128,512]{2,1,0:T(8,128)(2,1)S(1)} async-done(((bf16[16,128,512]{2,1,0:T(8,128)(2,1)}), bf16[16,128,512]{2,1,0:T(8,128)(2,1)S(1)}, u32[]{:S(2)}, u32[]{:S(2)}) %all-to-all-start) | async-done | bytes 2097184 | tf_op jit(solution)/shard_map/all_to_all | solution.py:89
  108.2 3.6 %convolution_bitcast_fusion.1 = f32[128,512]{1,0:T(8,128)S(1)} fusion(bf16[8,512,512]{2,1,0:T(8,128)(2,1)} %bitcast.112, bf16[128,8,2,512]{3,0,2,1:T(8,128)(2,1)S(1)} %bitcast.119, s32[]{:T(128)S(6)} %select_n.36), kind=kOutput, calls=%fused_computation.25 | convolution fusion | flops 536870912 | bytes 5505028 | tf_op jit(solution)/shard_map/tzc,zrc->tr/dot_general | solution.py:128
  111.9 4.4 %fusion.31 = (f32[128,512]{1,0:T(8,128)S(1)}, f32[128,512]{1,0:T(8,128)S(1)}, f32[128,512]{1,0:T(8,128)}) fusion(f32[3,128,512]{2,1,0:T(8,128)S(1)} %fusion.26, f32[128,512]{1,0:T(8,128)S(1)} %convolution_bitcast_fusion.1, bf16[8,512,512]{2,1,0:T(8,128)(2,1)} %collective-permute-done.1, bf16[128,8,2,512]{3,0,2,1:T(8,128)(2,1)S(1)} %bitcast.120, ...), kind=kOutput, calls=%fused_computation.58 | convolution fusion | flops 537067520 | bytes 7077892 | tf_op jit(solution)/shard_map/tzc,zrc->tr/dot_general | solution.py:130
  117.0 3.4 %copy.21 = f32[16,8,16,512]{3,1,2,0:T(8,128)S(1)} copy(f32[16,8,16,512]{3,2,1,0:T(8,128)S(1)} %bitcast.116) | data formatting | bytes 8388608
  121.0 3.4 %copy.18 = f32[16,8,16,512]{3,1,2,0:T(8,128)S(1)} copy(f32[16,8,16,512]{3,2,1,0:T(8,128)S(1)} %bitcast.117) | data formatting | bytes 8388608
  124.4 3.2 %fusion.4 = f32[128,8192]{1,0:T(8,128)S(1)} fusion(f32[128,8192]{1,0:T(8,128)S(1)} %bitcast.114, f32[8192]{0:T(1024)S(1)} %bitcast.129, f32[128]{0:T(128)S(1)} %iota_convert_fusion), kind=kOutput, calls=%fused_computation.6 | convolution fusion | flops 1612726272 | bytes 8421888 | tf_op jit(solution)/shard_map/dot_general | solution.py:122
  127.6 3.1 %fusion.8 = f32[128,8192]{1,0:T(8,128)S(1)} fusion(f32[128,8192]{1,0:T(8,128)S(1)} %bitcast.115, f32[128]{0:T(128)S(1)} %iota_convert_fusion, f32[8192]{0:T(1024)S(1)} %bitcast.128), kind=kOutput, calls=%fused_computation.10 | convolution fusion | flops 1612726272 | bytes 8421888 | tf_op jit(solution)/shard_map/dot_general | solution.py:122
  131.0 1.8 copy-done.1
  134.1 33.4 %shard_map.120 = f32[16,2,16,512]{3,2,1,0:T(8,128)} custom-call(f32[2,16,512]{2,1,0:T(8,128)} %pad_maximum_fusion.2.final_ref), custom_call_target="tpu_custom_call" | custom-call | tf_op jit(solution)/shard_map/pallas_call | solution.py:54
  167.5 5.6 %copy.22 = f32[16,8,16,512]{3,2,1,0:T(8,128)S(1)} copy(f32[16,8,16,512]{3,1,2,0:T(8,128)} %bitcast.109) | data formatting | bytes 8388608
  173.2 3.3 %copy.19 = f32[16,8,16,512]{3,2,1,0:T(8,128)S(1)} copy(f32[16,8,16,512]{3,1,2,0:T(8,128)S(1)} %bitcast.110) | data formatting | bytes 8388608
  176.9 3.8 %fusion.1 = (f32[128,512]{1,0:T(8,128)S(1)}, f32[128,512]{1,0:T(8,128)S(1)}) fusion(f32[16,8,16,512]{3,2,1,0:T(8,128)S(1)} %copy.22, f32[16,512]{1,0:T(8,128)S(1)} %get-tuple-element.18, f32[16,512]{1,0:T(8,128)S(1)} %copy-done.11, f32[128]{0:T(128)S(1)} %iota_convert_fusion, f32[16,512]{1,0:T(8,128)S(1)} %get-tuple-element.19, ...), kind=kLoop, calls=%fused_computation.2 | loop fusion | flops 10354688 | bytes 9077248 | tf_op jit(solution)/shard_map/reduce_sum | solution.py:166
  182.4 2.9 %fusion.17 = bf16[8,1,128,512]{3,2,0,1:T(8,128)(2,1)S(1)} fusion(bf16[128,512,1]{1,0,2:T(8,128)(2,1)S(1)} %get-tuple-element.10, bf16[8,512,512]{2,1,0:T(8,128)(2,1)} %collective-permute-done.1), kind=kOutput, calls=%fused_computation.23 | convolution fusion | flops 537395200 | bytes 5373952 | tf_op jit(solution)/shard_map/tr,zrc->ztc/dot_general | solution.py:153
  185.7 1.5 copy.15
  187.2 3.7 %all-to-all-start.1 = ((bf16[16,128,512]{2,1,0:T(8,128)(2,1)}), bf16[16,128,512]{2,1,0:T(8,128)(2,1)S(1)}, u32[]{:S(2)}, u32[]{:S(2)}) async-start(bf16[16,128,512]{2,1,0:T(8,128)(2,1)} %bitcast.118), calls=%async_computation.1 | async-start | bytes 4194304 | tf_op jit(solution)/shard_map/all_to_all | solution.py:161
  191.1 1.9 collective-permute-start.2
  193.0 3.4 %collective-permute-done.2 = f32[3,2,512]{2,1,0:T(2,128)S(1)} collective-permute-done((f32[3,2,512]{2,1,0:T(2,128)S(1)}, f32[3,2,512]{2,1,0:T(2,128)S(1)}, u32[]{:S(2)}, u32[]{:S(2)}) %collective-permute-start.2) | collective-permute-done | bytes 12320 | tf_op jit(solution)/shard_map/ppermute | solution.py:71
  197.5 27.6 %all-to-all-done.1 = bf16[16,128,512]{2,1,0:T(8,128)(2,1)S(1)} async-done(((bf16[16,128,512]{2,1,0:T(8,128)(2,1)}), bf16[16,128,512]{2,1,0:T(8,128)(2,1)S(1)}, u32[]{:S(2)}, u32[]{:S(2)}) %all-to-all-start.1) | async-done | bytes 2097184 | tf_op jit(solution)/shard_map/all_to_all | solution.py:161
  (67 shorter events, 8.5 us)
Async XLA Ops:
  7.2 67.6 %copy-start.14 = (bf16[128,512]{1,0:T(8,128)(2,1)S(1)}, bf16[128,512]{1,0:T(8,128)(2,1)}, u32[]{:S(2)}) copy-start(bf16[128,512]{1,0:T(8,128)(2,1)} %param.9) | copy-start | bytes 393220
  7.2 67.6 %copy-start.13 = (bf16[128,512]{1,0:T(8,128)(2,1)S(1)}, bf16[128,512]{1,0:T(8,128)(2,1)}, u32[]{:S(2)}) copy-start(bf16[128,512]{1,0:T(8,128)(2,1)} %param.10) | copy-start | bytes 393220
  7.2 67.6 %copy-start.12 = (bf16[128,512]{1,0:T(8,128)(2,1)S(1)}, bf16[128,512]{1,0:T(8,128)(2,1)}, u32[]{:S(2)}) copy-start(bf16[128,512]{1,0:T(8,128)(2,1)} %param.11) | copy-start | bytes 393220
  7.2 72.3 %copy-start.16 = (f32[3,3,512]{2,1,0:T(4,128)S(1)}, f32[3,3,512]{2,1,0:T(4,128)}, u32[]{:S(2)}) copy-start(f32[3,3,512]{2,1,0:T(4,128)} %param.12) | copy-start | bytes 55300
  7.2 72.3 %copy-start.11 = (f32[16,512]{1,0:T(8,128)S(1)}, f32[16,512]{1,0:T(8,128)}, u32[]{:S(2)}) copy-start(f32[16,512]{1,0:T(8,128)} %param.13) | copy-start | bytes 98308
  7.2 57.6 %all-gather.3.cloned.1.call-start = ((), (), s32[]{:S(2)}) async-start(), calls=%async_computation.2 | async-start | bytes 4718592 | tf_op jit(solution)/shard_map/all_gather | solution.py:85
  64.8 47.0 %collective-permute-start.1 = (bf16[8,512,512]{2,1,0:T(8,128)(2,1)}, bf16[8,512,512]{2,1,0:T(8,128)(2,1)}, u32[]{:S(2)}, u32[]{:S(2)}) collective-permute-start(bf16[8,512,512]{2,1,0:T(8,128)(2,1)} %bitcast.111), channel_id=1, source_target_pairs={{0,16},{16,0},{32,48},{48,32},{64,80},{80,64},{96,112},{112,96},{1... | collective-permute-start | bytes 12582920 | tf_op jit(solution)/shard_map/ppermute | solution.py:86
  68.3 40.0 %all-to-all-start = ((bf16[16,128,512]{2,1,0:T(8,128)(2,1)}), bf16[16,128,512]{2,1,0:T(8,128)(2,1)S(1)}, u32[]{:S(2)}, u32[]{:S(2)}) async-start(bf16[16,128,512]{2,1,0:T(8,128)(2,1)} %broadcast_in_dim.18), calls=%async_computation | async-start | bytes 4194304 | tf_op jit(solution)/shard_map/all_to_all | solution.py:89
  74.9 7.3 %collective-permute-start = (bf16[3,2,512]{2,1,0:T(2,128)(2,1)S(1)}, bf16[3,2,512]{2,1,0:T(2,128)(2,1)S(1)}, u32[]{:S(2)}, u32[]{:S(2)}) collective-permute-start(bf16[3,2,512]{2,1,0:T(2,128)(2,1)S(1)} %pad_maximum_fusion.3), channel_id=1, source_target_pairs={{0,16},{16,32},{32,48},{48,64},{64,80},{80,96},{96,112},{112,128},... | collective-permute-start | bytes 18440 | tf_op jit(solution)/shard_map/ppermute | solution.py:71
  116.3 0.7 copy-start.8
  116.3 4.2 %copy-start.6 = (f32[128,512]{1,0:T(8,128)}, f32[128,512]{1,0:T(8,128)S(1)}, u32[]{:S(2)}) copy-start(f32[128,512]{1,0:T(8,128)S(1)} %get-tuple-element.11) | copy-start | bytes 786436
  127.6 3.2 %copy-start = (f32[128,8192]{1,0:T(8,128)}, f32[128,8192]{1,0:T(8,128)S(1)}, u32[]{:S(2)}) copy-start(f32[128,8192]{1,0:T(8,128)S(1)} %fusion.4) | copy-start | bytes 12582916
  130.8 2.0 copy-start.1
  167.5 5.6 %copy-start.2 = (f32[128,8192]{1,0:T(8,128)S(1)}, f32[128,8192]{1,0:T(8,128)}, u32[]{:S(2)}) copy-start(f32[128,8192]{1,0:T(8,128)} %copy-done.1) | copy-start | bytes 12582916
  173.1 3.3 %copy-start.4 = (f32[16,2,16,512]{3,2,1,0:T(8,128)S(1)}, f32[16,2,16,512]{3,2,1,0:T(8,128)}, u32[]{:S(2)}) copy-start(f32[16,2,16,512]{3,2,1,0:T(8,128)} %shard_map.120) | copy-start | bytes 3145732
  173.2 3.6 %copy-start.15 = (f32[16,512]{1,0:T(8,128)S(1)}, f32[16,512]{1,0:T(8,128)}, u32[]{:S(2)}) copy-start(f32[16,512]{1,0:T(8,128)} %param.14) | copy-start | bytes 98308
  176.8 3.9 %copy-start.7 = (f32[128,512]{1,0:T(8,128)S(1)}, f32[128,512]{1,0:T(8,128)}, u32[]{:S(2)}) copy-start(f32[128,512]{1,0:T(8,128)} %copy-done.6) | copy-start | bytes 786436
  176.8 3.9 %copy-start.9 = (f32[128,512]{1,0:T(8,128)S(1)}, f32[128,512]{1,0:T(8,128)}, u32[]{:S(2)}) copy-start(f32[128,512]{1,0:T(8,128)} %copy-done.8) | copy-start | bytes 786436
  176.8 3.9 %copy-start.10 = (f32[128,512]{1,0:T(8,128)S(1)}, f32[128,512]{1,0:T(8,128)}, u32[]{:S(2)}) copy-start(f32[128,512]{1,0:T(8,128)} %get-tuple-element.25) | copy-start | bytes 786436
  176.8 3.9 %copy-start.17 = (f32[512]{0:T(512)S(1)}, f32[512]{0:T(512)}, u32[]{:S(2)}) copy-start(f32[512]{0:T(512)} %param.15) | copy-start | bytes 6148
  176.8 4.8 %copy-start.3 = (bf16[4096,512]{1,0:T(8,128)(2,1)S(1)}, bf16[4096,512]{1,0:T(8,128)(2,1)}, u32[]{:S(2)}) copy-start(bf16[4096,512]{1,0:T(8,128)(2,1)} %all-gather.3.cloned.1.call-done) | copy-start | bytes 12582916
  185.7 5.3 %copy-start.5 = (f32[1,128,512]{2,1,0:T(8,128)S(1)}, f32[1,128,512]{2,1,0:T(8,128)}, u32[]{:S(2)}) copy-start(f32[1,128,512]{2,1,0:T(8,128)} %get-tuple-element.13) | copy-start | bytes 786436
  187.2 37.8 %all-to-all-start.1 = ((bf16[16,128,512]{2,1,0:T(8,128)(2,1)}), bf16[16,128,512]{2,1,0:T(8,128)(2,1)S(1)}, u32[]{:S(2)}, u32[]{:S(2)}) async-start(bf16[16,128,512]{2,1,0:T(8,128)(2,1)} %bitcast.118), calls=%async_computation.1 | async-start | bytes 4194304 | tf_op jit(solution)/shard_map/all_to_all | solution.py:161
  191.1 5.3 %collective-permute-start.2 = (f32[3,2,512]{2,1,0:T(2,128)S(1)}, f32[3,2,512]{2,1,0:T(2,128)S(1)}, u32[]{:S(2)}, u32[]{:S(2)}) collective-permute-start(f32[3,2,512]{2,1,0:T(2,128)S(1)} %slice.101), channel_id=1, source_target_pairs={{16,0},{32,16},{48,32},{64,48},{80,64},{96,80},{112,96},{128,112},... | collective-permute-start | bytes 36872 | tf_op jit(solution)/shard_map/ppermute | solution.py:71
Sparse Core Ops, SparseCore 0:
  9.8 54.9 all-gather.2

commit v5 on v4

--- a/solution.py
+++ b/solution.py
@@ -71,6 +71,146 @@
     return lax.ppermute(block, axis, route)
 
 
+def fetch_kernel(count, lanes, w_ref, g_ref, w_all, g_all, w_send, w_recv, g_send, g_recv, own_sem):
+    me = lax.axis_index("seq")
+    lane = lax.axis_index("ch")
+    half = count // 2
+    core = me % 2
+    ring = me // 2
+    right = 2 * ((ring + 1) % half) + core
+    left = 2 * ((ring + half - 1) % half) + core
+    partner = me + 1 - 2 * core
+    right_steps = half // 2
+    left_steps = half - 1 - right_steps
+
+    barrier = pltpu.get_barrier_semaphore()
+    for peer in (right, left, partner):
+        pl.semaphore_signal(barrier, inc=1, device_id=(peer, lane), device_id_type=MESH)
+    for other in range(lanes):
+
+        @pl.when(lane != other)
+        def _():
+            pl.semaphore_signal(barrier, inc=1, device_id=(me, other), device_id_type=MESH)
+
+    pl.semaphore_wait(barrier, 3 + lanes - 1)
+
+    def grad_link(other):
+        return pltpu.make_async_remote_copy(
+            src_ref=g_ref,
+            dst_ref=g_all.at[lane],
+            send_sem=g_send.at[other],
+            recv_sem=g_recv.at[lane],
+            device_id=(me, other),
+            device_id_type=MESH,
+        )
+
+    def grad_arrival(other):
+        return pltpu.make_async_remote_copy(
+            src_ref=g_ref,
+            dst_ref=g_all.at[other],
+            send_sem=g_send.at[other],
+            recv_sem=g_recv.at[other],
+            device_id=(me, other),
+            device_id_type=MESH,
+        )
+
+    for other in range(lanes):
+
+        @pl.when(lane != other)
+        def _():
+            grad_link(other).start()
+
+    own_w = pltpu.make_async_copy(w_ref, w_all.at[me], own_sem.at[0])
+    own_g = pltpu.make_async_copy(g_ref, g_all.at[lane], own_sem.at[1])
+    own_w.start()
+    own_g.start()
+
+    sends = []
+
+    def send(source, origin, peer):
+        copy = pltpu.make_async_remote_copy(
+            src_ref=source,
+            dst_ref=w_all.at[origin],
+            send_sem=w_send.at[len(sends)],
+            recv_sem=w_recv.at[origin],
+            device_id=(peer, lane),
+            device_id_type=MESH,
+        )
+        copy.start()
+        sends.append(copy)
+
+    def arrived(origin):
+        pltpu.make_async_remote_copy(
+            src_ref=w_all.at[origin],
+            dst_ref=w_all.at[origin],
+            send_sem=w_send.at[0],
+            recv_sem=w_recv.at[origin],
+            device_id=(me, lane),
+            device_id_type=MESH,
+        ).wait_recv()
+
+    def right_origin(step):
+        return 2 * ((ring - step + 1 + half) % half) + core
+
+    def left_origin(step):
+        return 2 * ((ring + step - 1) % half) + core
+
+    send(w_ref, me, partner)
+    if right_steps >= 1:
+        send(w_ref, me, right)
+    if left_steps >= 1:
+        send(w_ref, me, left)
+    for step in range(2, max(right_steps, left_steps) + 2):
+        if step <= right_steps + 1:
+            origin = right_origin(step)
+            arrived(origin)
+            if step <= right_steps:
+                send(w_all.at[origin], origin, right)
+            send(w_all.at[origin], origin, partner)
+        if step <= left_steps + 1:
+            origin = left_origin(step)
+            arrived(origin)
+            if step <= left_steps:
+                send(w_all.at[origin], origin, left)
+            send(w_all.at[origin], origin, partner)
+
+    for twin in range(half):
+        arrived(2 * twin + 1 - core)
+    for copy in sends:
+        copy.wait_send()
+    for other in range(lanes):
+
+        @pl.when(lane != other)
+        def _():
+            grad_link(other).wait_send()
+            grad_arrival(other).wait_recv()
+
+    own_w.wait()
+    own_g.wait()
+
+
+def fetch(out_weight, grad_out, count, lanes):
+    half = count // 2
+    sends = half + half // 2 + (half - 1 - half // 2)
+    return pl.pallas_call(
+        functools.partial(fetch_kernel, count, lanes),
+        out_shape=(
+            jax.ShapeDtypeStruct((count,) + out_weight.shape, out_weight.dtype),
+            jax.ShapeDtypeStruct((lanes,) + grad_out.shape, grad_out.dtype),
+        ),
+        in_specs=[pl.BlockSpec(memory_space=pl.ANY)] * 2,
+        out_specs=(pl.BlockSpec(memory_space=pl.ANY), pl.BlockSpec(memory_space=pl.ANY)),
+        scratch_shapes=[
+            pltpu.SemaphoreType.DMA((sends,)),
+            pltpu.SemaphoreType.DMA((count,)),
+            pltpu.SemaphoreType.DMA((lanes,)),
+            pltpu.SemaphoreType.DMA((lanes,)),
+            pltpu.SemaphoreType.DMA((2,)),
+        ],
+        compiler_params=pltpu.CompilerParams(collective_id=1, has_side_effects=True),
+    )(out_weight, grad_out)
+
+
 def per_device(query, key, value, short_taps, decay_rate, residue, skip_gain, out_weight, grad_out):
     tok_rows, chan_width = query.shape
     tap_count = short_taps.shape[0]
@@ -79,17 +219,8 @@
     count = lax.axis_size("seq")
     place = lax.axis_index("seq")
 
-    core = place % 2
-    half = count // 2
-    groups = [[side + 2 * step for step in range(half)] for side in range(2)]
-    mine = lax.all_gather(out_weight, "seq", axis_index_groups=groups)
-    other = lax.ppermute(mine, "seq", [(i, i ^ 1) for i in range(count)])
     lanes = lax.axis_size("ch")
-    grad_copies = jnp.broadcast_to(grad_out[None], (lanes,) + grad_out.shape)
-    grad_blocks = lax.all_to_all(grad_copies, "ch", 0, 0, tiled=True)
-    grad_split = jnp.transpose(grad_blocks, (1, 0, 2)).reshape(tok_rows, half, 2, chan_width)
-    grad_mine = lax.dynamic_index_in_dim(grad_split, core, 2, False)
-    grad_other = lax.dynamic_index_in_dim(grad_split, 1 - core, 2, False)
+    w_all, g_all = fetch(out_weight, grad_out, count, lanes)
 
     streams = jnp.stack([query, key, value])
     before = from_behind(streams[:, tok_rows - (tap_count - 1) :, :], "seq", 1)
@@ -125,9 +256,7 @@
     fwd_sums = prefix(lower, grow, gated)
     fwd_final = shrink[tok_rows - 1] * fwd_sums[tok_rows - 1]
 
-    grad_mixer = jnp.einsum(
-        "tzc,zrc->tr", grad_mine, mine, preferred_element_type=jnp.float32
-    ) + jnp.einsum("tzc,zrc->tr", grad_other, other, preferred_element_type=jnp.float32)
+    grad_mixer = jnp.einsum("jtc,jrc->tr", g_all, w_all, preferred_element_type=jnp.float32)
     grad_long = grad_mixer * q_short
     bwd_sums = prefix(upper, shrink, grad_long)
     bwd_final = bwd_sums[0]
@@ -149,15 +278,8 @@
         jnp.sum(scaled_shrink * (fwd_sums + fwd_entry[None]), axis=1) + skip_gain[None, :] * gated
     )
     mixer = (q_short * long_out).astype(jnp.bfloat16)
-    part_mine = jnp.einsum("tr,zrc->ztc", mixer, mine, preferred_element_type=jnp.float32)
-    part_other = jnp.einsum("tr,zrc->ztc", mixer, other, preferred_element_type=jnp.float32)
-    part_mine = part_mine.astype(jnp.bfloat16)
-    part_other = part_other.astype(jnp.bfloat16)
-    parts = jnp.where(
-        core == 0,
-        jnp.stack([part_mine, part_other], axis=1),
-        jnp.stack([part_other, part_mine], axis=1),
-    ).reshape(count, tok_rows, chan_width)
+    parts = jnp.einsum("tr,jrc->jtc", mixer, w_all, preferred_element_type=jnp.float32)
+    parts = parts.astype(jnp.bfloat16)
     received = lax.all_to_all(parts, "ch", 0, 0, tiled=True)
     mixed = jnp.sum(received.astype(jnp.float32), axis=0).astype(jnp.bfloat16)
 

time: 233 us -> 186 us (0.80)
  waiting for transfers between devices: 114 us -> 29.8 us
  Pallas kernels: 33.4 us -> 93.4 us
  between operations: 14.6 us -> 1.02 us
  starting transfers between devices: 17.8 us -> 9.74 us
    pallas_call x0 -> x1, Pallas kernels: none -> 63.2 us  [fetch(): pl.pallas_call(functools.partial(fetch_kernel, count, lanes), out_shape=(...]
    all_gather x1 -> x0, waiting for transfers between devices: 56.9 us -> none  [per_device(): mine = lax.all_gather(out_weight, 'seq', axis_index_groups=groups)]
    all_to_all x1 -> x0, waiting for transfers between devices: 25.7 us -> none  [per_device(): grad_blocks = lax.all_to_all(grad_copies, 'ch', 0, 0, tiled=True)]
    all_to_all x1 -> x0, starting transfers between devices: 6.53 us -> none  [per_device(): grad_blocks = lax.all_to_all(grad_copies, 'ch', 0, 0, tiled=True)]
    pallas_call x1, Pallas kernels: 33.4 us -> 30.2 us  [exchange(): pl.pallas_call(functools.partial(exchange_kernel, count), out_shape=jax.S...]
    broadcast_in_dim x1 -> x0, local copies, waits for them, and re-layouts: 2.45 us -> none  [per_device(): grad_copies = jnp.broadcast_to(grad_out[None], (lanes,) + grad_out.shape)]
    unnamed x42 -> x35, local copies, waits for them, and re-layouts: 17.7 us -> 19.5 us
    dot_general x4 -> x2, matrix products: 11.6 us -> 10.6 us  [the longest x1 6.87 us: per_device(): jnp.einsum('jtc,jrc->tr', g_all, w_all, preferred_element_type=jnp.float32)]
  transfers between devices with their start and end apart: 6 -> 3, of which waited for: 4 -> 2; matrix products, arithmetic and copies ran while one was open for 4% -> 4% of each run, Pallas kernels for 0% -> 34%
where the time goes in v5:
time: 186 us
  Pallas kernels  93.4 us (50%)
  waiting for transfers between devices  29.8 us (16%)
  local copies, waits for them, and re-layouts  22.3 us (12%)
  matrix products  16.9 us (9%)
  other arithmetic  12.7 us (7%)
  starting transfers between devices  9.74 us (5%)
    pallas_call x1, Pallas kernels, fetch(): pl.pallas_call(functools.partial(fetch_kernel, count, lanes), out_shape=(...  63.2 us
    pallas_call x1, Pallas kernels, exchange(): pl.pallas_call(functools.partial(exchange_kernel, count), out_shape=jax.S...  30.2 us
    all_to_all x1, waiting for transfers between devices, per_device(): received = lax.all_to_all(parts, 'ch', 0, 0, tiled=True)  26.4 us
    unnamed x35, local copies, waits for them, and re-layouts  19.5 us
    dot_general x1, matrix products, per_device(): jnp.einsum('jtc,jrc->tr', g_all, w_all, preferred_element_type=jnp.float32)  6.87 us
    dot_general x2, matrix products, prefix(): jnp.dot(tri, spread, precision=highest, preferred_element_type=jnp.float32)  6.34 us
    ppermute x2, starting transfers between devices, from_behind(): return lax.ppermute(block, axis, route)  6.03 us
    reduce_sum x1, other arithmetic, per_device(): jnp.sum(scaled_grow * (bwd_sums + bwd_entry[None]), axis=1)  4.52 us
  transfers between devices with their start and end apart: 3, of which 2 were waited for; matrix products, arithmetic and copies ran while one was open for 4% of the time, Pallas kernels for 34%

profile of v5, /device:TPU:65, one launch (start us, length us, event | category | flops | bytes accessed | tf_op | source)
XLA Modules:
  0.0 185.9 jit_solution(7894619258384968128)
XLA Ops:
  0.7 0.8 pad_maximum_fusion.3
  1.5 4.1 %collective-permute-start = (bf16[3,2,512]{2,1,0:T(2,128)(2,1)S(1)}, bf16[3,2,512]{2,1,0:T(2,128)(2,1)S(1)}, u32[]{:S(2)}, u32[]{:S(2)}) collective-permute-start(bf16[3,2,512]{2,1,0:T(2,128)(2,1)S(1)} %pad_maximum_fusion.3), channel_id=1, source_target_pairs={{0,16},{16,32},{32,48},{48,64},{64,80},{80,96},{96,112},{112,128},... | collective-permute-start | bytes 18440 | tf_op jit(solution)/shard_map/ppermute | solution.py:71
  6.3 0.8 fusion.29
  7.1 2.6 %multiply_exponential_fusion = f32[128,16,512]{2,1,0:T(8,128)} fusion(f32[128]{0:T(128)S(1)} %iota_convert_fusion, f32[16,512]{1,0:T(8,128)S(1)} %get-tuple-element.26), kind=kLoop, calls=%fused_computation.14 | loop fusion | flops 1048576 | bytes 4227584 | tf_op jit(solution)/shard_map/exp | solution.py:241
  9.7 63.2 %shard_map.120 = (bf16[16,512,512]{2,1,0:T(8,128)(2,1)}, bf16[16,128,512]{2,1,0:T(8,128)(2,1)}) custom-call(bf16[512,512]{1,0:T(8,128)(2,1)} %w_ref.1, bf16[128,512]{1,0:T(8,128)(2,1)} %g_ref.1), custom_call_target="tpu_custom_call" | custom-call | tf_op jit(solution)/shard_map/pallas_call | solution.py:195
  73.4 1.2 copy-done.5
  74.5 6.9 %fusion.24 = (f32[128,512]{1,0:T(8,128)S(1)}, f32[128,512]{1,0:T(8,128)S(1)}, f32[128,512]{1,0:T(8,128)}) fusion(f32[3,128,512]{2,1,0:T(8,128)S(1)} %fusion.19, bf16[16,128,512]{2,1,0:T(8,128)(2,1)S(1)} %copy-done.5, bf16[16,512,512]{2,1,0:T(8,128)(2,1)} %get-tuple-element.6), kind=kOutput, calls=%fused_computation.48 | convolution fusion | flops 1073872896 | bytes 12058624 | tf_op jit(solution)/shard_map/jtc,jrc->tr/dot_general | solution.py:259
  82.0 3.4 %copy.24 = f32[16,8,16,512]{3,1,2,0:T(8,128)S(1)} copy(f32[16,8,16,512]{3,2,1,0:T(8,128)S(1)} %bitcast.91) | data formatting | bytes 8388608
  85.9 3.4 %copy.21 = f32[16,8,16,512]{3,1,2,0:T(8,128)S(1)} copy(f32[16,8,16,512]{3,2,1,0:T(8,128)S(1)} %bitcast.92) | data formatting | bytes 8388608
  89.4 3.2 %fusion.4 = f32[128,8192]{1,0:T(8,128)S(1)} fusion(f32[128,8192]{1,0:T(8,128)S(1)} %bitcast.89, f32[8192]{0:T(1024)S(1)} %bitcast.101, f32[128]{0:T(128)S(1)} %iota_convert_fusion), kind=kOutput, calls=%fused_computation.6 | convolution fusion | flops 1612726272 | bytes 8421888 | tf_op jit(solution)/shard_map/dot_general | solution.py:253
  92.6 3.1 %fusion.8 = f32[128,8192]{1,0:T(8,128)S(1)} fusion(f32[128,8192]{1,0:T(8,128)S(1)} %bitcast.90, f32[128]{0:T(128)S(1)} %iota_convert_fusion, f32[8192]{0:T(1024)S(1)} %bitcast.100), kind=kOutput, calls=%fused_computation.10 | convolution fusion | flops 1612726272 | bytes 8421888 | tf_op jit(solution)/shard_map/dot_general | solution.py:253
  95.9 1.7 copy-done.1
  97.7 0.8 slice_multiply_fusion.5
  99.1 30.2 %shard_map.121 = f32[16,2,16,512]{3,2,1,0:T(8,128)} custom-call(f32[2,16,512]{2,1,0:T(8,128)} %pad_maximum_fusion.2.final_ref), custom_call_target="tpu_custom_call" | custom-call | tf_op jit(solution)/shard_map/pallas_call | solution.py:54
  129.3 5.6 %copy.25 = f32[16,8,16,512]{3,2,1,0:T(8,128)S(1)} copy(f32[16,8,16,512]{3,1,2,0:T(8,128)} %bitcast.87) | data formatting | bytes 8388608
  135.0 3.3 %copy.22 = f32[16,8,16,512]{3,2,1,0:T(8,128)S(1)} copy(f32[16,8,16,512]{3,1,2,0:T(8,128)S(1)} %bitcast.88) | data formatting | bytes 8388608
  138.7 4.5 %fusion.1 = (f32[128,512]{1,0:T(8,128)}, f32[128,512]{1,0:T(8,128)S(1)}) fusion(f32[16,8,16,512]{3,2,1,0:T(8,128)S(1)} %copy.25, f32[16,512]{1,0:T(8,128)S(1)} %get-tuple-element.24, f32[16,512]{1,0:T(8,128)S(1)} %copy-done.6, f32[128]{0:T(128)S(1)} %iota_convert_fusion, f32[16,512]{1,0:T(8,128)S(1)} %get-tuple-element.25, ...), kind=kLoop, calls=%fused_computation.2 | loop fusion | flops 10354688 | bytes 9077248 | tf_op jit(solution)/shard_map/reduce_sum | solution.py:288
  143.2 3.7 %convert_bitcast_fusion = bf16[16,128,512]{1,2,0:T(8,128)(2,1)} fusion(bf16[16,512,512]{2,1,0:T(8,128)(2,1)S(1)} %bitcast.86, f32[3,128,512]{2,1,0:T(8,128)S(1)} %fusion.19, f32[128,512]{1,0:T(8,128)S(1)} %get-tuple-element.15, f32[128,512]{1,0:T(8,128)S(1)} %get-tuple-element.18, f32[512]{0:T(512)S(1)} %copy-done.11), kind=kOutput, calls=%fused_computation.15 | convolution fusion | flops 1075052544 | bytes 11274240 | tf_op jit(solution)/shard_map/tr,jrc->jtc/dot_general | solution.py:281
  146.9 3.7 %all-to-all-start = ((bf16[16,128,512]{1,2,0:T(8,128)(2,1)}), bf16[16,128,512]{1,2,0:T(8,128)(2,1)S(1)}, u32[]{:S(2)}, u32[]{:S(2)}) async-start(bf16[16,128,512]{1,2,0:T(8,128)(2,1)} %convert_bitcast_fusion), calls=%async_computation | async-start | bytes 4194304 | tf_op jit(solution)/shard_map/all_to_all | solution.py:283
  150.7 1.3 multiply_bitcast_fusion.1
  152.0 1.9 %collective-permute-start.1 = (f32[3,2,512]{2,1,0:T(2,128)S(1)}, f32[3,2,512]{2,1,0:T(2,128)S(1)}, u32[]{:S(2)}, u32[]{:S(2)}) collective-permute-start(f32[3,2,512]{2,1,0:T(2,128)S(1)} %slice.101), channel_id=1, source_target_pairs={{16,0},{32,16},{48,32},{64,48},{80,64},{96,80},{112,96},{128,112},... | collective-permute-start | bytes 36872 | tf_op jit(solution)/shard_map/ppermute | solution.py:71
  154.0 3.4 %collective-permute-done.1 = f32[3,2,512]{2,1,0:T(2,128)S(1)} collective-permute-done((f32[3,2,512]{2,1,0:T(2,128)S(1)}, f32[3,2,512]{2,1,0:T(2,128)S(1)}, u32[]{:S(2)}, u32[]{:S(2)}) %collective-permute-start.1) | collective-permute-done | bytes 12320 | tf_op jit(solution)/shard_map/ppermute | solution.py:71
  158.4 26.4 %all-to-all-done = bf16[16,128,512]{1,2,0:T(8,128)(2,1)S(1)} async-done(((bf16[16,128,512]{1,2,0:T(8,128)(2,1)}), bf16[16,128,512]{1,2,0:T(8,128)(2,1)S(1)}, u32[]{:S(2)}, u32[]{:S(2)}) %all-to-all-start) | async-done | bytes 2097184 | tf_op jit(solution)/shard_map/all_to_all | solution.py:283
  185.1 0.8 copy.17
  (50 shorter events, 4.9 us)
Async XLA Ops:
  0.6 72.3 %copy-start.9 = (bf16[128,512]{1,0:T(8,128)(2,1)S(1)}, bf16[128,512]{1,0:T(8,128)(2,1)}, u32[]{:S(2)}) copy-start(bf16[128,512]{1,0:T(8,128)(2,1)} %param.9) | copy-start | bytes 393220
  0.6 72.3 %copy-start.8 = (bf16[128,512]{1,0:T(8,128)(2,1)S(1)}, bf16[128,512]{1,0:T(8,128)(2,1)}, u32[]{:S(2)}) copy-start(bf16[128,512]{1,0:T(8,128)(2,1)} %param.10) | copy-start | bytes 393220
  0.7 72.3 %copy-start.7 = (bf16[128,512]{1,0:T(8,128)(2,1)S(1)}, bf16[128,512]{1,0:T(8,128)(2,1)}, u32[]{:S(2)}) copy-start(bf16[128,512]{1,0:T(8,128)(2,1)} %param.11) | copy-start | bytes 393220
  0.7 9.0 %copy-start.6 = (f32[16,512]{1,0:T(8,128)S(1)}, f32[16,512]{1,0:T(8,128)}, u32[]{:S(2)}) copy-start(f32[16,512]{1,0:T(8,128)} %param.13) | copy-start | bytes 98308
  1.5 71.5 %collective-permute-start = (bf16[3,2,512]{2,1,0:T(2,128)(2,1)S(1)}, bf16[3,2,512]{2,1,0:T(2,128)(2,1)S(1)}, u32[]{:S(2)}, u32[]{:S(2)}) collective-permute-start(bf16[3,2,512]{2,1,0:T(2,128)(2,1)S(1)} %pad_maximum_fusion.3), channel_id=1, source_target_pairs={{0,16},{16,32},{32,48},{48,64},{64,80},{80,96},{96,112},{112,128},... | collective-permute-start | bytes 18440 | tf_op jit(solution)/shard_map/ppermute | solution.py:71
  73.0 1.6 copy-start.5
  81.4 4.0 %copy-start.4 = (f32[128,512]{1,0:T(8,128)}, f32[128,512]{1,0:T(8,128)S(1)}, u32[]{:S(2)}) copy-start(f32[128,512]{1,0:T(8,128)S(1)} %get-tuple-element.19) | copy-start | bytes 786436
  92.6 3.2 %copy-start = (f32[128,8192]{1,0:T(8,128)}, f32[128,8192]{1,0:T(8,128)S(1)}, u32[]{:S(2)}) copy-start(f32[128,8192]{1,0:T(8,128)S(1)} %fusion.4) | copy-start | bytes 12582916
  95.7 1.9 %copy-start.1 = (f32[128,8192]{1,0:T(8,128)}, f32[128,8192]{1,0:T(8,128)S(1)}, u32[]{:S(2)}) copy-start(f32[128,8192]{1,0:T(8,128)S(1)} %fusion.8) | copy-start | bytes 12582916
  129.3 5.6 %copy-start.2 = (f32[128,8192]{1,0:T(8,128)S(1)}, f32[128,8192]{1,0:T(8,128)}, u32[]{:S(2)}) copy-start(f32[128,8192]{1,0:T(8,128)} %copy-done.1) | copy-start | bytes 12582916
  135.0 3.3 %copy-start.3 = (f32[16,2,16,512]{3,2,1,0:T(8,128)S(1)}, f32[16,2,16,512]{3,2,1,0:T(8,128)}, u32[]{:S(2)}) copy-start(f32[16,2,16,512]{3,2,1,0:T(8,128)} %shard_map.121) | copy-start | bytes 3145732
  135.0 3.6 %copy-start.10 = (f32[16,512]{1,0:T(8,128)S(1)}, f32[16,512]{1,0:T(8,128)}, u32[]{:S(2)}) copy-start(f32[16,512]{1,0:T(8,128)} %param.14) | copy-start | bytes 98308
  135.0 8.2 %slice-start = ((s8[8388608]{0:T(1024)(128)(4,1)}), s8[4194304]{0:T(1024)(128)(4,1)S(1)}, s32[]{:S(2)}) async-start(s8[8388608]{0:T(1024)(128)(4,1)} %bitcast.85), calls=%async_computation.1 | async-start | bytes 8388608
  138.3 4.9 %slice-start.1 = ((s8[8388608]{0:T(1024)(128)(4,1)}), s8[4194304]{0:T(1024)(128)(4,1)S(1)}, s32[]{:S(2)}) async-start(s8[8388608]{0:T(1024)(128)(4,1)} %bitcast.85), calls=%async_computation.2 | async-start | bytes 8388608
  138.7 4.5 %copy-start.11 = (f32[512]{0:T(512)S(1)}, f32[512]{0:T(512)}, u32[]{:S(2)}) copy-start(f32[512]{0:T(512)} %param.15) | copy-start | bytes 6148
  146.9 37.9 %all-to-all-start = ((bf16[16,128,512]{1,2,0:T(8,128)(2,1)}), bf16[16,128,512]{1,2,0:T(8,128)(2,1)S(1)}, u32[]{:S(2)}, u32[]{:S(2)}) async-start(bf16[16,128,512]{1,2,0:T(8,128)(2,1)} %convert_bitcast_fusion), calls=%async_computation | async-start | bytes 4194304 | tf_op jit(solution)/shard_map/all_to_all | solution.py:283
  152.0 5.3 %collective-permute-start.1 = (f32[3,2,512]{2,1,0:T(2,128)S(1)}, f32[3,2,512]{2,1,0:T(2,128)S(1)}, u32[]{:S(2)}, u32[]{:S(2)}) collective-permute-start(f32[3,2,512]{2,1,0:T(2,128)S(1)} %slice.101), channel_id=1, source_target_pairs={{16,0},{32,16},{48,32},{64,48},{80,64},{96,80},{112,96},{128,112},... | collective-permute-start | bytes 36872 | tf_op jit(solution)/shard_map/ppermute | solution.py:71

commit v6 on v5

--- a/solution.py
+++ b/solution.py
@@ -10,7 +10,7 @@
 MESH = pl.DeviceIdType.MESH
 
 
-def exchange_kernel(count, final_ref, out_ref, slots, send_sems, recv_sems):
+def exchange_kernel(count, final_ref, fwd_ref, bwd_ref, send_sems, recv_sems):
     me = lax.axis_index("seq")
     lane = lax.axis_index("ch")
     barrier = pltpu.get_barrier_semaphore()
@@ -22,10 +22,10 @@
 
     pl.semaphore_wait(barrier, count - 1)
 
-    def link(peer, slot):
+    def link(peer, later, slot):
         return pltpu.make_async_remote_copy(
-            src_ref=final_ref,
-            dst_ref=slots.at[slot],
+            src_ref=final_ref.at[0 if later else 1],
+            dst_ref=(fwd_ref if later else bwd_ref).at[slot],
             send_sem=send_sems.at[peer],
             recv_sem=recv_sems.at[slot],
             device_id=(peer, lane),
@@ -34,35 +34,98 @@
 
     for peer in range(count):
 
-        @pl.when(me != peer)
-        def _():
-            link(peer, me).start()
-
-    slots[me] = final_ref[...]
+        @pl.when(me < peer)
+        def _():
+            link(peer, True, me).start()
+
+        @pl.when(me > peer)
+        def _():
+            link(peer, False, me).start()
+
     for peer in range(count):
 
-        @pl.when(me != peer)
-        def _():
-            link(peer, me).wait_send()
-            link(peer, peer).wait_recv()
-
-    out_ref[...] = slots[...]
+        @pl.when(me < peer)
+        def _():
+            link(peer, True, me).wait_send()
+            link(peer, False, peer).wait_recv()
+
+        @pl.when(me > peer)
+        def _():
+            link(peer, False, me).wait_send()
+            link(peer, True, peer).wait_recv()
 
 
 def exchange(final, count):
-    shape = (count,) + final.shape
+    shape = (count,) + final.shape[1:]
     return pl.pallas_call(
         functools.partial(exchange_kernel, count),
-        out_shape=jax.ShapeDtypeStruct(shape, final.dtype),
+        out_shape=(
+            jax.ShapeDtypeStruct(shape, final.dtype),
+            jax.ShapeDtypeStruct(shape, final.dtype),
+        ),
         in_specs=[pl.BlockSpec(memory_space=pltpu.VMEM)],
-        out_specs=pl.BlockSpec(memory_space=pltpu.VMEM),
+        out_specs=(pl.BlockSpec(memory_space=pltpu.VMEM), pl.BlockSpec(memory_space=pltpu.VMEM)),
         scratch_shapes=[
-            pltpu.VMEM(shape, final.dtype),
             pltpu.SemaphoreType.DMA((count,)),
             pltpu.SemaphoreType.DMA((count,)),
         ],
         compiler_params=pltpu.CompilerParams(collective_id=0, has_side_effects=True),
     )(final)
+
+
+def scatter_kernel(lanes, parts_ref, out_ref, send_sems, recv_sems, own_sem):
+    me = lax.axis_index("seq")
+    lane = lax.axis_index("ch")
+    barrier = pltpu.get_barrier_semaphore()
+    for other in range(lanes):
+
+        @pl.when(lane != other)
+        def _():
+            pl.semaphore_signal(barrier, inc=1, device_id=(me, other), device_id_type=MESH)
+
+    pl.semaphore_wait(barrier, lanes - 1)
+
+    def link(other, slot):
+        return pltpu.make_async_remote_copy(
+            src_ref=parts_ref.at[other],
+            dst_ref=out_ref.at[slot],
+            send_sem=send_sems.at[other],
+            recv_sem=recv_sems.at[slot],
+            device_id=(me, other),
+            device_id_type=MESH,
+        )
+
+    for other in range(lanes):
+
+        @pl.when(lane != other)
+        def _():
+            link(other, lane).start()
+
+    own = pltpu.make_async_copy(parts_ref.at[lane], out_ref.at[lane], own_sem.at[0])
+    own.start()
+    for other in range(lanes):
+
+        @pl.when(lane != other)
+        def _():
+            link(other, lane).wait_send()
+            link(other, other).wait_recv()
+
+    own.wait()
+
+
+def scatter(parts, lanes):
+    return pl.pallas_call(
+        functools.partial(scatter_kernel, lanes),
+        out_shape=jax.ShapeDtypeStruct(parts.shape, parts.dtype),
+        in_specs=[pl.BlockSpec(memory_space=pl.ANY)],
+        out_specs=pl.BlockSpec(memory_space=pl.ANY),
+        scratch_shapes=[
+            pltpu.SemaphoreType.DMA((lanes,)),
+            pltpu.SemaphoreType.DMA((lanes,)),
+            pltpu.SemaphoreType.DMA((1,)),
+        ],
+        compiler_params=pltpu.CompilerParams(collective_id=2, has_side_effects=True),
+    )(parts)
 
 
 def from_behind(block, axis, distance):
@@ -261,18 +324,19 @@
     bwd_sums = prefix(upper, shrink, grad_long)
     bwd_final = bwd_sums[0]
 
-    finals = jnp.stack([fwd_final, bwd_final])
-    gathered = exchange(finals, count)
+    finals = jnp.stack([fwd_final, bwd_final]).astype(jnp.bfloat16)
+    fwd_got, bwd_got = exchange(finals, count)
     source = jnp.arange(count)
     fwd_gap = place - 1 - source
     bwd_gap = source - place - 1
 
-    def weights(gap):
+    def entry(gap, got):
         span = (tok_rows * jnp.maximum(gap, 0)).astype(jnp.float32)[:, None, None]
-        return jnp.where((gap >= 0)[:, None, None], jnp.exp(-decay_rate[None] * span), 0.0)
-
-    fwd_entry = jnp.sum(weights(fwd_gap) * gathered[:, 0], axis=0) * one_step
-    bwd_entry = jnp.sum(weights(bwd_gap) * gathered[:, 1], axis=0) * block_decay
+        held = jnp.where((gap >= 0)[:, None, None], got.astype(jnp.float32), 0.0)
+        return jnp.sum(jnp.exp(-decay_rate[None] * span) * held, axis=0)
+
+    fwd_entry = entry(fwd_gap, fwd_got) * one_step
+    bwd_entry = entry(bwd_gap, bwd_got) * block_decay
 
     long_out = (
         jnp.sum(scaled_shrink * (fwd_sums + fwd_entry[None]), axis=1) + skip_gain[None, :] * gated
@@ -280,7 +344,7 @@
     mixer = (q_short * long_out).astype(jnp.bfloat16)
     parts = jnp.einsum("tr,jrc->jtc", mixer, w_all, preferred_element_type=jnp.float32)
     parts = parts.astype(jnp.bfloat16)
-    received = lax.all_to_all(parts, "ch", 0, 0, tiled=True)
+    received = scatter(parts, lanes)
     mixed = jnp.sum(received.astype(jnp.float32), axis=0).astype(jnp.bfloat16)
 
     grad_qshort = grad_mixer * long_out

time: 186 us -> 180 us (0.968); the launches traced: 186 us -> 177 us
  waiting for transfers between devices: 29.8 us -> 0.01 us
  Pallas kernels: 93.4 us -> 118 us
  starting transfers between devices: 9.74 us -> 6.41 us
  matrix products: 16.9 us -> 14.8 us
    all_to_all x1 -> x0, waiting for transfers between devices: 26.4 us -> none  [per_device(): received = lax.all_to_all(parts, 'ch', 0, 0, tiled=True)]
    pallas_call x1 -> x2, Pallas kernels: 30.2 us -> 54.5 us  [the longest x1 41.4 us: scatter(): pl.pallas_call(functools.partial(scatter_kernel, lanes), out_shape=jax.Sh...]
    all_to_all x1 -> x0, starting transfers between devices: 3.72 us -> none  [per_device(): received = lax.all_to_all(parts, 'ch', 0, 0, tiled=True)]
    ppermute x2, waiting for transfers between devices: 3.38 us -> 0.01 us  [from_behind(): return lax.ppermute(block, axis, route)]
    reduce_sum x1, other arithmetic: 0.29 us -> 2.57 us  [per_device(): mixed = jnp.sum(received.astype(jnp.float32), axis=0).astype(jnp.bfloat16)]
    unnamed x35 -> x34, local copies, waits for them, and re-layouts: 19.5 us -> 21 us
  transfers between devices with their start and end apart: 3 -> 2, of which waited for: 2 -> 0; matrix products, arithmetic and copies ran while one was open for 4% -> 5% of each run, Pallas kernels for 34% -> 59%
where the time goes in v6:
time: 180 us; the launch traced here: 177 us
  Pallas kernels  118 us (66%)
  local copies, waits for them, and re-layouts  23.8 us (13%)
  matrix products  14.8 us (8%)
  other arithmetic  13.2 us (7%)
  starting transfers between devices  6.41 us (4%)
    pallas_call x1, Pallas kernels, fetch(): pl.pallas_call(functools.partial(fetch_kernel, count, lanes), out_shape=(...  63.2 us
    pallas_call x1, Pallas kernels, scatter(): pl.pallas_call(functools.partial(scatter_kernel, lanes), out_shape=jax.Sh...  41.4 us
    unnamed x34, local copies, waits for them, and re-layouts  21 us
    pallas_call x1, Pallas kernels, exchange(): pl.pallas_call(functools.partial(exchange_kernel, count), out_shape=(jax....  13.1 us
    ppermute x2, starting transfers between devices, from_behind(): return lax.ppermute(block, axis, route)  6.41 us
    dot_general x1, matrix products, per_device(): jnp.einsum('jtc,jrc->tr', g_all, w_all, preferred_element_type=jnp.float32)  6.16 us
    dot_general x2, matrix products, prefix(): jnp.dot(tri, spread, precision=highest, preferred_element_type=jnp.float32)  6.02 us
    reduce_sum x1, other arithmetic, per_device(): jnp.sum(scaled_grow * (bwd_sums + bwd_entry[None]), axis=1)  3.82 us
  transfers between devices with their start and end apart: 2, of which 0 were waited for; matrix products, arithmetic and copies ran while one was open for 5% of the time, Pallas kernels for 59%

profile of v6, /device:TPU:65, one launch (start us, length us, event | category | flops | bytes accessed | tf_op | source)
XLA Modules:
  0.0 177.0 jit_solution(2559913157054658587)
XLA Ops:
  0.7 0.8 pad_maximum_fusion.3
  1.5 4.1 %collective-permute-start = (bf16[3,2,512]{2,1,0:T(2,128)(2,1)S(1)}, bf16[3,2,512]{2,1,0:T(2,128)(2,1)S(1)}, u32[]{:S(2)}, u32[]{:S(2)}) collective-permute-start(bf16[3,2,512]{2,1,0:T(2,128)(2,1)S(1)} %pad_maximum_fusion.3), channel_id=1, source_target_pairs={{0,16},{16,32},{32,48},{48,64},{64,80},{80,96},{96,112},{112,128},... | collective-permute-start | bytes 18440 | tf_op jit(solution)/shard_map/ppermute | solution.py:134
  5.6 0.7 slice_bitcast_fusion.8
  6.3 0.8 fusion.29
  7.1 2.6 %multiply_exponential_fusion = f32[128,16,512]{2,1,0:T(8,128)} fusion(f32[128]{0:T(128)S(1)} %iota_convert_fusion, f32[16,512]{1,0:T(8,128)S(1)} %get-tuple-element.26), kind=kLoop, calls=%fused_computation.14 | loop fusion | flops 1048576 | bytes 4227584 | tf_op jit(solution)/shard_map/exp | solution.py:304
  9.7 63.2 %shard_map.120 = (bf16[16,512,512]{2,1,0:T(8,128)(2,1)}, bf16[16,128,512]{2,1,0:T(8,128)(2,1)}) custom-call(bf16[512,512]{1,0:T(8,128)(2,1)} %w_ref.1, bf16[128,512]{1,0:T(8,128)(2,1)} %g_ref.1), custom_call_target="tpu_custom_call" | custom-call | tf_op jit(solution)/shard_map/pallas_call | solution.py:258
  73.4 1.2 copy-done.3
  74.6 6.2 %fusion.22 = (f32[128,512]{1,0:T(8,128)S(1)}, f32[128,512]{1,0:T(8,128)S(1)}, f32[128,512]{1,0:T(8,128)S(1)}) fusion(f32[3,128,512]{2,1,0:T(8,128)S(1)} %fusion.19, bf16[16,128,512]{2,1,0:T(8,128)(2,1)S(1)} %copy-done.3, bf16[16,512,512]{2,1,0:T(8,128)(2,1)} %get-tuple-element.8), kind=kOutput, calls=%fused_computation.46 | convolution fusion | flops 1073872896 | bytes 12058624 | tf_op jit(solution)/shard_map/jtc,jrc->tr/dot_general | solution.py:322
  81.3 3.4 %copy.18 = f32[16,8,16,512]{3,1,2,0:T(8,128)S(1)} copy(f32[16,8,16,512]{3,2,1,0:T(8,128)S(1)} %bitcast.81) | data formatting | bytes 8388608
  84.7 3.0 %fusion.8 = f32[128,8192]{1,0:T(8,128)S(1)} fusion(f32[128,8192]{1,0:T(8,128)S(1)} %bitcast.79, f32[128]{0:T(128)S(1)} %iota_convert_fusion, f32[8192]{0:T(1024)S(1)} %bitcast.91), kind=kOutput, calls=%fused_computation.10 | convolution fusion | flops 1612726272 | bytes 8421888 | tf_op jit(solution)/shard_map/dot_general | solution.py:316
  87.7 1.9 %copy-done = f32[128,8192]{1,0:T(8,128)} copy-done((f32[128,8192]{1,0:T(8,128)}, f32[128,8192]{1,0:T(8,128)S(1)}, u32[]{:S(2)}) %copy-start) | copy-done | bytes 4194328
  90.3 3.6 %copy.21 = f32[16,8,16,512]{3,1,2,0:T(8,128)S(1)} copy(f32[16,8,16,512]{3,2,1,0:T(8,128)S(1)} %bitcast.82) | data formatting | bytes 8388608
  93.9 3.0 %fusion.4 = f32[128,8192]{1,0:T(8,128)S(1)} fusion(f32[128,8192]{1,0:T(8,128)S(1)} %bitcast.80, f32[8192]{0:T(1024)S(1)} %bitcast.90, f32[128]{0:T(128)S(1)} %iota_convert_fusion), kind=kOutput, calls=%fused_computation.6 | convolution fusion | flops 1612726272 | bytes 8421888 | tf_op jit(solution)/shard_map/dot_general | solution.py:316
  96.9 1.9 %copy-done.2 = f32[128,8192]{1,0:T(8,128)} copy-done((f32[128,8192]{1,0:T(8,128)}, f32[128,8192]{1,0:T(8,128)S(1)}, u32[]{:S(2)}) %copy-start.2) | copy-done | bytes 4194328
  99.0 0.8 fusion.26
  100.3 13.1 %shard_map.121 = (bf16[16,16,512]{2,1,0:T(8,128)(2,1)}, bf16[16,16,512]{2,1,0:T(8,128)(2,1)}) custom-call(bf16[2,16,512]{2,1,0:T(8,128)(2,1)} %pad_maximum_fusion.2.final_ref), custom_call_target="tpu_custom_call" | custom-call | tf_op jit(solution)/shard_map/pallas_call | solution.py:60
  113.5 5.6 %copy.22 = f32[16,8,16,512]{3,2,1,0:T(8,128)S(1)} copy(f32[16,8,16,512]{3,1,2,0:T(8,128)} %bitcast.78) | data formatting | bytes 8388608
  119.1 3.3 %copy.19 = f32[16,8,16,512]{3,2,1,0:T(8,128)S(1)} copy(f32[16,8,16,512]{3,1,2,0:T(8,128)S(1)} %bitcast.77) | data formatting | bytes 8388608
  122.9 3.8 %fusion.1 = (f32[128,512]{1,0:T(8,128)S(1)}, f32[128,512]{1,0:T(8,128)S(1)}) fusion(f32[16,8,16,512]{3,2,1,0:T(8,128)S(1)} %copy.22, f32[16,512]{1,0:T(8,128)S(1)} %get-tuple-element.24, f32[16,512]{1,0:T(8,128)S(1)} %copy-done.4, f32[128]{0:T(128)S(1)} %iota_convert_fusion, f32[16,512]{1,0:T(8,128)S(1)} %get-tuple-element.25, ...), kind=kLoop, calls=%fused_computation.2 | loop fusion | flops 10354688 | bytes 9077248 | tf_op jit(solution)/shard_map/reduce_sum | solution.py:352
  127.0 2.3 %collective-permute-start.1 = (f32[3,2,512]{2,1,0:T(2,128)S(1)}, f32[3,2,512]{2,1,0:T(2,128)S(1)}, u32[]{:S(2)}, u32[]{:S(2)}) collective-permute-start(f32[3,2,512]{2,1,0:T(2,128)S(1)} %slice.94), channel_id=1, source_target_pairs={{16,0},{32,16},{48,32},{64,48},{80,64},{96,80},{112,96},{128,112},... | collective-permute-start | bytes 36872 | tf_op jit(solution)/shard_map/ppermute | solution.py:134
  129.3 2.6 %convert_bitcast_fusion.parts_ref = bf16[16,128,512]{2,1,0:T(8,128)(2,1)} fusion(bf16[16,512,512]{2,1,0:T(8,128)(2,1)S(1)} %bitcast.76, f32[3,128,512]{2,1,0:T(8,128)S(1)} %fusion.19, f32[128,512]{1,0:T(8,128)S(1)} %get-tuple-element.13, f32[128,512]{1,0:T(8,128)S(1)} %get-tuple-element.18, f32[512]{0:T(512)S(1)} %copy-done.11), kind=kOutput, calls=%fused_computation.15 | convolution fusion | flops 1075052544 | bytes 11274240 | tf_op jit(solution)/shard_map/tr,jrc->jtc/dot_general | solution.py:345
  131.9 41.4 %shard_map.122 = bf16[16,128,512]{2,1,0:T(8,128)(2,1)} custom-call(bf16[16,128,512]{2,1,0:T(8,128)(2,1)} %convert_bitcast_fusion.parts_ref), custom_call_target="tpu_custom_call" | custom-call | tf_op jit(solution)/shard_map/pallas_call | solution.py:117
  173.3 2.6 %reduce_sum.50 = bf16[128,512]{1,0:T(8,128)(2,1)} reduce(bf16[16,128,512]{2,1,0:T(8,128)(2,1)} %shard_map.122, bf16[]{:T(256)} %constant.20.clone.1), dimensions={0}, to_apply=%region_2.3 | reduce | flops 983040 | bytes 2228226 | tf_op jit(solution)/shard_map/reduce_sum | solution.py:348
  176.2 0.8 slice_bitcast_fusion.3
  (49 shorter events, 3.3 us)
Async XLA Ops:
  0.6 72.4 %copy-start.7 = (bf16[128,512]{1,0:T(8,128)(2,1)S(1)}, bf16[128,512]{1,0:T(8,128)(2,1)}, u32[]{:S(2)}) copy-start(bf16[128,512]{1,0:T(8,128)(2,1)} %param.9) | copy-start | bytes 393220
  0.6 72.4 %copy-start.6 = (bf16[128,512]{1,0:T(8,128)(2,1)S(1)}, bf16[128,512]{1,0:T(8,128)(2,1)}, u32[]{:S(2)}) copy-start(bf16[128,512]{1,0:T(8,128)(2,1)} %param.10) | copy-start | bytes 393220
  0.7 72.4 %copy-start.5 = (bf16[128,512]{1,0:T(8,128)(2,1)S(1)}, bf16[128,512]{1,0:T(8,128)(2,1)}, u32[]{:S(2)}) copy-start(bf16[128,512]{1,0:T(8,128)(2,1)} %param.11) | copy-start | bytes 393220
  0.7 9.0 %copy-start.4 = (f32[16,512]{1,0:T(8,128)S(1)}, f32[16,512]{1,0:T(8,128)}, u32[]{:S(2)}) copy-start(f32[16,512]{1,0:T(8,128)} %param.13) | copy-start | bytes 98308
  1.5 71.5 %collective-permute-start = (bf16[3,2,512]{2,1,0:T(2,128)(2,1)S(1)}, bf16[3,2,512]{2,1,0:T(2,128)(2,1)S(1)}, u32[]{:S(2)}, u32[]{:S(2)}) collective-permute-start(bf16[3,2,512]{2,1,0:T(2,128)(2,1)S(1)} %pad_maximum_fusion.3), channel_id=1, source_target_pairs={{0,16},{16,32},{32,48},{48,64},{64,80},{80,96},{96,112},{112,128},... | collective-permute-start | bytes 18440 | tf_op jit(solution)/shard_map/ppermute | solution.py:134
  73.0 1.6 copy-start.3
  87.7 1.9 %copy-start = (f32[128,8192]{1,0:T(8,128)}, f32[128,8192]{1,0:T(8,128)S(1)}, u32[]{:S(2)}) copy-start(f32[128,8192]{1,0:T(8,128)S(1)} %fusion.8) | copy-start | bytes 12582916
  96.9 1.9 %copy-start.2 = (f32[128,8192]{1,0:T(8,128)}, f32[128,8192]{1,0:T(8,128)S(1)}, u32[]{:S(2)}) copy-start(f32[128,8192]{1,0:T(8,128)S(1)} %fusion.4) | copy-start | bytes 12582916
  113.5 5.6 %copy-start.1 = (f32[128,8192]{1,0:T(8,128)S(1)}, f32[128,8192]{1,0:T(8,128)}, u32[]{:S(2)}) copy-start(f32[128,8192]{1,0:T(8,128)} %copy-done) | copy-start | bytes 12582916
  119.1 3.3 %copy-start.8 = (bf16[16,16,512]{2,1,0:T(8,128)(2,1)S(1)}, bf16[16,16,512]{2,1,0:T(8,128)(2,1)}, u32[]{:S(2)}) copy-start(bf16[16,16,512]{2,1,0:T(8,128)(2,1)} %get-tuple-element.10) | copy-start | bytes 786436
  119.1 3.3 %copy-start.9 = (bf16[16,16,512]{2,1,0:T(8,128)(2,1)S(1)}, bf16[16,16,512]{2,1,0:T(8,128)(2,1)}, u32[]{:S(2)}) copy-start(bf16[16,16,512]{2,1,0:T(8,128)(2,1)} %get-tuple-element.11) | copy-start | bytes 786436
  119.1 3.7 %copy-start.10 = (f32[16,512]{1,0:T(8,128)S(1)}, f32[16,512]{1,0:T(8,128)}, u32[]{:S(2)}) copy-start(f32[16,512]{1,0:T(8,128)} %param.14) | copy-start | bytes 98308
  119.1 10.2 %slice-start = ((s8[8388608]{0:T(1024)(128)(4,1)}), s8[4194304]{0:T(1024)(128)(4,1)S(1)}, s32[]{:S(2)}) async-start(s8[8388608]{0:T(1024)(128)(4,1)} %bitcast.75), calls=%async_computation | async-start | bytes 8388608
  122.9 3.8 %copy-start.11 = (f32[512]{0:T(512)S(1)}, f32[512]{0:T(512)}, u32[]{:S(2)}) copy-start(f32[512]{0:T(512)} %param.15) | copy-start | bytes 6148
  122.9 6.4 %slice-start.1 = ((s8[8388608]{0:T(1024)(128)(4,1)}), s8[4194304]{0:T(1024)(128)(4,1)S(1)}, s32[]{:S(2)}) async-start(s8[8388608]{0:T(1024)(128)(4,1)} %bitcast.75), calls=%async_computation.1 | async-start | bytes 8388608
  127.0 48.9 %collective-permute-start.1 = (f32[3,2,512]{2,1,0:T(2,128)S(1)}, f32[3,2,512]{2,1,0:T(2,128)S(1)}, u32[]{:S(2)}, u32[]{:S(2)}) collective-permute-start(f32[3,2,512]{2,1,0:T(2,128)S(1)} %slice.94), channel_id=1, source_target_pairs={{16,0},{32,16},{48,32},{64,48},{80,64},{96,80},{112,96},{128,112},... | collective-permute-start | bytes 36872 | tf_op jit(solution)/shard_map/ppermute | solution.py:134

commit v7 on v6

--- a/solution.py
+++ b/solution.py
@@ -344,7 +344,7 @@
     mixer = (q_short * long_out).astype(jnp.bfloat16)
     parts = jnp.einsum("tr,jrc->jtc", mixer, w_all, preferred_element_type=jnp.float32)
     parts = parts.astype(jnp.bfloat16)
-    received = scatter(parts, lanes)
+    received = lax.all_to_all(parts, "ch", 0, 0, tiled=True)
     mixed = jnp.sum(received.astype(jnp.float32), axis=0).astype(jnp.bfloat16)
 
     grad_qshort = grad_mixer * long_out

time: 180 us -> 171 us (0.950); the launches traced: 177 us -> 170 us
  Pallas kernels: 118 us -> 76.3 us
  waiting for transfers between devices: 0.01 us -> 28.2 us
  starting transfers between devices: 6.41 us -> 10.1 us
  matrix products: 14.8 us -> 16.6 us
    pallas_call x1 -> x0, Pallas kernels: 41.4 us -> none  [scatter(): pl.pallas_call(functools.partial(scatter_kernel, lanes), out_shape=jax.Sh...]
    all_to_all x0 -> x1, waiting for transfers between devices: none -> 25.2 us  [per_device(): received = lax.all_to_all(parts, 'ch', 0, 0, tiled=True)]
    all_to_all x0 -> x1, starting transfers between devices: none -> 3.72 us  [per_device(): received = lax.all_to_all(parts, 'ch', 0, 0, tiled=True)]
    ppermute x2, waiting for transfers between devices: 0.01 us -> 3.01 us  [from_behind(): return lax.ppermute(block, axis, route)]
    reduce_sum x1, other arithmetic: 2.57 us -> 0.29 us  [per_device(): mixed = jnp.sum(received.astype(jnp.float32), axis=0).astype(jnp.bfloat16)]
    unnamed x34 -> x37, local copies, waits for them, and re-layouts: 21 us -> 21.8 us
  transfers between devices with their start and end apart: 2 -> 3, of which waited for: 0 -> 2; matrix products, arithmetic and copies ran while one was open for 5% -> 4% of each run, Pallas kernels for 59% -> 37%
where the time goes in v7:
time: 171 us; the launch traced here: 170 us
  Pallas kernels  76.3 us (45%)
  waiting for transfers between devices  28.2 us (16%)
  local copies, waits for them, and re-layouts  24.5 us (14%)
  matrix products  16.6 us (10%)
  other arithmetic  13 us (8%)
  starting transfers between devices  10.1 us (6%)
    pallas_call x1, Pallas kernels, fetch(): pl.pallas_call(functools.partial(fetch_kernel, count, lanes), out_shape=(...  63.2 us
    all_to_all x1, waiting for transfers between devices, per_device(): received = lax.all_to_all(parts, 'ch', 0, 0, tiled=True)  25.2 us
    unnamed x37, local copies, waits for them, and re-layouts  21.8 us
    pallas_call x1, Pallas kernels, exchange(): pl.pallas_call(functools.partial(exchange_kernel, count), out_shape=(jax....  13.1 us
    dot_general x1, matrix products, per_device(): jnp.einsum('jtc,jrc->tr', g_all, w_all, preferred_element_type=jnp.float32)  6.87 us
    ppermute x2, starting transfers between devices, from_behind(): return lax.ppermute(block, axis, route)  6.4 us
    dot_general x2, matrix products, prefix(): jnp.dot(tri, spread, precision=highest, preferred_element_type=jnp.float32)  6.02 us
    reduce_sum x1, other arithmetic, per_device(): jnp.sum(scaled_grow * (bwd_sums + bwd_entry[None]), axis=1)  4.74 us
  transfers between devices with their start and end apart: 3, of which 2 were waited for; matrix products, arithmetic and copies ran while one was open for 4% of the time, Pallas kernels for 37%

profile of v7, /device:TPU:65, one launch (start us, length us, event | category | flops | bytes accessed | tf_op | source)
XLA Modules:
  0.0 169.8 jit_solution(12719847029281749708)
XLA Ops:
  0.7 0.8 pad_maximum_fusion.3
  1.5 4.1 %collective-permute-start = (bf16[3,2,512]{2,1,0:T(2,128)(2,1)S(1)}, bf16[3,2,512]{2,1,0:T(2,128)(2,1)S(1)}, u32[]{:S(2)}, u32[]{:S(2)}) collective-permute-start(bf16[3,2,512]{2,1,0:T(2,128)(2,1)S(1)} %pad_maximum_fusion.3), channel_id=1, source_target_pairs={{0,16},{16,32},{32,48},{48,64},{64,80},{80,96},{96,112},{112,128},... | collective-permute-start | bytes 18440 | tf_op jit(solution)/shard_map/ppermute | solution.py:134
  7.1 2.6 %multiply_exponential_fusion = f32[128,16,512]{2,1,0:T(8,128)} fusion(f32[128]{0:T(128)S(1)} %iota_convert_fusion, f32[16,512]{1,0:T(8,128)S(1)} %get-tuple-element.30), kind=kLoop, calls=%fused_computation.14 | loop fusion | flops 1048576 | bytes 4227584 | tf_op jit(solution)/shard_map/exp | solution.py:304
  9.7 63.2 %shard_map.120 = (bf16[16,512,512]{2,1,0:T(8,128)(2,1)}, bf16[16,128,512]{2,1,0:T(8,128)(2,1)}) custom-call(bf16[512,512]{1,0:T(8,128)(2,1)} %w_ref.1, bf16[128,512]{1,0:T(8,128)(2,1)} %g_ref.1), custom_call_target="tpu_custom_call" | custom-call | tf_op jit(solution)/shard_map/pallas_call | solution.py:258
  73.4 1.2 copy-done.4
  74.5 6.9 %fusion.22 = (f32[128,512]{1,0:T(8,128)S(1)}, f32[128,512]{1,0:T(8,128)S(1)}, f32[128,512]{1,0:T(8,128)}) fusion(f32[3,128,512]{2,1,0:T(8,128)S(1)} %fusion.19, bf16[16,128,512]{2,1,0:T(8,128)(2,1)S(1)} %copy-done.4, bf16[16,512,512]{2,1,0:T(8,128)(2,1)} %get-tuple-element.8), kind=kOutput, calls=%fused_computation.46 | convolution fusion | flops 1073872896 | bytes 12058624 | tf_op jit(solution)/shard_map/jtc,jrc->tr/dot_general | solution.py:322
  81.9 3.4 %copy.18 = f32[16,8,16,512]{3,1,2,0:T(8,128)S(1)} copy(f32[16,8,16,512]{3,2,1,0:T(8,128)S(1)} %bitcast.81) | data formatting | bytes 8388608
  85.4 3.0 %fusion.8 = f32[128,8192]{1,0:T(8,128)S(1)} fusion(f32[128,8192]{1,0:T(8,128)S(1)} %bitcast.79, f32[128]{0:T(128)S(1)} %iota_convert_fusion, f32[8192]{0:T(1024)S(1)} %bitcast.91), kind=kOutput, calls=%fused_computation.10 | convolution fusion | flops 1612726272 | bytes 8421888 | tf_op jit(solution)/shard_map/dot_general | solution.py:316
  88.4 1.9 %copy-done = f32[128,8192]{1,0:T(8,128)} copy-done((f32[128,8192]{1,0:T(8,128)}, f32[128,8192]{1,0:T(8,128)S(1)}, u32[]{:S(2)}) %copy-start) | copy-done | bytes 4194328
  91.0 3.6 %copy.21 = f32[16,8,16,512]{3,1,2,0:T(8,128)S(1)} copy(f32[16,8,16,512]{3,2,1,0:T(8,128)S(1)} %bitcast.82) | data formatting | bytes 8388608
  94.6 3.0 %fusion.4 = f32[128,8192]{1,0:T(8,128)S(1)} fusion(f32[128,8192]{1,0:T(8,128)S(1)} %bitcast.80, f32[8192]{0:T(1024)S(1)} %bitcast.90, f32[128]{0:T(128)S(1)} %iota_convert_fusion), kind=kOutput, calls=%fused_computation.6 | convolution fusion | flops 1612726272 | bytes 8421888 | tf_op jit(solution)/shard_map/dot_general | solution.py:316
  97.6 1.9 %copy-done.2 = f32[128,8192]{1,0:T(8,128)} copy-done((f32[128,8192]{1,0:T(8,128)}, f32[128,8192]{1,0:T(8,128)S(1)}, u32[]{:S(2)}) %copy-start.2) | copy-done | bytes 4194328
  99.6 0.8 fusion.26
  101.0 13.1 %shard_map.121 = (bf16[16,16,512]{2,1,0:T(8,128)(2,1)}, bf16[16,16,512]{2,1,0:T(8,128)(2,1)}) custom-call(bf16[2,16,512]{2,1,0:T(8,128)(2,1)} %pad_maximum_fusion.2.final_ref), custom_call_target="tpu_custom_call" | custom-call | tf_op jit(solution)/shard_map/pallas_call | solution.py:60
  114.1 5.6 %copy.22 = f32[16,8,16,512]{3,2,1,0:T(8,128)S(1)} copy(f32[16,8,16,512]{3,1,2,0:T(8,128)} %bitcast.78) | data formatting | bytes 8388608
  119.8 3.3 %copy.19 = f32[16,8,16,512]{3,2,1,0:T(8,128)S(1)} copy(f32[16,8,16,512]{3,1,2,0:T(8,128)S(1)} %bitcast.77) | data formatting | bytes 8388608
  123.5 4.7 %fusion.1 = (f32[128,512]{1,0:T(8,128)}, f32[128,512]{1,0:T(8,128)S(1)}) fusion(f32[16,8,16,512]{3,2,1,0:T(8,128)S(1)} %copy.22, f32[16,512]{1,0:T(8,128)S(1)} %get-tuple-element.28, f32[16,512]{1,0:T(8,128)S(1)} %copy-done.5, f32[128]{0:T(128)S(1)} %iota_convert_fusion, f32[16,512]{1,0:T(8,128)S(1)} %get-tuple-element.29, ...), kind=kLoop, calls=%fused_computation.2 | loop fusion | flops 10354688 | bytes 9077248 | tf_op jit(solution)/shard_map/reduce_sum | solution.py:352
  128.3 3.7 %convert_bitcast_fusion = bf16[16,128,512]{1,2,0:T(8,128)(2,1)} fusion(bf16[16,512,512]{2,1,0:T(8,128)(2,1)S(1)} %bitcast.76, f32[3,128,512]{2,1,0:T(8,128)S(1)} %fusion.19, f32[128,512]{1,0:T(8,128)S(1)} %get-tuple-element.17, f32[128,512]{1,0:T(8,128)S(1)} %get-tuple-element.22, f32[512]{0:T(512)S(1)} %copy-done.12), kind=kOutput, calls=%fused_computation.15 | convolution fusion | flops 1075052544 | bytes 11274240 | tf_op jit(solution)/shard_map/tr,jrc->jtc/dot_general | solution.py:345
  132.0 3.7 %all-to-all-start = ((bf16[16,128,512]{1,2,0:T(8,128)(2,1)}), bf16[16,128,512]{1,2,0:T(8,128)(2,1)S(1)}, u32[]{:S(2)}, u32[]{:S(2)}) async-start(bf16[16,128,512]{1,2,0:T(8,128)(2,1)} %convert_bitcast_fusion), calls=%async_computation | async-start | bytes 4194304 | tf_op jit(solution)/shard_map/all_to_all | solution.py:347
  135.7 1.3 multiply_bitcast_fusion.1
  137.1 2.3 %collective-permute-start.1 = (f32[3,2,512]{2,1,0:T(2,128)S(1)}, f32[3,2,512]{2,1,0:T(2,128)S(1)}, u32[]{:S(2)}, u32[]{:S(2)}) collective-permute-start(f32[3,2,512]{2,1,0:T(2,128)S(1)} %slice.94), channel_id=1, source_target_pairs={{16,0},{32,16},{48,32},{64,48},{80,64},{96,80},{112,96},{128,112},... | collective-permute-start | bytes 36872 | tf_op jit(solution)/shard_map/ppermute | solution.py:134
  139.4 3.0 %collective-permute-done.1 = f32[3,2,512]{2,1,0:T(2,128)S(1)} collective-permute-done((f32[3,2,512]{2,1,0:T(2,128)S(1)}, f32[3,2,512]{2,1,0:T(2,128)S(1)}, u32[]{:S(2)}, u32[]{:S(2)}) %collective-permute-start.1) | collective-permute-done | bytes 12320 | tf_op jit(solution)/shard_map/ppermute | solution.py:134
  143.5 25.2 %all-to-all-done = bf16[16,128,512]{1,2,0:T(8,128)(2,1)S(1)} async-done(((bf16[16,128,512]{1,2,0:T(8,128)(2,1)}), bf16[16,128,512]{1,2,0:T(8,128)(2,1)S(1)}, u32[]{:S(2)}, u32[]{:S(2)}) %all-to-all-start) | async-done | bytes 2097184 | tf_op jit(solution)/shard_map/all_to_all | solution.py:347
  169.0 0.8 copy.15
  (53 shorter events, 5.7 us)
Async XLA Ops:
  0.6 72.3 %copy-start.8 = (bf16[128,512]{1,0:T(8,128)(2,1)S(1)}, bf16[128,512]{1,0:T(8,128)(2,1)}, u32[]{:S(2)}) copy-start(bf16[128,512]{1,0:T(8,128)(2,1)} %param.9) | copy-start | bytes 393220
  0.6 72.3 %copy-start.7 = (bf16[128,512]{1,0:T(8,128)(2,1)S(1)}, bf16[128,512]{1,0:T(8,128)(2,1)}, u32[]{:S(2)}) copy-start(bf16[128,512]{1,0:T(8,128)(2,1)} %param.10) | copy-start | bytes 393220
  0.7 72.3 %copy-start.6 = (bf16[128,512]{1,0:T(8,128)(2,1)S(1)}, bf16[128,512]{1,0:T(8,128)(2,1)}, u32[]{:S(2)}) copy-start(bf16[128,512]{1,0:T(8,128)(2,1)} %param.11) | copy-start | bytes 393220
  0.7 9.0 %copy-start.5 = (f32[16,512]{1,0:T(8,128)S(1)}, f32[16,512]{1,0:T(8,128)}, u32[]{:S(2)}) copy-start(f32[16,512]{1,0:T(8,128)} %param.13) | copy-start | bytes 98308
  1.5 71.5 %collective-permute-start = (bf16[3,2,512]{2,1,0:T(2,128)(2,1)S(1)}, bf16[3,2,512]{2,1,0:T(2,128)(2,1)S(1)}, u32[]{:S(2)}, u32[]{:S(2)}) collective-permute-start(bf16[3,2,512]{2,1,0:T(2,128)(2,1)S(1)} %pad_maximum_fusion.3), channel_id=1, source_target_pairs={{0,16},{16,32},{32,48},{48,64},{64,80},{80,96},{96,112},{112,128},... | collective-permute-start | bytes 18440 | tf_op jit(solution)/shard_map/ppermute | solution.py:134
  72.9 1.6 copy-start.4
  81.4 9.0 %copy-start.3 = (f32[128,512]{1,0:T(8,128)}, f32[128,512]{1,0:T(8,128)S(1)}, u32[]{:S(2)}) copy-start(f32[128,512]{1,0:T(8,128)S(1)} %get-tuple-element.23) | copy-start | bytes 786436
  88.4 1.9 %copy-start = (f32[128,8192]{1,0:T(8,128)}, f32[128,8192]{1,0:T(8,128)S(1)}, u32[]{:S(2)}) copy-start(f32[128,8192]{1,0:T(8,128)S(1)} %fusion.8) | copy-start | bytes 12582916
  97.6 1.9 %copy-start.2 = (f32[128,8192]{1,0:T(8,128)}, f32[128,8192]{1,0:T(8,128)S(1)}, u32[]{:S(2)}) copy-start(f32[128,8192]{1,0:T(8,128)S(1)} %fusion.4) | copy-start | bytes 12582916
  114.1 5.6 %copy-start.1 = (f32[128,8192]{1,0:T(8,128)S(1)}, f32[128,8192]{1,0:T(8,128)}, u32[]{:S(2)}) copy-start(f32[128,8192]{1,0:T(8,128)} %copy-done) | copy-start | bytes 12582916
  119.7 3.3 %copy-start.9 = (bf16[16,16,512]{2,1,0:T(8,128)(2,1)S(1)}, bf16[16,16,512]{2,1,0:T(8,128)(2,1)}, u32[]{:S(2)}) copy-start(bf16[16,16,512]{2,1,0:T(8,128)(2,1)} %get-tuple-element.10) | copy-start | bytes 786436
  119.8 3.3 %copy-start.10 = (bf16[16,16,512]{2,1,0:T(8,128)(2,1)S(1)}, bf16[16,16,512]{2,1,0:T(8,128)(2,1)}, u32[]{:S(2)}) copy-start(bf16[16,16,512]{2,1,0:T(8,128)(2,1)} %get-tuple-element.11) | copy-start | bytes 786436
  119.8 3.7 %copy-start.11 = (f32[16,512]{1,0:T(8,128)S(1)}, f32[16,512]{1,0:T(8,128)}, u32[]{:S(2)}) copy-start(f32[16,512]{1,0:T(8,128)} %param.14) | copy-start | bytes 98308
  119.8 8.5 %slice-start = ((s8[8388608]{0:T(1024)(128)(4,1)}), s8[4194304]{0:T(1024)(128)(4,1)S(1)}, s32[]{:S(2)}) async-start(s8[8388608]{0:T(1024)(128)(4,1)} %bitcast.75), calls=%async_computation.1 | async-start | bytes 8388608
  123.5 4.8 %slice-start.1 = ((s8[8388608]{0:T(1024)(128)(4,1)}), s8[4194304]{0:T(1024)(128)(4,1)S(1)}, s32[]{:S(2)}) async-start(s8[8388608]{0:T(1024)(128)(4,1)} %bitcast.75), calls=%async_computation.2 | async-start | bytes 8388608
  123.5 4.8 %copy-start.12 = (f32[512]{0:T(512)S(1)}, f32[512]{0:T(512)}, u32[]{:S(2)}) copy-start(f32[512]{0:T(512)} %param.15) | copy-start | bytes 6148
  132.0 36.7 %all-to-all-start = ((bf16[16,128,512]{1,2,0:T(8,128)(2,1)}), bf16[16,128,512]{1,2,0:T(8,128)(2,1)S(1)}, u32[]{:S(2)}, u32[]{:S(2)}) async-start(bf16[16,128,512]{1,2,0:T(8,128)(2,1)} %convert_bitcast_fusion), calls=%async_computation | async-start | bytes 4194304 | tf_op jit(solution)/shard_map/all_to_all | solution.py:347
  137.1 5.3 %collective-permute-start.1 = (f32[3,2,512]{2,1,0:T(2,128)S(1)}, f32[3,2,512]{2,1,0:T(2,128)S(1)}, u32[]{:S(2)}, u32[]{:S(2)}) collective-permute-start(f32[3,2,512]{2,1,0:T(2,128)S(1)} %slice.94), channel_id=1, source_target_pairs={{16,0},{32,16},{48,32},{64,48},{80,64},{96,80},{112,96},{128,112},... | collective-permute-start | bytes 36872 | tf_op jit(solution)/shard_map/ppermute | solution.py:134

commit v8 on v5

--- a/solution.py
+++ b/solution.py
@@ -10,7 +10,7 @@
 MESH = pl.DeviceIdType.MESH
 
 
-def exchange_kernel(count, final_ref, out_ref, slots, send_sems, recv_sems):
+def exchange_kernel(count, later, final_ref, got_ref, send_sems, recv_sems):
     me = lax.axis_index("seq")
     lane = lax.axis_index("ch")
     barrier = pltpu.get_barrier_semaphore()
@@ -25,43 +25,48 @@
     def link(peer, slot):
         return pltpu.make_async_remote_copy(
             src_ref=final_ref,
-            dst_ref=slots.at[slot],
+            dst_ref=got_ref.at[slot],
             send_sem=send_sems.at[peer],
             recv_sem=recv_sems.at[slot],
             device_id=(peer, lane),
             device_id_type=MESH,
         )
 
+    def sends_to(peer):
+        return me < peer if later else me > peer
+
+    def hears_from(peer):
+        return me > peer if later else me < peer
+
     for peer in range(count):
 
-        @pl.when(me != peer)
+        @pl.when(sends_to(peer))
         def _():
             link(peer, me).start()
 
-    slots[me] = final_ref[...]
     for peer in range(count):
 
-        @pl.when(me != peer)
+        @pl.when(sends_to(peer))
         def _():
             link(peer, me).wait_send()
+
+        @pl.when(hears_from(peer))
+        def _():
             link(peer, peer).wait_recv()
 
-    out_ref[...] = slots[...]
-
-
-def exchange(final, count):
+
+def exchange(final, count, later, collective):
     shape = (count,) + final.shape
     return pl.pallas_call(
-        functools.partial(exchange_kernel, count),
+        functools.partial(exchange_kernel, count, later),
         out_shape=jax.ShapeDtypeStruct(shape, final.dtype),
         in_specs=[pl.BlockSpec(memory_space=pltpu.VMEM)],
         out_specs=pl.BlockSpec(memory_space=pltpu.VMEM),
         scratch_shapes=[
-            pltpu.VMEM(shape, final.dtype),
             pltpu.SemaphoreType.DMA((count,)),
             pltpu.SemaphoreType.DMA((count,)),
         ],
-        compiler_params=pltpu.CompilerParams(collective_id=0, has_side_effects=True),
+        compiler_params=pltpu.CompilerParams(collective_id=collective, has_side_effects=True),
     )(final)
 
 
@@ -253,35 +258,32 @@
         summed = jnp.dot(tri, spread, precision=highest, preferred_element_type=jnp.float32)
         return summed.reshape(tok_rows, mode_count, chan_width)
 
+    source = jnp.arange(count)
+
+    def entry(gap, got):
+        span = (tok_rows * jnp.maximum(gap, 0)).astype(jnp.float32)[:, None, None]
+        held = jnp.where((gap >= 0)[:, None, None], got.astype(jnp.float32), 0.0)
+        return jnp.sum(jnp.exp(-decay_rate[None] * span) * held, axis=0)
+
     fwd_sums = prefix(lower, grow, gated)
-    fwd_final = shrink[tok_rows - 1] * fwd_sums[tok_rows - 1]
-
-    grad_mixer = jnp.einsum("jtc,jrc->tr", g_all, w_all, preferred_element_type=jnp.float32)
-    grad_long = grad_mixer * q_short
-    bwd_sums = prefix(upper, shrink, grad_long)
-    bwd_final = bwd_sums[0]
-
-    finals = jnp.stack([fwd_final, bwd_final])
-    gathered = exchange(finals, count)
-    source = jnp.arange(count)
-    fwd_gap = place - 1 - source
-    bwd_gap = source - place - 1
-
-    def weights(gap):
-        span = (tok_rows * jnp.maximum(gap, 0)).astype(jnp.float32)[:, None, None]
-        return jnp.where((gap >= 0)[:, None, None], jnp.exp(-decay_rate[None] * span), 0.0)
-
-    fwd_entry = jnp.sum(weights(fwd_gap) * gathered[:, 0], axis=0) * one_step
-    bwd_entry = jnp.sum(weights(bwd_gap) * gathered[:, 1], axis=0) * block_decay
-
+    fwd_final = (shrink[tok_rows - 1] * fwd_sums[tok_rows - 1]).astype(jnp.bfloat16)
+    fwd_got = exchange(fwd_final, count, True, 0)
+    fwd_entry = entry(place - 1 - source, fwd_got) * one_step
     long_out = (
         jnp.sum(scaled_shrink * (fwd_sums + fwd_entry[None]), axis=1) + skip_gain[None, :] * gated
     )
     mixer = (q_short * long_out).astype(jnp.bfloat16)
     parts = jnp.einsum("tr,jrc->jtc", mixer, w_all, preferred_element_type=jnp.float32)
     parts = parts.astype(jnp.bfloat16)
+    parts, g_all, w_all = lax.optimization_barrier((parts, g_all, w_all))
     received = lax.all_to_all(parts, "ch", 0, 0, tiled=True)
     mixed = jnp.sum(received.astype(jnp.float32), axis=0).astype(jnp.bfloat16)
+
+    grad_mixer = jnp.einsum("jtc,jrc->tr", g_all, w_all, preferred_element_type=jnp.float32)
+    grad_long = grad_mixer * q_short
+    bwd_sums = prefix(upper, shrink, grad_long)
+    bwd_got = exchange(bwd_sums[0].astype(jnp.bfloat16), count, False, 3)
+    bwd_entry = entry(source - place - 1, bwd_got) * block_decay
 
     grad_qshort = grad_mixer * long_out
     grad_gated = (

time: 186 us -> 162 us (0.87); the launches traced: 186 us -> 160 us
  waiting for transfers between devices: 29.8 us -> 2.72 us
  Pallas kernels: 93.4 us -> 87.1 us
  local copies, waits for them, and re-layouts: 22.3 us -> 25.8 us
    all_to_all x1, waiting for transfers between devices: 26.4 us -> 0.01 us  [per_device(): received = lax.all_to_all(parts, 'ch', 0, 0, tiled=True)]
    pallas_call x1 -> x2, Pallas kernels: 30.2 us -> 23.9 us  [exchange(): pl.pallas_call(functools.partial(exchange_kernel, count, later), out_shap...]
    dot_general x1, matrix products: 6.87 us -> 2.75 us  [per_device(): jnp.einsum('jtc,jrc->tr', g_all, w_all, preferred_element_type=jnp.float32)]
    dot_general x1, matrix products: 3.72 us -> 7.28 us  [per_device(): jnp.einsum('tr,jrc->jtc', mixer, w_all, preferred_element_type=jnp.float32)]
    unnamed x35 -> x43, local copies, waits for them, and re-layouts: 19.5 us -> 22.5 us
    reduce_sum x1 -> x3, other arithmetic: 0.29 us -> 2.77 us  [the longest x1 1.43 us: per_device(): jnp.sum(scaled_shrink * (fwd_sums + fwd_entry[None]), axis=1)]
    dot_general x2, matrix products: 6.34 us -> 8.3 us  [prefix(): jnp.dot(tri, spread, precision=highest, preferred_element_type=jnp.float32)]
    convert_element_type x1 -> x3, other arithmetic: 0.01 us -> 1.9 us  [the longest x1 1.37 us: per_device(): (shrink[tok_rows - 1] * fwd_sums[tok_rows - 1]).astype(jnp.bfloat16)]
  transfers between devices with their start and end apart: 3 -> 3, of which waited for: 2 -> 1; matrix products, arithmetic and copies ran while one was open for 4% -> 14% of each run, Pallas kernels for 34% -> 49%
where the time goes in v8:
time: 162 us; the launch traced here: 160 us
  Pallas kernels  87.1 us (54%)
  local copies, waits for them, and re-layouts  25.8 us (16%)
  matrix products  18.3 us (11%)
  other arithmetic  14.3 us (9%)
  starting transfers between devices  10.1 us (6%)
  waiting for transfers between devices  2.72 us (2%)
    pallas_call x1, Pallas kernels, fetch(): pl.pallas_call(functools.partial(fetch_kernel, count, lanes), out_shape=(...  63.2 us
    pallas_call x2, Pallas kernels, exchange(): pl.pallas_call(functools.partial(exchange_kernel, count, later), out_shap...  23.9 us
    unnamed x43, local copies, waits for them, and re-layouts  22.5 us
    dot_general x2, matrix products, prefix(): jnp.dot(tri, spread, precision=highest, preferred_element_type=jnp.float32)  8.3 us
    dot_general x1, matrix products, per_device(): jnp.einsum('tr,jrc->jtc', mixer, w_all, preferred_element_type=jnp.float32)  7.28 us
    ppermute x2, starting transfers between devices, from_behind(): return lax.ppermute(block, axis, route)  6.4 us
    all_to_all x1, starting transfers between devices, per_device(): received = lax.all_to_all(parts, 'ch', 0, 0, tiled=True)  3.73 us
    reduce_sum x1, other arithmetic, per_device(): jnp.sum(scaled_grow * (bwd_sums + bwd_entry[None]), axis=1)  3.66 us
  transfers between devices with their start and end apart: 3, of which 1 were waited for; matrix products, arithmetic and copies ran while one was open for 14% of the time, Pallas kernels for 49%

profile of v8, /device:TPU:65, one launch (start us, length us, event | category | flops | bytes accessed | tf_op | source)
XLA Modules:
  0.0 159.6 jit_solution(17267471688357200626)
XLA Ops:
  0.7 0.8 pad_maximum_fusion.2
  1.5 4.1 %collective-permute-start = (bf16[3,2,512]{2,1,0:T(2,128)(2,1)S(1)}, bf16[3,2,512]{2,1,0:T(2,128)(2,1)S(1)}, u32[]{:S(2)}, u32[]{:S(2)}) collective-permute-start(bf16[3,2,512]{2,1,0:T(2,128)(2,1)S(1)} %pad_maximum_fusion.2), channel_id=1, source_target_pairs={{0,16},{16,32},{32,48},{48,64},{64,80},{80,96},{96,112},{112,128},... | collective-permute-start | bytes 18440 | tf_op jit(solution)/shard_map/ppermute | solution.py:76
  7.0 0.8 neg.12
  7.7 2.6 %multiply_exponential_fusion = f32[128,16,512]{2,1,0:T(8,128)} fusion(f32[128]{0:T(128)S(1)} %iota_convert_fusion, f32[16,512]{1,0:T(8,128)S(1)} %neg.12), kind=kLoop, calls=%fused_computation.14 | loop fusion | flops 1048576 | bytes 4227584 | tf_op jit(solution)/shard_map/exp | solution.py:246
  10.8 63.2 %shard_map.120 = (bf16[16,512,512]{2,1,0:T(8,128)(2,1)}, bf16[16,128,512]{2,1,0:T(8,128)(2,1)}) custom-call(bf16[512,512]{1,0:T(8,128)(2,1)} %w_ref.1, bf16[128,512]{1,0:T(8,128)(2,1)} %g_ref.1), custom_call_target="tpu_custom_call" | custom-call | tf_op jit(solution)/shard_map/pallas_call | solution.py:200
  75.1 3.4 %copy.18 = f32[16,8,16,512]{3,1,2,0:T(8,128)S(1)} copy(f32[16,8,16,512]{3,2,1,0:T(8,128)S(1)} %bitcast.89) | data formatting | bytes 8388608
  78.5 3.1 %fusion.8 = f32[128,8192]{1,0:T(8,128)S(1)} fusion(f32[128,8192]{1,0:T(8,128)S(1)} %bitcast.88, f32[128]{0:T(128)S(1)} %iota_convert_fusion, f32[8192]{0:T(1024)S(1)} %bitcast.98), kind=kOutput, calls=%fused_computation.10 | convolution fusion | flops 1612726272 | bytes 8421888 | tf_op jit(solution)/shard_map/dot_general | solution.py:258
  81.6 1.9 %copy-done = f32[128,8192]{1,0:T(8,128)} copy-done((f32[128,8192]{1,0:T(8,128)}, f32[128,8192]{1,0:T(8,128)S(1)}, u32[]{:S(2)}) %copy-start) | copy-done | bytes 4194328
  83.7 1.4 fusion.27.final_ref
  85.0 8.9 %shard_map.121 = bf16[16,16,512]{2,1,0:T(8,128)(2,1)} custom-call(bf16[16,512]{1,0:T(8,128)(2,1)} %fusion.27.final_ref), custom_call_target="tpu_custom_call" | custom-call | tf_op jit(solution)/shard_map/pallas_call | solution.py:60
  94.0 5.5 %copy.19 = f32[16,8,16,512]{3,2,1,0:T(8,128)S(1)} copy(f32[16,8,16,512]{3,1,2,0:T(8,128)} %bitcast.85) | data formatting | bytes 8388608
  99.8 1.4 fusion.3
  101.2 7.3 %convert_bitcast_fusion = bf16[16,128,512]{1,2,0:T(8,128)(2,1)} fusion(bf16[16,512,512]{2,1,0:T(8,128)(2,1)} %get-tuple-element.13, f32[3,128,512]{2,1,0:T(8,128)S(1)} %fusion.19, f32[128,512]{1,0:T(8,128)S(1)} %fusion.3, f32[128,512]{1,0:T(8,128)S(1)} %fusion.22, f32[512]{0:T(512)S(1)} %copy-done.10), kind=kOutput, calls=%fused_computation.16 | convolution fusion | flops 1075052544 | bytes 11274240 | tf_op jit(solution)/shard_map/tr,jrc->jtc/dot_general | solution.py:276
  108.5 2.8 %multiply_bitcast_fusion.2 = (f32[1,128,512]{2,1,0:T(8,128)S(1)}, f32[128,512]{1,0:T(8,128)S(1)}) fusion(f32[128,512]{1,0:T(8,128)S(1)} %fusion.3, f32[128,512]{1,0:T(8,128)S(1)} %fusion.22, f32[512]{0:T(512)S(1)} %copy-done.10, f32[3,128,512]{2,1,0:T(8,128)S(1)} %fusion.19, bf16[16,128,512]{2,1,0:T(8,128)(2,1)S(1)} %copy-done.1, ...), kind=kOutput, calls=%fused_computation.42 | convolution fusion | flops 1074003968 | bytes 11798528 | tf_op jit(solution)/shard_map/jtc,jrc->tr/dot_general | solution.py:282
  111.8 5.6 %copy.21 = f32[16,8,16,512]{3,1,2,0:T(8,128)} copy(f32[16,8,16,512]{3,2,1,0:T(8,128)S(1)} %bitcast.90) | data formatting | bytes 8388608
  117.4 3.7 %all-to-all-start = ((bf16[16,128,512]{1,2,0:T(8,128)(2,1)}), bf16[16,128,512]{1,2,0:T(8,128)(2,1)S(1)}, u32[]{:S(2)}, u32[]{:S(2)}) async-start(bf16[16,128,512]{1,2,0:T(8,128)(2,1)} %convert_bitcast_fusion), calls=%async_computation | async-start | bytes 4194304 | tf_op jit(solution)/shard_map/all_to_all | solution.py:279
  121.2 5.2 %fusion.4 = f32[128,8192]{1,0:T(8,128)S(1)} fusion(f32[128,8192]{1,0:T(8,128)} %bitcast.87, f32[8192]{0:T(1024)S(1)} %bitcast.99, f32[128]{0:T(128)} %copy-done.12), kind=kOutput, calls=%fused_computation.6 | convolution fusion | flops 1612726272 | bytes 8421888 | tf_op jit(solution)/shard_map/dot_general | solution.py:258
  126.4 5.2 %copy.22 = f32[16,8,16,512]{3,2,1,0:T(8,128)} copy(f32[16,8,16,512]{3,1,2,0:T(8,128)S(1)} %bitcast.86) | data formatting | bytes 8388608
  132.3 15.0 %shard_map.122 = bf16[16,16,512]{2,1,0:T(8,128)(2,1)} custom-call(bf16[16,512]{1,0:T(8,128)(2,1)} %convert_element_type.67.final_ref), custom_call_target="tpu_custom_call" | custom-call | tf_op jit(solution)/shard_map/pallas_call | solution.py:60
  147.3 1.1 multiply_reduce_fusion
  148.5 3.7 %fusion.1 = f32[128,512]{1,0:T(8,128)S(1)} fusion(f32[16,8,16,512]{3,2,1,0:T(8,128)} %copy.22, f32[16,512]{1,0:T(8,128)S(1)} %exponential_multiply_fusion, f32[16,512]{1,0:T(8,128)S(1)} %copy-done.3, f32[128]{0:T(128)S(1)} %copy-done.13, f32[16,512]{1,0:T(8,128)S(1)} %get-tuple-element.27), kind=kLoop, calls=%fused_computation.2 | loop fusion | flops 5177344 | bytes 4555264 | tf_op jit(solution)/shard_map/reduce_sum | solution.py:290
  152.4 2.3 %collective-permute-start.1 = (f32[3,2,512]{2,1,0:T(2,128)S(1)}, f32[3,2,512]{2,1,0:T(2,128)S(1)}, u32[]{:S(2)}, u32[]{:S(2)}) collective-permute-start(f32[3,2,512]{2,1,0:T(2,128)S(1)} %slice.91), channel_id=1, source_target_pairs={{16,0},{32,16},{48,32},{64,48},{80,64},{96,80},{112,96},{128,112},... | collective-permute-start | bytes 36872 | tf_op jit(solution)/shard_map/ppermute | solution.py:76
  154.7 2.7 %collective-permute-done.1 = f32[3,2,512]{2,1,0:T(2,128)S(1)} collective-permute-done((f32[3,2,512]{2,1,0:T(2,128)S(1)}, f32[3,2,512]{2,1,0:T(2,128)S(1)}, u32[]{:S(2)}, u32[]{:S(2)}) %collective-permute-start.1) | collective-permute-done | bytes 12320 | tf_op jit(solution)/shard_map/ppermute | solution.py:76
  158.8 0.8 copy.15
  (65 shorter events, 6.0 us)
Async XLA Ops:
  0.6 73.4 %copy-start.6 = (bf16[128,512]{1,0:T(8,128)(2,1)S(1)}, bf16[128,512]{1,0:T(8,128)(2,1)}, u32[]{:S(2)}) copy-start(bf16[128,512]{1,0:T(8,128)(2,1)} %param.9) | copy-start | bytes 393220
  0.6 73.4 %copy-start.5 = (bf16[128,512]{1,0:T(8,128)(2,1)S(1)}, bf16[128,512]{1,0:T(8,128)(2,1)}, u32[]{:S(2)}) copy-start(bf16[128,512]{1,0:T(8,128)(2,1)} %param.10) | copy-start | bytes 393220
  0.7 73.4 %copy-start.4 = (bf16[128,512]{1,0:T(8,128)(2,1)S(1)}, bf16[128,512]{1,0:T(8,128)(2,1)}, u32[]{:S(2)}) copy-start(bf16[128,512]{1,0:T(8,128)(2,1)} %param.11) | copy-start | bytes 393220
  0.7 10.2 %copy-start.3 = (f32[16,512]{1,0:T(8,128)S(1)}, f32[16,512]{1,0:T(8,128)}, u32[]{:S(2)}) copy-start(f32[16,512]{1,0:T(8,128)} %param.13) | copy-start | bytes 98308
  1.5 72.6 %collective-permute-start = (bf16[3,2,512]{2,1,0:T(2,128)(2,1)S(1)}, bf16[3,2,512]{2,1,0:T(2,128)(2,1)S(1)}, u32[]{:S(2)}, u32[]{:S(2)}) collective-permute-start(bf16[3,2,512]{2,1,0:T(2,128)(2,1)S(1)} %pad_maximum_fusion.2), channel_id=1, source_target_pairs={{0,16},{16,32},{32,48},{48,64},{64,80},{80,96},{96,112},{112,128},... | collective-permute-start | bytes 18440 | tf_op jit(solution)/shard_map/ppermute | solution.py:76
  5.6 94.2 %copy-start.12 = (f32[128]{0:T(128)}, f32[128]{0:T(128)S(1)}, u32[]{:S(2)}) copy-start(f32[128]{0:T(128)S(1)} %iota_convert_fusion) | copy-start | bytes 1540
  7.0 67.5 %copy-start.7 = (f32[3,512]{1,0:T(4,128)}, f32[3,512]{1,0:T(4,128)S(1)}, u32[]{:S(2)}) copy-start(f32[3,512]{1,0:T(4,128)S(1)} %get-tuple-element.30) | copy-start | bytes 18436
  81.6 1.9 %copy-start = (f32[128,8192]{1,0:T(8,128)}, f32[128,8192]{1,0:T(8,128)S(1)}, u32[]{:S(2)}) copy-start(f32[128,8192]{1,0:T(8,128)S(1)} %fusion.8) | copy-start | bytes 12582916
  94.0 5.5 %copy-start.2 = (bf16[16,16,512]{2,1,0:T(8,128)(2,1)S(1)}, bf16[16,16,512]{2,1,0:T(8,128)(2,1)}, u32[]{:S(2)}) copy-start(bf16[16,16,512]{2,1,0:T(8,128)(2,1)} %shard_map.121) | copy-start | bytes 786436
  94.0 5.7 %copy-start.9 = (f32[16,512]{1,0:T(8,128)S(1)}, f32[16,512]{1,0:T(8,128)}, u32[]{:S(2)}) copy-start(f32[16,512]{1,0:T(8,128)} %param.14) | copy-start | bytes 98308
  99.5 1.7 %copy-start.10 = (f32[512]{0:T(512)S(1)}, f32[512]{0:T(512)}, u32[]{:S(2)}) copy-start(f32[512]{0:T(512)} %param.15) | copy-start | bytes 6148
  99.8 8.8 %slice-start = ((s8[8388608]{0:T(1024)(128)(4,1)}), s8[4194304]{0:T(1024)(128)(4,1)S(1)}, s32[]{:S(2)}) async-start(s8[8388608]{0:T(1024)(128)(4,1)} %bitcast.83), calls=%async_computation.1 | async-start | bytes 8388608
  101.2 7.3 %slice-start.1 = ((s8[8388608]{0:T(1024)(128)(4,1)}), s8[4194304]{0:T(1024)(128)(4,1)S(1)}, s32[]{:S(2)}) async-start(s8[8388608]{0:T(1024)(128)(4,1)} %bitcast.83), calls=%async_computation.2 | async-start | bytes 8388608
  101.2 7.3 %copy-start.1 = (bf16[16,128,512]{2,1,0:T(8,128)(2,1)S(1)}, bf16[16,128,512]{2,1,0:T(8,128)(2,1)}, u32[]{:S(2)}) copy-start(bf16[16,128,512]{2,1,0:T(8,128)(2,1)} %get-tuple-element.12) | copy-start | bytes 6291460
  117.4 41.1 %all-to-all-start = ((bf16[16,128,512]{1,2,0:T(8,128)(2,1)}), bf16[16,128,512]{1,2,0:T(8,128)(2,1)S(1)}, u32[]{:S(2)}, u32[]{:S(2)}) async-start(bf16[16,128,512]{1,2,0:T(8,128)(2,1)} %convert_bitcast_fusion), calls=%async_computation | async-start | bytes 4194304 | tf_op jit(solution)/shard_map/all_to_all | solution.py:279
  126.4 21.0 %copy-start.14 = (pred[16]{0:T(512)(128)(4,1)S(1)}, pred[16]{0:T(512)(128)(4,1)}, u32[]{:S(2)}) copy-start(pred[16]{0:T(512)(128)(4,1)} %fusion.29) | copy-start | bytes 52
  126.4 21.0 %copy-start.15 = (f32[16]{0:T(128)S(1)}, f32[16]{0:T(128)}, u32[]{:S(2)}) copy-start(f32[16]{0:T(128)} %multiply_convert_fusion.1) | copy-start | bytes 196
  126.4 22.1 %copy-start.13 = (f32[128]{0:T(128)S(1)}, f32[128]{0:T(128)}, u32[]{:S(2)}) copy-start(f32[128]{0:T(128)} %copy-done.12) | copy-start | bytes 1540
  131.6 20.6 %copy-start.11 = (f32[512]{0:T(512)S(1)}, f32[512]{0:T(512)}, u32[]{:S(2)}) copy-start(f32[512]{0:T(512)} %param.15) | copy-start | bytes 6148
  148.5 9.0 %copy-start.8 = (f32[3,512]{1,0:T(4,128)S(1)}, f32[3,512]{1,0:T(4,128)}, u32[]{:S(2)}) copy-start(f32[3,512]{1,0:T(4,128)} %copy-done.7) | copy-start | bytes 18436
  152.4 5.0 %collective-permute-start.1 = (f32[3,2,512]{2,1,0:T(2,128)S(1)}, f32[3,2,512]{2,1,0:T(2,128)S(1)}, u32[]{:S(2)}, u32[]{:S(2)}) collective-permute-start(f32[3,2,512]{2,1,0:T(2,128)S(1)} %slice.91), channel_id=1, source_target_pairs={{16,0},{32,16},{48,32},{64,48},{80,64},{96,80},{112,96},{128,112},... | collective-permute-start | bytes 36872 | tf_op jit(solution)/shard_map/ppermute | solution.py:76

commit v9 on v8

--- a/solution.py
+++ b/solution.py
@@ -241,37 +241,43 @@
     v_short = featured[2]
     gated = k_short * v_short
 
-    mode_scale = residue * jnp.sqrt(-jnp.expm1(-2.0 * decay_rate))
-    offsets = jnp.arange(tok_rows).astype(jnp.float32)
-    shrink = jnp.exp(-decay_rate[None, :, :] * offsets[:, None, None])
-    grow = jnp.exp(decay_rate[None, :, :] * offsets[:, None, None])
-    scaled_shrink = mode_scale[None] * shrink
-    scaled_grow = mode_scale[None] * grow
-    one_step = jnp.exp(-decay_rate)
-    block_decay = jnp.exp(-decay_rate * tok_rows)
+    width = mode_count * chan_width
+    rate = decay_rate.reshape(1, width)
+    mode_scale = (residue * jnp.sqrt(-jnp.expm1(-2.0 * decay_rate))).reshape(1, width)
+    offsets = jnp.arange(tok_rows).astype(jnp.float32)[:, None]
+    shrink = jnp.exp(-rate * offsets)
+    grow = jnp.exp(rate * offsets)
+    scaled_shrink = mode_scale * shrink
+    scaled_grow = mode_scale * grow
+    one_step = jnp.exp(-rate)
+    block_decay = jnp.exp(-rate * tok_rows)
     rows = jnp.arange(tok_rows)
     lower = (rows[:, None] >= rows[None, :]).astype(jnp.float32)
     upper = (rows[:, None] <= rows[None, :]).astype(jnp.float32)
 
     def prefix(tri, weights, signal):
-        spread = (weights * signal[:, None, :]).reshape(tok_rows, mode_count * chan_width)
-        summed = jnp.dot(tri, spread, precision=highest, preferred_element_type=jnp.float32)
-        return summed.reshape(tok_rows, mode_count, chan_width)
+        spread = weights * jnp.concatenate([signal] * mode_count, axis=1)
+        return jnp.dot(tri, spread, precision=highest, preferred_element_type=jnp.float32)
+
+    def over_modes(table):
+        total = table[:, :chan_width]
+        for mode in range(1, mode_count):
+            total = total + table[:, mode * chan_width : (mode + 1) * chan_width]
+        return total
 
     source = jnp.arange(count)
 
     def entry(gap, got):
-        span = (tok_rows * jnp.maximum(gap, 0)).astype(jnp.float32)[:, None, None]
-        held = jnp.where((gap >= 0)[:, None, None], got.astype(jnp.float32), 0.0)
-        return jnp.sum(jnp.exp(-decay_rate[None] * span) * held, axis=0)
+        span = (tok_rows * jnp.maximum(gap, 0)).astype(jnp.float32)[:, None]
+        held = jnp.where((gap >= 0)[:, None], got.astype(jnp.float32), 0.0)
+        return jnp.sum(jnp.exp(-rate * span) * held, axis=0, keepdims=True)
 
     fwd_sums = prefix(lower, grow, gated)
     fwd_final = (shrink[tok_rows - 1] * fwd_sums[tok_rows - 1]).astype(jnp.bfloat16)
-    fwd_got = exchange(fwd_final, count, True, 0)
+    fwd_got = exchange(fwd_final.reshape(mode_count, chan_width), count, True, 0)
+    fwd_got = fwd_got.reshape(count, width)
     fwd_entry = entry(place - 1 - source, fwd_got) * one_step
-    long_out = (
-        jnp.sum(scaled_shrink * (fwd_sums + fwd_entry[None]), axis=1) + skip_gain[None, :] * gated
-    )
+    long_out = over_modes(scaled_shrink * (fwd_sums + fwd_entry)) + skip_gain[None, :] * gated
     mixer = (q_short * long_out).astype(jnp.bfloat16)
     parts = jnp.einsum("tr,jrc->jtc", mixer, w_all, preferred_element_type=jnp.float32)
     parts = parts.astype(jnp.bfloat16)
@@ -282,12 +288,13 @@
     grad_mixer = jnp.einsum("jtc,jrc->tr", g_all, w_all, preferred_element_type=jnp.float32)
     grad_long = grad_mixer * q_short
     bwd_sums = prefix(upper, shrink, grad_long)
-    bwd_got = exchange(bwd_sums[0].astype(jnp.bfloat16), count, False, 3)
+    bwd_final = bwd_sums[0].astype(jnp.bfloat16).reshape(mode_count, chan_width)
+    bwd_got = exchange(bwd_final, count, False, 3).reshape(count, width)
     bwd_entry = entry(source - place - 1, bwd_got) * block_decay
 
     grad_qshort = grad_mixer * long_out
     grad_gated = (
-        jnp.sum(scaled_grow * (bwd_sums + bwd_entry[None]), axis=1) + skip_gain[None, :] * grad_long
+        over_modes(scaled_grow * (bwd_sums + bwd_entry)) + skip_gain[None, :] * grad_long
     )
     grad_stack = jnp.stack([grad_qshort, grad_gated * v_short, grad_gated * k_short])
     after = from_behind(grad_stack[:, : tap_count - 1, :], "seq", -1)

time: 162 us -> 150 us (0.926)
  local copies, waits for them, and re-layouts: 25.8 us -> 9.16 us
  other arithmetic: 14.3 us -> 16.9 us
  matrix products: 18.3 us -> 20.3 us
    unnamed x43 -> x57, local copies, waits for them, and re-layouts: 22.5 us -> 6.29 us
    mul x1 -> x3, other arithmetic: 0.04 us -> 6.14 us  [the longest x1 3.07 us: per_device(): scaled_grow * (bwd_sums + bwd_entry)]
    reduce_sum x4 -> x2, other arithmetic: 6.43 us -> 2.3 us  [entry(): return jnp.sum(jnp.exp(-rate * span) * held, axis=0, keepdims=True)]
    dot_general x1, matrix products: 2.75 us -> 6.76 us  [per_device(): jnp.einsum('jtc,jrc->tr', g_all, w_all, preferred_element_type=jnp.float32)]
    dot_general x2, matrix products: 8.3 us -> 6.26 us  [prefix(): jnp.dot(tri, spread, precision=highest, preferred_element_type=jnp.float32)]
  transfers between devices with their start and end apart: 3 -> 3, of which waited for: 1 -> 1; matrix products, arithmetic and copies ran while one was open for 14% -> 15% of each run, Pallas kernels for 49% -> 53%
where the time goes in v9:
time: 150 us; the launch traced here: 148 us
  Pallas kernels  87.1 us (58%)
  matrix products  20.3 us (14%)
  other arithmetic  16.9 us (11%)
  starting transfers between devices  10.3 us (7%)
  local copies, waits for them, and re-layouts  9.16 us (6%)
  waiting for transfers between devices  2.72 us (2%)
    pallas_call x1, Pallas kernels, fetch(): pl.pallas_call(functools.partial(fetch_kernel, count, lanes), out_shape=(...  63.2 us
    pallas_call x2, Pallas kernels, exchange(): pl.pallas_call(functools.partial(exchange_kernel, count, later), out_shap...  23.9 us
    dot_general x1, matrix products, per_device(): jnp.einsum('tr,jrc->jtc', mixer, w_all, preferred_element_type=jnp.float32)  7.25 us
    dot_general x1, matrix products, per_device(): jnp.einsum('jtc,jrc->tr', g_all, w_all, preferred_element_type=jnp.float32)  6.76 us
    ppermute x2, starting transfers between devices, from_behind(): return lax.ppermute(block, axis, route)  6.4 us
    unnamed x57, local copies, waits for them, and re-layouts  6.29 us
    dot_general x2, matrix products, prefix(): jnp.dot(tri, spread, precision=highest, preferred_element_type=jnp.float32)  6.26 us
    all_to_all x1, starting transfers between devices, per_device(): received = lax.all_to_all(parts, 'ch', 0, 0, tiled=True)  3.9 us
  transfers between devices with their start and end apart: 3, of which 1 were waited for; matrix products, arithmetic and copies ran while one was open for 15% of the time, Pallas kernels for 53%

profile of v9, /device:TPU:65, one launch (start us, length us, event | category | flops | bytes accessed | tf_op | source)
XLA Modules:
  0.0 147.8 jit_solution(16017391117446842148)
XLA Ops:
  0.7 0.8 pad_maximum_fusion.2
  1.5 4.1 %collective-permute-start = (bf16[3,2,512]{2,1,0:T(2,128)(2,1)S(1)}, bf16[3,2,512]{2,1,0:T(2,128)(2,1)S(1)}, u32[]{:S(2)}, u32[]{:S(2)}) collective-permute-start(bf16[3,2,512]{2,1,0:T(2,128)(2,1)S(1)} %pad_maximum_fusion.2), channel_id=1, source_target_pairs={{0,16},{16,32},{32,48},{48,64},{64,80},{80,96},{96,112},{112,128},... | collective-permute-start | bytes 18440 | tf_op jit(solution)/shard_map/ppermute | solution.py:76
  6.9 0.8 copy.18
  7.7 0.8 multiply_bitcast_fusion.3
  8.5 2.5 %multiply_exponential_fusion.2 = f32[128,8192]{1,0:T(8,128)} fusion(f32[128]{0:T(128)S(1)} %iota_convert_fusion, f32[8192]{0:T(1024)S(1)} %neg.25), kind=kLoop, calls=%fused_computation.7 | loop fusion | flops 1048576 | bytes 4227584 | tf_op jit(solution)/shard_map/exp | solution.py:248
  11.6 63.2 %shard_map.120 = (bf16[16,512,512]{2,1,0:T(8,128)(2,1)}, bf16[16,128,512]{2,1,0:T(8,128)(2,1)}) custom-call(bf16[512,512]{1,0:T(8,128)(2,1)} %w_ref.1, bf16[128,512]{1,0:T(8,128)(2,1)} %g_ref.1), custom_call_target="tpu_custom_call" | custom-call | tf_op jit(solution)/shard_map/pallas_call | solution.py:200
  75.7 3.1 %fusion.2 = f32[128,8192]{1,0:T(8,128)S(1)} fusion(f32[128,8192]{1,0:T(8,128)S(1)} %constant_dynamic-update-slice_fusion, f32[8192]{0:T(1024)S(1)} %bitcast.67, f32[128]{0:T(128)S(1)} %iota_convert_fusion), kind=kOutput, calls=%fused_computation.4 | convolution fusion | flops 1612726272 | bytes 8421888 | tf_op jit(solution)/shard_map/dot_general | solution.py:260
  78.8 1.9 %copy-done.1 = f32[128,8192]{1,0:T(8,128)} copy-done((f32[128,8192]{1,0:T(8,128)}, f32[128,8192]{1,0:T(8,128)S(1)}, u32[]{:S(2)}) %copy-start.1) | copy-done | bytes 4194328
  80.8 1.1 fusion.21
  82.5 8.9 %shard_map.121 = bf16[16,16,512]{2,1,0:T(8,128)(2,1)} custom-call(bf16[16,512]{1,0:T(8,128)(2,1)} %convert_element_type.66.final_ref), custom_call_target="tpu_custom_call" | custom-call | tf_op jit(solution)/shard_map/pallas_call | solution.py:60
  91.4 1.1 multiply_reduce_fusion.1
  92.6 3.1 %add_multiply_fusion.1 = f32[128,8192]{1,0:T(8,128)S(1)} fusion(f32[128,8192]{1,0:T(8,128)} %copy-done.1, f32[8192]{0:T(1024)S(1)} %exponential_multiply_fusion.1, f32[128]{0:T(128)S(1)} %iota_convert_fusion, f32[8192]{0:T(1024)S(1)} %neg.25, f32[8192]{0:T(1024)S(1)} %bitcast.77), kind=kLoop, calls=%fused_computation.3 | loop fusion | flops 4194304 | bytes 8487424 | tf_op jit(solution)/shard_map/mul | solution.py:280
  96.2 7.2 %convert_bitcast_fusion = bf16[16,128,512]{1,2,0:T(8,128)(2,1)} fusion(bf16[16,512,512]{2,1,0:T(8,128)(2,1)} %get-tuple-element.13, f32[128,512]{1,0:T(8,128)S(1)} %fusion.14, f32[3,128,512]{2,1,0:T(8,128)S(1)} %fusion.11), kind=kOutput, calls=%fused_computation.8 | convolution fusion | flops 1074921472 | bytes 11010048 | tf_op jit(solution)/shard_map/tr,jrc->jtc/dot_general | solution.py:282
  103.5 3.9 %all-to-all-start = ((bf16[16,128,512]{1,2,0:T(8,128)(2,1)}), bf16[16,128,512]{1,2,0:T(8,128)(2,1)S(1)}, u32[]{:S(2)}, u32[]{:S(2)}) async-start(bf16[16,128,512]{1,2,0:T(8,128)(2,1)} %convert_bitcast_fusion), calls=%async_computation | async-start | bytes 4194304 | tf_op jit(solution)/shard_map/all_to_all | solution.py:285
  107.4 6.8 %constant_dynamic-update-slice_fusion.31 = (f32[128,8192]{1,0:T(8,128)S(1)}, f32[128,512]{1,0:T(8,128)S(1)}, f32[1,128,512]{2,1,0:T(8,128)S(1)}) fusion(f32[3,128,512]{2,1,0:T(8,128)S(1)} %fusion.11, f32[128,512]{1,0:T(8,128)} %copy-done.2, bf16[16,128,512]{2,1,0:T(8,128)(2,1)} %get-tuple-element.12, bf16[16,512,512]{2,1,0:T(8,128)(2,1)} %get-tuple-element.13), kind=kOutput, calls=%fused_computation.105 | convolution fusion | flops 1073872896 | bytes 11796480 | tf_op jit(solution)/shard_map/jtc,jrc->tr/dot_general | solution.py:288
  114.8 3.1 %fusion = f32[128,8192]{1,0:T(8,128)S(1)} fusion(f32[128,8192]{1,0:T(8,128)S(1)} %constant_dynamic-update-slice_fusion.16, f32[128]{0:T(128)S(1)} %copy-done.9, f32[8192]{0:T(1024)S(1)} %neg.25), kind=kOutput, calls=%fused_computation.1 | convolution fusion | flops 1612726272 | bytes 8421888 | tf_op jit(solution)/shard_map/dot_general | solution.py:260
  117.9 1.9 %copy-done = f32[128,8192]{1,0:T(8,128)} copy-done((f32[128,8192]{1,0:T(8,128)}, f32[128,8192]{1,0:T(8,128)S(1)}, u32[]{:S(2)}) %copy-start) | copy-done | bytes 4194328
  120.6 15.0 %shard_map.122 = bf16[16,16,512]{2,1,0:T(8,128)(2,1)} custom-call(bf16[16,512]{1,0:T(8,128)(2,1)} %convert_element_type.72.final_ref), custom_call_target="tpu_custom_call" | custom-call | tf_op jit(solution)/shard_map/pallas_call | solution.py:60
  135.6 1.2 multiply_reduce_fusion
  136.8 3.1 %add_multiply_fusion = f32[128,8192]{1,0:T(8,128)S(1)} fusion(f32[128,8192]{1,0:T(8,128)} %copy-done, f32[8192]{0:T(1024)S(1)} %exponential_multiply_fusion, f32[8192]{0:T(1024)S(1)} %bitcast.70, f32[128]{0:T(128)} %copy-done.8, f32[8192]{0:T(1024)S(1)} %bitcast.78), kind=kLoop, calls=%fused_computation | loop fusion | flops 4194304 | bytes 8487424 | tf_op jit(solution)/shard_map/mul | solution.py:297
  140.6 2.3 %collective-permute-start.1 = (f32[3,2,512]{2,1,0:T(2,128)S(1)}, f32[3,2,512]{2,1,0:T(2,128)S(1)}, u32[]{:S(2)}, u32[]{:S(2)}) collective-permute-start(f32[3,2,512]{2,1,0:T(2,128)S(1)} %slice.249), channel_id=1, source_target_pairs={{16,0},{32,16},{48,32},{64,48},{80,64},{96,80},{112,96},{128,112},... | collective-permute-start | bytes 36872 | tf_op jit(solution)/shard_map/ppermute | solution.py:76
  142.9 2.7 %collective-permute-done.1 = f32[3,2,512]{2,1,0:T(2,128)S(1)} collective-permute-done((f32[3,2,512]{2,1,0:T(2,128)S(1)}, f32[3,2,512]{2,1,0:T(2,128)S(1)}, u32[]{:S(2)}, u32[]{:S(2)}) %collective-permute-start.1) | collective-permute-done | bytes 12320 | tf_op jit(solution)/shard_map/ppermute | solution.py:76
  145.9 0.8 slice_bitcast_fusion.3
  147.0 0.8 copy.15
  (80 shorter events, 6.3 us)
Async XLA Ops:
  0.6 74.2 %copy-start.3 = (bf16[128,512]{1,0:T(8,128)(2,1)S(1)}, bf16[128,512]{1,0:T(8,128)(2,1)}, u32[]{:S(2)}) copy-start(bf16[128,512]{1,0:T(8,128)(2,1)} %param.11) | copy-start | bytes 393220
  0.6 74.2 %copy-start.4 = (bf16[128,512]{1,0:T(8,128)(2,1)S(1)}, bf16[128,512]{1,0:T(8,128)(2,1)}, u32[]{:S(2)}) copy-start(bf16[128,512]{1,0:T(8,128)(2,1)} %param.10) | copy-start | bytes 393220
  0.7 74.2 %copy-start.5 = (bf16[128,512]{1,0:T(8,128)(2,1)S(1)}, bf16[128,512]{1,0:T(8,128)(2,1)}, u32[]{:S(2)}) copy-start(bf16[128,512]{1,0:T(8,128)(2,1)} %param.9) | copy-start | bytes 393220
  1.5 73.4 %collective-permute-start = (bf16[3,2,512]{2,1,0:T(2,128)(2,1)S(1)}, bf16[3,2,512]{2,1,0:T(2,128)(2,1)S(1)}, u32[]{:S(2)}, u32[]{:S(2)}) collective-permute-start(bf16[3,2,512]{2,1,0:T(2,128)(2,1)S(1)} %pad_maximum_fusion.2), channel_id=1, source_target_pairs={{0,16},{16,32},{32,48},{48,64},{64,80},{80,96},{96,112},{112,128},... | collective-permute-start | bytes 18440 | tf_op jit(solution)/shard_map/ppermute | solution.py:76
  5.6 87.0 %copy-start.8 = (f32[128]{0:T(128)}, f32[128]{0:T(128)S(1)}, u32[]{:S(2)}) copy-start(f32[128]{0:T(128)S(1)} %iota_convert_fusion) | copy-start | bytes 1540
  6.9 68.1 %copy-start.6 = (f32[3,512]{1,0:T(4,128)}, f32[3,512]{1,0:T(4,128)S(1)}, u32[]{:S(2)}) copy-start(f32[3,512]{1,0:T(4,128)S(1)} %get-tuple-element.32) | copy-start | bytes 18436
  78.8 2.0 %copy-start.1 = (f32[128,8192]{1,0:T(8,128)}, f32[128,8192]{1,0:T(8,128)S(1)}, u32[]{:S(2)}) copy-start(f32[128,8192]{1,0:T(8,128)S(1)} %fusion.2) | copy-start | bytes 12582916
  92.6 3.1 %copy-start.10 = (f32[512]{0:T(512)S(1)}, f32[512]{0:T(512)}, u32[]{:S(2)}) copy-start(f32[512]{0:T(512)} %param.15) | copy-start | bytes 6148
  96.2 7.3 %copy-start.2 = (f32[128,512]{1,0:T(8,128)}, f32[128,512]{1,0:T(8,128)S(1)}, u32[]{:S(2)}) copy-start(f32[128,512]{1,0:T(8,128)S(1)} %fusion.14) | copy-start | bytes 786436
  103.5 43.2 %all-to-all-start = ((bf16[16,128,512]{1,2,0:T(8,128)(2,1)}), bf16[16,128,512]{1,2,0:T(8,128)(2,1)S(1)}, u32[]{:S(2)}, u32[]{:S(2)}) async-start(bf16[16,128,512]{1,2,0:T(8,128)(2,1)} %convert_bitcast_fusion), calls=%async_computation | async-start | bytes 4194304 | tf_op jit(solution)/shard_map/all_to_all | solution.py:285
  114.1 0.7 copy-start.9
  117.9 1.9 %copy-start = (f32[128,8192]{1,0:T(8,128)}, f32[128,8192]{1,0:T(8,128)S(1)}, u32[]{:S(2)}) copy-start(f32[128,8192]{1,0:T(8,128)S(1)} %fusion) | copy-start | bytes 12582916
  136.8 3.1 %copy-start.11 = (f32[512]{0:T(512)S(1)}, f32[512]{0:T(512)}, u32[]{:S(2)}) copy-start(f32[512]{0:T(512)} %param.15) | copy-start | bytes 6148
  139.9 5.8 %copy-start.7 = (f32[3,512]{1,0:T(4,128)S(1)}, f32[3,512]{1,0:T(4,128)}, u32[]{:S(2)}) copy-start(f32[3,512]{1,0:T(4,128)} %copy-done.6) | copy-start | bytes 18436
  140.6 5.0 %collective-permute-start.1 = (f32[3,2,512]{2,1,0:T(2,128)S(1)}, f32[3,2,512]{2,1,0:T(2,128)S(1)}, u32[]{:S(2)}, u32[]{:S(2)}) collective-permute-start(f32[3,2,512]{2,1,0:T(2,128)S(1)} %slice.249), channel_id=1, source_target_pairs={{16,0},{32,16},{48,32},{64,48},{80,64},{96,80},{112,96},{128,112},... | collective-permute-start | bytes 36872 | tf_op jit(solution)/shard_map/ppermute | solution.py:76

commit v10 on v9

--- a/solution.py
+++ b/solution.py
@@ -131,25 +131,31 @@
     own_g.start()
 
     sends = []
-
-    def send(source, origin, peer):
+    pieces = w_recv.shape[0] // count
+    depth = w_ref.shape[0] // pieces
+
+    def rows(piece):
+        return pl.ds(piece * depth, depth)
+
+    def send(origin, piece, peer, own):
+        source = w_ref.at[rows(piece)] if own else w_all.at[origin, rows(piece)]
         copy = pltpu.make_async_remote_copy(
             src_ref=source,
-            dst_ref=w_all.at[origin],
+            dst_ref=w_all.at[origin, rows(piece)],
             send_sem=w_send.at[len(sends)],
-            recv_sem=w_recv.at[origin],
+            recv_sem=w_recv.at[origin * pieces + piece],
             device_id=(peer, lane),
             device_id_type=MESH,
         )
         copy.start()
         sends.append(copy)
 
-    def arrived(origin):
+    def arrived(origin, piece):
         pltpu.make_async_remote_copy(
-            src_ref=w_all.at[origin],
-            dst_ref=w_all.at[origin],
+            src_ref=w_all.at[origin, rows(piece)],
+            dst_ref=w_all.at[origin, rows(piece)],
             send_sem=w_send.at[0],
-            recv_sem=w_recv.at[origin],
+            recv_sem=w_recv.at[origin * pieces + piece],
             device_id=(me, lane),
             device_id_type=MESH,
         ).wait_recv()
@@ -160,27 +166,30 @@
     def left_origin(step):
         return 2 * ((ring + step - 1) % half) + core
 
-    send(w_ref, me, partner)
-    if right_steps >= 1:
-        send(w_ref, me, right)
-    if left_steps >= 1:
-        send(w_ref, me, left)
+    for piece in range(pieces):
+        if right_steps >= 1:
+            send(me, piece, right, True)
+        if left_steps >= 1:
+            send(me, piece, left, True)
+        send(me, piece, partner, True)
     for step in range(2, max(right_steps, left_steps) + 2):
-        if step <= right_steps + 1:
-            origin = right_origin(step)
-            arrived(origin)
-            if step <= right_steps:
-                send(w_all.at[origin], origin, right)
-            send(w_all.at[origin], origin, partner)
-        if step <= left_steps + 1:
-            origin = left_origin(step)
-            arrived(origin)
-            if step <= left_steps:
-                send(w_all.at[origin], origin, left)
-            send(w_all.at[origin], origin, partner)
+        for piece in range(pieces):
+            if step <= right_steps + 1:
+                origin = right_origin(step)
+                arrived(origin, piece)
+                if step <= right_steps:
+                    send(origin, piece, right, False)
+                send(origin, piece, partner, False)
+            if step <= left_steps + 1:
+                origin = left_origin(step)
+                arrived(origin, piece)
+                if step <= left_steps:
+                    send(origin, piece, left, False)
+                send(origin, piece, partner, False)
 
     for twin in range(half):
-        arrived(2 * twin + 1 - core)
+        for piece in range(pieces):
+            arrived(2 * twin + 1 - core, piece)
     for copy in sends:
         copy.wait_send()
     for other in range(lanes):
@@ -194,9 +203,9 @@
     own_g.wait()
 
 
-def fetch(out_weight, grad_out, count, lanes):
+def fetch(out_weight, grad_out, count, lanes, pieces=4):
     half = count // 2
-    sends = half + half // 2 + (half - 1 - half // 2)
+    sends = (half + half // 2 + (half - 1 - half // 2)) * pieces
     return pl.pallas_call(
         functools.partial(fetch_kernel, count, lanes),
         out_shape=(
@@ -207,7 +216,7 @@
         out_specs=(pl.BlockSpec(memory_space=pl.ANY), pl.BlockSpec(memory_space=pl.ANY)),
         scratch_shapes=[
             pltpu.SemaphoreType.DMA((sends,)),
-            pltpu.SemaphoreType.DMA((count,)),
+            pltpu.SemaphoreType.DMA((count * pieces,)),
             pltpu.SemaphoreType.DMA((lanes,)),
             pltpu.SemaphoreType.DMA((lanes,)),
             pltpu.SemaphoreType.DMA((2,)),

time: 150 us -> 145 us (0.967)
  Pallas kernels: 87.1 us -> 82.4 us
    pallas_call x1, Pallas kernels: 63.2 us -> 53.3 us  [fetch(): pl.pallas_call(functools.partial(fetch_kernel, count, lanes), out_shape=(...]
    pallas_call x2, Pallas kernels: 23.9 us -> 29 us  [exchange(): pl.pallas_call(functools.partial(exchange_kernel, count, later), out_shap...]
  transfers between devices with their start and end apart: 3 -> 3, of which waited for: 1 -> 1; matrix products, arithmetic and copies ran while one was open for 15% -> 16% of each run, Pallas kernels for 53% -> 48%
where the time goes in v10:
time: 145 us; the launch traced here: 143 us
  Pallas kernels  82.4 us (57%)
  matrix products  20.3 us (14%)
  other arithmetic  16.9 us (12%)
  starting transfers between devices  10.3 us (7%)
  local copies, waits for them, and re-layouts  9.16 us (6%)
  waiting for transfers between devices  2.72 us (2%)
    pallas_call x1, Pallas kernels, fetch(): pl.pallas_call(functools.partial(fetch_kernel, count, lanes), out_shape=(...  53.3 us
    pallas_call x2, Pallas kernels, exchange(): pl.pallas_call(functools.partial(exchange_kernel, count, later), out_shap...  29 us
    dot_general x1, matrix products, per_device(): jnp.einsum('tr,jrc->jtc', mixer, w_all, preferred_element_type=jnp.float32)  7.25 us
    dot_general x1, matrix products, per_device(): jnp.einsum('jtc,jrc->tr', g_all, w_all, preferred_element_type=jnp.float32)  6.75 us
    ppermute x2, starting transfers between devices, from_behind(): return lax.ppermute(block, axis, route)  6.4 us
    unnamed x57, local copies, waits for them, and re-layouts  6.29 us
    dot_general x2, matrix products, prefix(): jnp.dot(tri, spread, precision=highest, preferred_element_type=jnp.float32)  6.27 us
    all_to_all x1, starting transfers between devices, per_device(): received = lax.all_to_all(parts, 'ch', 0, 0, tiled=True)  3.9 us
  transfers between devices with their start and end apart: 3, of which 1 were waited for; matrix products, arithmetic and copies ran while one was open for 16% of the time, Pallas kernels for 48%

profile of v10, /device:TPU:65, one launch (start us, length us, event | category | flops | bytes accessed | tf_op | source)
XLA Modules:
  0.0 143.0 jit_solution(1271848063951300560)
XLA Ops:
  0.7 0.8 pad_maximum_fusion.2
  1.5 4.1 %collective-permute-start = (bf16[3,2,512]{2,1,0:T(2,128)(2,1)S(1)}, bf16[3,2,512]{2,1,0:T(2,128)(2,1)S(1)}, u32[]{:S(2)}, u32[]{:S(2)}) collective-permute-start(bf16[3,2,512]{2,1,0:T(2,128)(2,1)S(1)} %pad_maximum_fusion.2), channel_id=1, source_target_pairs={{0,16},{16,32},{32,48},{48,64},{64,80},{80,96},{96,112},{112,128},... | collective-permute-start | bytes 18440 | tf_op jit(solution)/shard_map/ppermute | solution.py:76
  6.9 0.8 copy.18
  7.7 0.8 multiply_bitcast_fusion.3
  8.5 2.5 %multiply_exponential_fusion.2 = f32[128,8192]{1,0:T(8,128)} fusion(f32[128]{0:T(128)S(1)} %iota_convert_fusion, f32[8192]{0:T(1024)S(1)} %neg.25), kind=kLoop, calls=%fused_computation.7 | loop fusion | flops 1048576 | bytes 4227584 | tf_op jit(solution)/shard_map/exp | solution.py:257
  11.6 53.3 %shard_map.120 = (bf16[16,512,512]{2,1,0:T(8,128)(2,1)}, bf16[16,128,512]{2,1,0:T(8,128)(2,1)}) custom-call(bf16[512,512]{1,0:T(8,128)(2,1)} %w_ref.1, bf16[128,512]{1,0:T(8,128)(2,1)} %g_ref.1), custom_call_target="tpu_custom_call" | custom-call | tf_op jit(solution)/shard_map/pallas_call | solution.py:209
  65.8 3.1 %fusion.2 = f32[128,8192]{1,0:T(8,128)S(1)} fusion(f32[128,8192]{1,0:T(8,128)S(1)} %constant_dynamic-update-slice_fusion, f32[8192]{0:T(1024)S(1)} %bitcast.67, f32[128]{0:T(128)S(1)} %iota_convert_fusion), kind=kOutput, calls=%fused_computation.4 | convolution fusion | flops 1612726272 | bytes 8421888 | tf_op jit(solution)/shard_map/dot_general | solution.py:269
  69.0 1.9 %copy-done.1 = f32[128,8192]{1,0:T(8,128)} copy-done((f32[128,8192]{1,0:T(8,128)}, f32[128,8192]{1,0:T(8,128)S(1)}, u32[]{:S(2)}) %copy-start.1) | copy-done | bytes 4194328
  70.9 1.1 fusion.21
  72.6 13.8 %shard_map.121 = bf16[16,16,512]{2,1,0:T(8,128)(2,1)} custom-call(bf16[16,512]{1,0:T(8,128)(2,1)} %convert_element_type.66.final_ref), custom_call_target="tpu_custom_call" | custom-call | tf_op jit(solution)/shard_map/pallas_call | solution.py:60
  86.4 1.1 multiply_reduce_fusion.1
  87.7 3.1 %add_multiply_fusion.1 = f32[128,8192]{1,0:T(8,128)S(1)} fusion(f32[128,8192]{1,0:T(8,128)} %copy-done.1, f32[8192]{0:T(1024)S(1)} %exponential_multiply_fusion.1, f32[128]{0:T(128)S(1)} %iota_convert_fusion, f32[8192]{0:T(1024)S(1)} %neg.25, f32[8192]{0:T(1024)S(1)} %bitcast.77), kind=kLoop, calls=%fused_computation.3 | loop fusion | flops 4194304 | bytes 8487424 | tf_op jit(solution)/shard_map/mul | solution.py:289
  91.3 7.2 %convert_bitcast_fusion = bf16[16,128,512]{1,2,0:T(8,128)(2,1)} fusion(bf16[16,512,512]{2,1,0:T(8,128)(2,1)} %get-tuple-element.13, f32[128,512]{1,0:T(8,128)S(1)} %fusion.14, f32[3,128,512]{2,1,0:T(8,128)S(1)} %fusion.11), kind=kOutput, calls=%fused_computation.8 | convolution fusion | flops 1074921472 | bytes 11010048 | tf_op jit(solution)/shard_map/tr,jrc->jtc/dot_general | solution.py:291
  98.5 3.9 %all-to-all-start = ((bf16[16,128,512]{1,2,0:T(8,128)(2,1)}), bf16[16,128,512]{1,2,0:T(8,128)(2,1)S(1)}, u32[]{:S(2)}, u32[]{:S(2)}) async-start(bf16[16,128,512]{1,2,0:T(8,128)(2,1)} %convert_bitcast_fusion), calls=%async_computation | async-start | bytes 4194304 | tf_op jit(solution)/shard_map/all_to_all | solution.py:294
  102.4 6.8 %constant_dynamic-update-slice_fusion.31 = (f32[128,8192]{1,0:T(8,128)S(1)}, f32[128,512]{1,0:T(8,128)S(1)}, f32[1,128,512]{2,1,0:T(8,128)S(1)}) fusion(f32[3,128,512]{2,1,0:T(8,128)S(1)} %fusion.11, f32[128,512]{1,0:T(8,128)} %copy-done.2, bf16[16,128,512]{2,1,0:T(8,128)(2,1)} %get-tuple-element.12, bf16[16,512,512]{2,1,0:T(8,128)(2,1)} %get-tuple-element.13), kind=kOutput, calls=%fused_computation.105 | convolution fusion | flops 1073872896 | bytes 11796480 | tf_op jit(solution)/shard_map/jtc,jrc->tr/dot_general | solution.py:297
  109.8 3.1 %fusion = f32[128,8192]{1,0:T(8,128)S(1)} fusion(f32[128,8192]{1,0:T(8,128)S(1)} %constant_dynamic-update-slice_fusion.16, f32[128]{0:T(128)S(1)} %copy-done.9, f32[8192]{0:T(1024)S(1)} %neg.25), kind=kOutput, calls=%fused_computation.1 | convolution fusion | flops 1612726272 | bytes 8421888 | tf_op jit(solution)/shard_map/dot_general | solution.py:269
  113.0 1.9 %copy-done = f32[128,8192]{1,0:T(8,128)} copy-done((f32[128,8192]{1,0:T(8,128)}, f32[128,8192]{1,0:T(8,128)S(1)}, u32[]{:S(2)}) %copy-start) | copy-done | bytes 4194328
  115.6 15.2 %shard_map.122 = bf16[16,16,512]{2,1,0:T(8,128)(2,1)} custom-call(bf16[16,512]{1,0:T(8,128)(2,1)} %convert_element_type.72.final_ref), custom_call_target="tpu_custom_call" | custom-call | tf_op jit(solution)/shard_map/pallas_call | solution.py:60
  130.9 1.2 multiply_reduce_fusion
  132.1 3.1 %add_multiply_fusion = f32[128,8192]{1,0:T(8,128)S(1)} fusion(f32[128,8192]{1,0:T(8,128)} %copy-done, f32[8192]{0:T(1024)S(1)} %exponential_multiply_fusion, f32[8192]{0:T(1024)S(1)} %bitcast.70, f32[128]{0:T(128)} %copy-done.8, f32[8192]{0:T(1024)S(1)} %bitcast.78), kind=kLoop, calls=%fused_computation | loop fusion | flops 4194304 | bytes 8487424 | tf_op jit(solution)/shard_map/mul | solution.py:306
  135.9 2.3 %collective-permute-start.1 = (f32[3,2,512]{2,1,0:T(2,128)S(1)}, f32[3,2,512]{2,1,0:T(2,128)S(1)}, u32[]{:S(2)}, u32[]{:S(2)}) collective-permute-start(f32[3,2,512]{2,1,0:T(2,128)S(1)} %slice.249), channel_id=1, source_target_pairs={{16,0},{32,16},{48,32},{64,48},{80,64},{96,80},{112,96},{128,112},... | collective-permute-start | bytes 36872 | tf_op jit(solution)/shard_map/ppermute | solution.py:76
  138.2 2.7 %collective-permute-done.1 = f32[3,2,512]{2,1,0:T(2,128)S(1)} collective-permute-done((f32[3,2,512]{2,1,0:T(2,128)S(1)}, f32[3,2,512]{2,1,0:T(2,128)S(1)}, u32[]{:S(2)}, u32[]{:S(2)}) %collective-permute-start.1) | collective-permute-done | bytes 12320 | tf_op jit(solution)/shard_map/ppermute | solution.py:76
  141.2 0.8 slice_bitcast_fusion.3
  142.3 0.8 copy.15
  (80 shorter events, 6.3 us)
Async XLA Ops:
  0.6 64.3 %copy-start.3 = (bf16[128,512]{1,0:T(8,128)(2,1)S(1)}, bf16[128,512]{1,0:T(8,128)(2,1)}, u32[]{:S(2)}) copy-start(bf16[128,512]{1,0:T(8,128)(2,1)} %param.11) | copy-start | bytes 393220
  0.6 64.3 %copy-start.4 = (bf16[128,512]{1,0:T(8,128)(2,1)S(1)}, bf16[128,512]{1,0:T(8,128)(2,1)}, u32[]{:S(2)}) copy-start(bf16[128,512]{1,0:T(8,128)(2,1)} %param.10) | copy-start | bytes 393220
  0.7 64.3 %copy-start.5 = (bf16[128,512]{1,0:T(8,128)(2,1)S(1)}, bf16[128,512]{1,0:T(8,128)(2,1)}, u32[]{:S(2)}) copy-start(bf16[128,512]{1,0:T(8,128)(2,1)} %param.9) | copy-start | bytes 393220
  1.5 63.5 %collective-permute-start = (bf16[3,2,512]{2,1,0:T(2,128)(2,1)S(1)}, bf16[3,2,512]{2,1,0:T(2,128)(2,1)S(1)}, u32[]{:S(2)}, u32[]{:S(2)}) collective-permute-start(bf16[3,2,512]{2,1,0:T(2,128)(2,1)S(1)} %pad_maximum_fusion.2), channel_id=1, source_target_pairs={{0,16},{16,32},{32,48},{48,64},{64,80},{80,96},{96,112},{112,128},... | collective-permute-start | bytes 18440 | tf_op jit(solution)/shard_map/ppermute | solution.py:76
  5.6 82.1 %copy-start.8 = (f32[128]{0:T(128)}, f32[128]{0:T(128)S(1)}, u32[]{:S(2)}) copy-start(f32[128]{0:T(128)S(1)} %iota_convert_fusion) | copy-start | bytes 1540
  6.9 58.2 %copy-start.6 = (f32[3,512]{1,0:T(4,128)}, f32[3,512]{1,0:T(4,128)S(1)}, u32[]{:S(2)}) copy-start(f32[3,512]{1,0:T(4,128)S(1)} %get-tuple-element.32) | copy-start | bytes 18436
  69.0 2.0 %copy-start.1 = (f32[128,8192]{1,0:T(8,128)}, f32[128,8192]{1,0:T(8,128)S(1)}, u32[]{:S(2)}) copy-start(f32[128,8192]{1,0:T(8,128)S(1)} %fusion.2) | copy-start | bytes 12582916
  87.6 3.1 %copy-start.10 = (f32[512]{0:T(512)S(1)}, f32[512]{0:T(512)}, u32[]{:S(2)}) copy-start(f32[512]{0:T(512)} %param.15) | copy-start | bytes 6148
  91.2 7.3 %copy-start.2 = (f32[128,512]{1,0:T(8,128)}, f32[128,512]{1,0:T(8,128)S(1)}, u32[]{:S(2)}) copy-start(f32[128,512]{1,0:T(8,128)S(1)} %fusion.14) | copy-start | bytes 786436
  98.5 43.5 %all-to-all-start = ((bf16[16,128,512]{1,2,0:T(8,128)(2,1)}), bf16[16,128,512]{1,2,0:T(8,128)(2,1)S(1)}, u32[]{:S(2)}, u32[]{:S(2)}) async-start(bf16[16,128,512]{1,2,0:T(8,128)(2,1)} %convert_bitcast_fusion), calls=%async_computation | async-start | bytes 4194304 | tf_op jit(solution)/shard_map/all_to_all | solution.py:294
  109.2 0.7 copy-start.9
  113.0 1.9 %copy-start = (f32[128,8192]{1,0:T(8,128)}, f32[128,8192]{1,0:T(8,128)S(1)}, u32[]{:S(2)}) copy-start(f32[128,8192]{1,0:T(8,128)S(1)} %fusion) | copy-start | bytes 12582916
  132.1 3.1 %copy-start.11 = (f32[512]{0:T(512)S(1)}, f32[512]{0:T(512)}, u32[]{:S(2)}) copy-start(f32[512]{0:T(512)} %param.15) | copy-start | bytes 6148
  135.2 5.8 %copy-start.7 = (f32[3,512]{1,0:T(4,128)S(1)}, f32[3,512]{1,0:T(4,128)}, u32[]{:S(2)}) copy-start(f32[3,512]{1,0:T(4,128)} %copy-done.6) | copy-start | bytes 18436
  135.9 5.0 %collective-permute-start.1 = (f32[3,2,512]{2,1,0:T(2,128)S(1)}, f32[3,2,512]{2,1,0:T(2,128)S(1)}, u32[]{:S(2)}, u32[]{:S(2)}) collective-permute-start(f32[3,2,512]{2,1,0:T(2,128)S(1)} %slice.249), channel_id=1, source_target_pairs={{16,0},{32,16},{48,32},{64,48},{80,64},{96,80},{112,96},{128,112},... | collective-permute-start | bytes 36872 | tf_op jit(solution)/shard_map/ppermute | solution.py:76

commit v11 on v10

--- a/solution.py
+++ b/solution.py
@@ -76,7 +76,9 @@
     return lax.ppermute(block, axis, route)
 
 
-def fetch_kernel(count, lanes, w_ref, g_ref, w_all, g_all, w_send, w_recv, g_send, g_recv, own_sem):
+def fetch_kernel(
+    count, lanes, w_ref, g_ref, f_ref, w_all, g_all, f_got, w_send, w_recv, g_send, g_recv, own_sem, f_send, f_recv
+):
     me = lax.axis_index("seq")
     lane = lax.axis_index("ch")
     half = count // 2
@@ -85,19 +87,36 @@
     right = 2 * ((ring + 1) % half) + core
     left = 2 * ((ring + half - 1) % half) + core
     partner = me + 1 - 2 * core
-    right_steps = half // 2
-    left_steps = half - 1 - right_steps
-
     barrier = pltpu.get_barrier_semaphore()
-    for peer in (right, left, partner):
-        pl.semaphore_signal(barrier, inc=1, device_id=(peer, lane), device_id_type=MESH)
+    for peer in range(count):
+
+        @pl.when(me != peer)
+        def _():
+            pl.semaphore_signal(barrier, inc=1, device_id=(peer, lane), device_id_type=MESH)
+
     for other in range(lanes):
 
         @pl.when(lane != other)
         def _():
             pl.semaphore_signal(barrier, inc=1, device_id=(me, other), device_id_type=MESH)
 
-    pl.semaphore_wait(barrier, 3 + lanes - 1)
+    pl.semaphore_wait(barrier, count - 1 + lanes - 1)
+
+    def state_link(peer, slot):
+        return pltpu.make_async_remote_copy(
+            src_ref=f_ref,
+            dst_ref=f_got.at[slot],
+            send_sem=f_send.at[peer],
+            recv_sem=f_recv.at[slot],
+            device_id=(peer, lane),
+            device_id_type=MESH,
+        )
+
+    for peer in range(count):
+
+        @pl.when(me < peer)
+        def _():
+            state_link(peer, me).start()
 
     def grad_link(other):
         return pltpu.make_async_remote_copy(
@@ -160,30 +179,37 @@
             device_id_type=MESH,
         ).wait_recv()
 
+    def right_steps(piece):
+        return half // 2 if piece < pieces // 2 else half - 1 - half // 2
+
+    def left_steps(piece):
+        return half - 1 - right_steps(piece)
+
     def right_origin(step):
         return 2 * ((ring - step + 1 + half) % half) + core
 
     def left_origin(step):
         return 2 * ((ring + step - 1) % half) + core
 
+    longest = max(max(right_steps(p), left_steps(p)) for p in range(pieces))
     for piece in range(pieces):
-        if right_steps >= 1:
+        if right_steps(piece) >= 1:
             send(me, piece, right, True)
-        if left_steps >= 1:
+        if left_steps(piece) >= 1:
             send(me, piece, left, True)
         send(me, piece, partner, True)
-    for step in range(2, max(right_steps, left_steps) + 2):
+    for step in range(2, longest + 2):
         for piece in range(pieces):
-            if step <= right_steps + 1:
+            if step <= right_steps(piece) + 1:
                 origin = right_origin(step)
                 arrived(origin, piece)
-                if step <= right_steps:
+                if step <= right_steps(piece):
                     send(origin, piece, right, False)
                 send(origin, piece, partner, False)
-            if step <= left_steps + 1:
+            if step <= left_steps(piece) + 1:
                 origin = left_origin(step)
                 arrived(origin, piece)
-                if step <= left_steps:
+                if step <= left_steps(piece):
                     send(origin, piece, left, False)
                 send(origin, piece, partner, False)
 
@@ -199,11 +225,21 @@
             grad_link(other).wait_send()
             grad_arrival(other).wait_recv()
 
+    for peer in range(count):
+
+        @pl.when(me < peer)
+        def _():
+            state_link(peer, me).wait_send()
+
+        @pl.when(me > peer)
+        def _():
+            state_link(peer, peer).wait_recv()
+
     own_w.wait()
     own_g.wait()
 
 
-def fetch(out_weight, grad_out, count, lanes, pieces=4):
+def fetch(out_weight, grad_out, final, count, lanes, pieces=4):
     half = count // 2
     sends = (half + half // 2 + (half - 1 - half // 2)) * pieces
     return pl.pallas_call(
@@ -211,18 +247,25 @@
         out_shape=(
             jax.ShapeDtypeStruct((count,) + out_weight.shape, out_weight.dtype),
             jax.ShapeDtypeStruct((lanes,) + grad_out.shape, grad_out.dtype),
+            jax.ShapeDtypeStruct((count,) + final.shape, final.dtype),
         ),
-        in_specs=[pl.BlockSpec(memory_space=pl.ANY)] * 2,
-        out_specs=(pl.BlockSpec(memory_space=pl.ANY), pl.BlockSpec(memory_space=pl.ANY)),
+        in_specs=[pl.BlockSpec(memory_space=pl.ANY)] * 2 + [pl.BlockSpec(memory_space=pltpu.VMEM)],
+        out_specs=(
+            pl.BlockSpec(memory_space=pl.ANY),
+            pl.BlockSpec(memory_space=pl.ANY),
+            pl.BlockSpec(memory_space=pltpu.VMEM),
+        ),
         scratch_shapes=[
             pltpu.SemaphoreType.DMA((sends,)),
             pltpu.SemaphoreType.DMA((count * pieces,)),
             pltpu.SemaphoreType.DMA((lanes,)),
             pltpu.SemaphoreType.DMA((lanes,)),
             pltpu.SemaphoreType.DMA((2,)),
+            pltpu.SemaphoreType.DMA((count,)),
+            pltpu.SemaphoreType.DMA((count,)),
         ],
         compiler_params=pltpu.CompilerParams(collective_id=1, has_side_effects=True),
-    )(out_weight, grad_out)
+    )(out_weight, grad_out, final)
 
 
 def per_device(query, key, value, short_taps, decay_rate, residue, skip_gain, out_weight, grad_out):
@@ -234,7 +277,6 @@
     place = lax.axis_index("seq")
 
     lanes = lax.axis_size("ch")
-    w_all, g_all = fetch(out_weight, grad_out, count, lanes)
 
     streams = jnp.stack([query, key, value])
     before = from_behind(streams[:, tok_rows - (tap_count - 1) :, :], "seq", 1)
@@ -283,7 +325,9 @@
 
     fwd_sums = prefix(lower, grow, gated)
     fwd_final = (shrink[tok_rows - 1] * fwd_sums[tok_rows - 1]).astype(jnp.bfloat16)
-    fwd_got = exchange(fwd_final.reshape(mode_count, chan_width), count, True, 0)
+    w_all, g_all, fwd_got = fetch(
+        out_weight, grad_out, fwd_final.reshape(mode_count, chan_width), count, lanes
+    )
     fwd_got = fwd_got.reshape(count, width)
     fwd_entry = entry(place - 1 - source, fwd_got) * one_step
     long_out = over_modes(scaled_shrink * (fwd_sums + fwd_entry)) + skip_gain[None, :] * gated

time: 145 us -> 130 us (0.90)
  Pallas kernels: 82.4 us -> 70.6 us
  matrix products: 20.3 us -> 16.8 us
  other arithmetic: 16.9 us -> 14.4 us
  starting transfers between devices: 10.3 us -> 12.5 us
    pallas_call x2 -> x1, Pallas kernels: 29 us -> 14.7 us  [exchange(): pl.pallas_call(functools.partial(exchange_kernel, count, later), out_shap...]
    dot_general x1, matrix products: 7.25 us -> 3.77 us  [per_device(): jnp.einsum('tr,jrc->jtc', mixer, w_all, preferred_element_type=jnp.float32)]
    pallas_call x1, Pallas kernels: 53.3 us -> 55.9 us  [fetch(): pl.pallas_call(functools.partial(fetch_kernel, count, lanes), out_shape=(...]
    all_to_all x1, starting transfers between devices: 3.9 us -> 6.15 us  [per_device(): received = lax.all_to_all(parts, 'ch', 0, 0, tiled=True)]
    exp x1, other arithmetic: 2.55 us -> 0.83 us  [per_device(): shrink = jnp.exp(-rate * offsets)]
    unnamed x57 -> x59, local copies, waits for them, and re-layouts: 6.29 us -> 7.19 us
  transfers between devices with their start and end apart: 3 -> 3, of which waited for: 1 -> 1; matrix products, arithmetic and copies ran while one was open for 16% -> 16% of each run, Pallas kernels for 48% -> 11%
where the time goes in v11:
time: 130 us; the launch traced here: 128 us
  Pallas kernels  70.6 us (54%)
  matrix products  16.8 us (13%)
  other arithmetic  14.4 us (11%)
  starting transfers between devices  12.5 us (10%)
  local copies, waits for them, and re-layouts  10.1 us (8%)
  waiting for transfers between devices  2.72 us (2%)
    pallas_call x1, Pallas kernels, fetch(): pl.pallas_call(functools.partial(fetch_kernel, count, lanes), out_shape=(...  55.9 us
    pallas_call x1, Pallas kernels, exchange(): pl.pallas_call(functools.partial(exchange_kernel, count, later), out_shap...  14.7 us
    unnamed x59, local copies, waits for them, and re-layouts  7.19 us
    dot_general x1, matrix products, per_device(): jnp.einsum('jtc,jrc->tr', g_all, w_all, preferred_element_type=jnp.float32)  6.75 us
    ppermute x2, starting transfers between devices, from_behind(): return lax.ppermute(block, axis, route)  6.4 us
    dot_general x2, matrix products, prefix(): jnp.dot(tri, spread, precision=highest, preferred_element_type=jnp.float32)  6.26 us
    all_to_all x1, starting transfers between devices, per_device(): received = lax.all_to_all(parts, 'ch', 0, 0, tiled=True)  6.15 us
    dot_general x1, matrix products, per_device(): jnp.einsum('tr,jrc->jtc', mixer, w_all, preferred_element_type=jnp.float32)  3.77 us
  transfers between devices with their start and end apart: 3, of which 1 were waited for; matrix products, arithmetic and copies ran while one was open for 16% of the time, Pallas kernels for 11%

profile of v11, /device:TPU:65, one launch (start us, length us, event | category | flops | bytes accessed | tf_op | source)
XLA Modules:
  0.0 128.4 jit_solution(9463528331046115962)
XLA Ops:
  0.7 0.8 pad_maximum_fusion.2
  1.5 4.1 %collective-permute-start = (bf16[3,2,512]{2,1,0:T(2,128)(2,1)S(1)}, bf16[3,2,512]{2,1,0:T(2,128)(2,1)S(1)}, u32[]{:S(2)}, u32[]{:S(2)}) collective-permute-start(bf16[3,2,512]{2,1,0:T(2,128)(2,1)S(1)} %pad_maximum_fusion.2), channel_id=1, source_target_pairs={{0,16},{16,32},{32,48},{48,64},{64,80},{80,96},{96,112},{112,128},... | collective-permute-start | bytes 18440 | tf_op jit(solution)/shard_map/ppermute | solution.py:76
  6.1 0.7 slice_bitcast_fusion.8
  6.9 0.8 copy.17
  7.7 0.8 multiply_bitcast_fusion.3
  8.5 0.8 multiply_exponential_fusion.2
  10.7 3.1 %fusion.2 = f32[128,8192]{1,0:T(8,128)S(1)} fusion(f32[128,8192]{1,0:T(8,128)S(1)} %constant_dynamic-update-slice_fusion, f32[8192]{0:T(1024)S(1)} %bitcast.67, f32[128]{0:T(128)S(1)} %iota_convert_fusion), kind=kOutput, calls=%fused_computation.4 | convolution fusion | flops 1612726272 | bytes 8421888 | tf_op jit(solution)/shard_map/dot_general | solution.py:311
  13.9 2.0 %copy-done.1 = f32[128,8192]{1,0:T(8,128)} copy-done((f32[128,8192]{1,0:T(8,128)}, f32[128,8192]{1,0:T(8,128)S(1)}, u32[]{:S(2)}) %copy-start.1) | copy-done | bytes 4194328
  16.6 55.9 %shard_map.120 = (bf16[16,512,512]{2,1,0:T(8,128)(2,1)}, bf16[16,128,512]{2,1,0:T(8,128)(2,1)}, bf16[16,16,512]{2,1,0:T(8,128)(2,1)}) custom-call(bf16[512,512]{1,0:T(8,128)(2,1)} %w_ref.1, bf16[128,512]{1,0:T(8,128)(2,1)} %g_ref.1, bf16[16,512]{1,0:T(8,128)(2,1)} %convert_element_type.65.f_ref), custom_call_target="tpu_custom_call" | custom-call | tf_op jit(solution)/shard_map/pallas_call | solution.py:245
  72.5 1.1 multiply_reduce_fusion.1
  73.7 3.2 %add_multiply_fusion.1 = f32[128,8192]{1,0:T(8,128)S(1)} fusion(f32[128,8192]{1,0:T(8,128)} %copy-done.1, f32[8192]{0:T(1024)S(1)} %exponential_multiply_fusion.1, f32[8192]{0:T(1024)S(1)} %bitcast.77, f32[128]{0:T(128)S(1)} %iota_convert_fusion, f32[8192]{0:T(1024)S(1)} %neg.24), kind=kLoop, calls=%fused_computation.3 | loop fusion | flops 4194304 | bytes 8487424 | tf_op jit(solution)/shard_map/mul | solution.py:333
  77.5 0.9 copy-done
  78.4 3.8 %convert_bitcast_fusion = bf16[16,128,512]{1,2,0:T(8,128)(2,1)} fusion(bf16[16,512,512]{2,1,0:T(8,128)(2,1)S(1)} %copy-done, f32[128,512]{1,0:T(8,128)S(1)} %fusion.14, f32[3,128,512]{2,1,0:T(8,128)S(1)} %fusion.11), kind=kOutput, calls=%fused_computation.8 | convolution fusion | flops 1074921472 | bytes 11010048 | tf_op jit(solution)/shard_map/tr,jrc->jtc/dot_general | solution.py:335
  82.1 6.1 %all-to-all-start = ((bf16[16,128,512]{1,2,0:T(8,128)(2,1)}), bf16[16,128,512]{1,2,0:T(8,128)(2,1)S(1)}, u32[]{:S(2)}, u32[]{:S(2)}) async-start(bf16[16,128,512]{1,2,0:T(8,128)(2,1)} %convert_bitcast_fusion), calls=%async_computation | async-start | bytes 4194304 | tf_op jit(solution)/shard_map/all_to_all | solution.py:338
  88.3 6.7 %constant_dynamic-update-slice_fusion.31 = (f32[128,8192]{1,0:T(8,128)S(1)}, f32[128,512]{1,0:T(8,128)S(1)}, f32[1,128,512]{2,1,0:T(8,128)S(1)}) fusion(f32[3,128,512]{2,1,0:T(8,128)S(1)} %fusion.11, f32[128,512]{1,0:T(8,128)} %copy-done.3, bf16[16,128,512]{2,1,0:T(8,128)(2,1)} %get-tuple-element.14, bf16[16,512,512]{2,1,0:T(8,128)(2,1)} %get-tuple-element.15), kind=kOutput, calls=%fused_computation.105 | convolution fusion | flops 1073872896 | bytes 11796480 | tf_op jit(solution)/shard_map/jtc,jrc->tr/dot_general | solution.py:341
  95.7 3.1 %fusion = f32[128,8192]{1,0:T(8,128)S(1)} fusion(f32[128,8192]{1,0:T(8,128)S(1)} %constant_dynamic-update-slice_fusion.16, f32[128]{0:T(128)S(1)} %copy-done.10, f32[8192]{0:T(1024)S(1)} %neg.24), kind=kOutput, calls=%fused_computation.1 | convolution fusion | flops 1612726272 | bytes 8421888 | tf_op jit(solution)/shard_map/dot_general | solution.py:311
  98.9 1.9 %copy-done.2 = f32[128,8192]{1,0:T(8,128)} copy-done((f32[128,8192]{1,0:T(8,128)}, f32[128,8192]{1,0:T(8,128)S(1)}, u32[]{:S(2)}) %copy-start.2) | copy-done | bytes 4194328
  101.5 14.7 %shard_map.121 = bf16[16,16,512]{2,1,0:T(8,128)(2,1)} custom-call(bf16[16,512]{1,0:T(8,128)(2,1)} %convert_element_type.72.final_ref), custom_call_target="tpu_custom_call" | custom-call | tf_op jit(solution)/shard_map/pallas_call | solution.py:60
  116.2 1.2 multiply_reduce_fusion
  117.4 3.1 %add_multiply_fusion = f32[128,8192]{1,0:T(8,128)S(1)} fusion(f32[128,8192]{1,0:T(8,128)} %copy-done.2, f32[8192]{0:T(1024)S(1)} %exponential_multiply_fusion, f32[8192]{0:T(1024)S(1)} %bitcast.78, f32[8192]{0:T(1024)S(1)} %bitcast.70, f32[128]{0:T(128)} %copy-done.9), kind=kLoop, calls=%fused_computation | loop fusion | flops 4194304 | bytes 8487424 | tf_op jit(solution)/shard_map/mul | solution.py:350
  121.2 2.3 %collective-permute-start.1 = (f32[3,2,512]{2,1,0:T(2,128)S(1)}, f32[3,2,512]{2,1,0:T(2,128)S(1)}, u32[]{:S(2)}, u32[]{:S(2)}) collective-permute-start(f32[3,2,512]{2,1,0:T(2,128)S(1)} %slice.249), channel_id=1, source_target_pairs={{16,0},{32,16},{48,32},{64,48},{80,64},{96,80},{112,96},{128,112},... | collective-permute-start | bytes 36872 | tf_op jit(solution)/shard_map/ppermute | solution.py:76
  123.5 2.7 %collective-permute-done.1 = f32[3,2,512]{2,1,0:T(2,128)S(1)} collective-permute-done((f32[3,2,512]{2,1,0:T(2,128)S(1)}, f32[3,2,512]{2,1,0:T(2,128)S(1)}, u32[]{:S(2)}, u32[]{:S(2)}) %collective-permute-start.1) | collective-permute-done | bytes 12320 | tf_op jit(solution)/shard_map/ppermute | solution.py:76
  126.6 0.8 slice_bitcast_fusion.3
  127.6 0.8 copy.15
  (81 shorter events, 5.7 us)
Async XLA Ops:
  0.6 9.2 %copy-start.4 = (bf16[128,512]{1,0:T(8,128)(2,1)S(1)}, bf16[128,512]{1,0:T(8,128)(2,1)}, u32[]{:S(2)}) copy-start(bf16[128,512]{1,0:T(8,128)(2,1)} %param.11) | copy-start | bytes 393220
  0.6 9.2 %copy-start.5 = (bf16[128,512]{1,0:T(8,128)(2,1)S(1)}, bf16[128,512]{1,0:T(8,128)(2,1)}, u32[]{:S(2)}) copy-start(bf16[128,512]{1,0:T(8,128)(2,1)} %param.10) | copy-start | bytes 393220
  0.7 9.2 %copy-start.6 = (bf16[128,512]{1,0:T(8,128)(2,1)S(1)}, bf16[128,512]{1,0:T(8,128)(2,1)}, u32[]{:S(2)}) copy-start(bf16[128,512]{1,0:T(8,128)(2,1)} %param.9) | copy-start | bytes 393220
  1.5 8.4 %collective-permute-start = (bf16[3,2,512]{2,1,0:T(2,128)(2,1)S(1)}, bf16[3,2,512]{2,1,0:T(2,128)(2,1)S(1)}, u32[]{:S(2)}, u32[]{:S(2)}) collective-permute-start(bf16[3,2,512]{2,1,0:T(2,128)(2,1)S(1)} %pad_maximum_fusion.2), channel_id=1, source_target_pairs={{0,16},{16,32},{32,48},{48,64},{64,80},{80,96},{96,112},{112,128},... | collective-permute-start | bytes 18440 | tf_op jit(solution)/shard_map/ppermute | solution.py:76
  5.6 68.1 %copy-start.9 = (f32[128]{0:T(128)}, f32[128]{0:T(128)S(1)}, u32[]{:S(2)}) copy-start(f32[128]{0:T(128)S(1)} %iota_convert_fusion) | copy-start | bytes 1540
  6.9 3.4 %copy-start.7 = (f32[3,512]{1,0:T(4,128)}, f32[3,512]{1,0:T(4,128)S(1)}, u32[]{:S(2)}) copy-start(f32[3,512]{1,0:T(4,128)S(1)} %get-tuple-element.34) | copy-start | bytes 18436
  13.9 2.0 %copy-start.1 = (f32[128,8192]{1,0:T(8,128)}, f32[128,8192]{1,0:T(8,128)S(1)}, u32[]{:S(2)}) copy-start(f32[128,8192]{1,0:T(8,128)S(1)} %fusion.2) | copy-start | bytes 12582916
  73.7 3.2 %copy-start.11 = (f32[512]{0:T(512)S(1)}, f32[512]{0:T(512)}, u32[]{:S(2)}) copy-start(f32[512]{0:T(512)} %param.15) | copy-start | bytes 6148
  73.7 4.6 %copy-start = (bf16[16,512,512]{2,1,0:T(8,128)(2,1)S(1)}, bf16[16,512,512]{2,1,0:T(8,128)(2,1)}, u32[]{:S(2)}) copy-start(bf16[16,512,512]{2,1,0:T(8,128)(2,1)} %get-tuple-element.15) | copy-start | bytes 25165828
  77.5 4.7 %copy-start.3 = (f32[128,512]{1,0:T(8,128)}, f32[128,512]{1,0:T(8,128)S(1)}, u32[]{:S(2)}) copy-start(f32[128,512]{1,0:T(8,128)S(1)} %fusion.14) | copy-start | bytes 786436
  82.1 45.2 %all-to-all-start = ((bf16[16,128,512]{1,2,0:T(8,128)(2,1)}), bf16[16,128,512]{1,2,0:T(8,128)(2,1)S(1)}, u32[]{:S(2)}, u32[]{:S(2)}) async-start(bf16[16,128,512]{1,2,0:T(8,128)(2,1)} %convert_bitcast_fusion), calls=%async_computation | async-start | bytes 4194304 | tf_op jit(solution)/shard_map/all_to_all | solution.py:338
  95.1 0.7 copy-start.10
  98.9 1.9 %copy-start.2 = (f32[128,8192]{1,0:T(8,128)}, f32[128,8192]{1,0:T(8,128)S(1)}, u32[]{:S(2)}) copy-start(f32[128,8192]{1,0:T(8,128)S(1)} %fusion) | copy-start | bytes 12582916
  117.4 3.1 %copy-start.12 = (f32[512]{0:T(512)S(1)}, f32[512]{0:T(512)}, u32[]{:S(2)}) copy-start(f32[512]{0:T(512)} %param.15) | copy-start | bytes 6148
  120.5 5.8 %copy-start.8 = (f32[3,512]{1,0:T(4,128)S(1)}, f32[3,512]{1,0:T(4,128)}, u32[]{:S(2)}) copy-start(f32[3,512]{1,0:T(4,128)} %copy-done.7) | copy-start | bytes 18436
  121.2 5.0 %collective-permute-start.1 = (f32[3,2,512]{2,1,0:T(2,128)S(1)}, f32[3,2,512]{2,1,0:T(2,128)S(1)}, u32[]{:S(2)}, u32[]{:S(2)}) collective-permute-start(f32[3,2,512]{2,1,0:T(2,128)S(1)} %slice.249), channel_id=1, source_target_pairs={{16,0},{32,16},{48,32},{64,48},{80,64},{96,80},{112,96},{128,112},... | collective-permute-start | bytes 36872 | tf_op jit(solution)/shard_map/ppermute | solution.py:76

commit v12 on v11

--- a/solution.py
+++ b/solution.py
@@ -239,7 +239,7 @@
     own_g.wait()
 
 
-def fetch(out_weight, grad_out, final, count, lanes, pieces=4):
+def fetch(out_weight, grad_out, final, count, lanes, pieces=8):
     half = count // 2
     sends = (half + half // 2 + (half - 1 - half // 2)) * pieces
     return pl.pallas_call(

time: 130 us -> 131 us (level)
  no operation moved by 1% of the time
where the time goes in v12:
time: 131 us; the launch traced here: 129 us
  Pallas kernels  71.2 us (54%)
  matrix products  16.8 us (13%)
  other arithmetic  14.4 us (11%)
  starting transfers between devices  12.9 us (10%)
  local copies, waits for them, and re-layouts  10.1 us (8%)
  waiting for transfers between devices  2.72 us (2%)
    pallas_call x1, Pallas kernels, fetch(): pl.pallas_call(functools.partial(fetch_kernel, count, lanes), out_shape=(...  56.5 us
    pallas_call x1, Pallas kernels, exchange(): pl.pallas_call(functools.partial(exchange_kernel, count, later), out_shap...  14.7 us
    unnamed x59, local copies, waits for them, and re-layouts  7.19 us
    dot_general x1, matrix products, per_device(): jnp.einsum('jtc,jrc->tr', g_all, w_all, preferred_element_type=jnp.float32)  6.76 us
    all_to_all x1, starting transfers between devices, per_device(): received = lax.all_to_all(parts, 'ch', 0, 0, tiled=True)  6.53 us
    ppermute x2, starting transfers between devices, from_behind(): return lax.ppermute(block, axis, route)  6.4 us
    dot_general x2, matrix products, prefix(): jnp.dot(tri, spread, precision=highest, preferred_element_type=jnp.float32)  6.26 us
    dot_general x1, matrix products, per_device(): jnp.einsum('tr,jrc->jtc', mixer, w_all, preferred_element_type=jnp.float32)  3.77 us
  transfers between devices with their start and end apart: 3, of which 1 were waited for; matrix products, arithmetic and copies ran while one was open for 16% of the time, Pallas kernels for 11%

profile of v12, /device:TPU:65, one launch (start us, length us, event | category | flops | bytes accessed | tf_op | source)
XLA Modules:
  0.0 129.4 jit_solution(3553119186728448255)
XLA Ops:
  0.7 0.8 pad_maximum_fusion.2
  1.5 4.1 %collective-permute-start = (bf16[3,2,512]{2,1,0:T(2,128)(2,1)S(1)}, bf16[3,2,512]{2,1,0:T(2,128)(2,1)S(1)}, u32[]{:S(2)}, u32[]{:S(2)}) collective-permute-start(bf16[3,2,512]{2,1,0:T(2,128)(2,1)S(1)} %pad_maximum_fusion.2), channel_id=1, source_target_pairs={{0,16},{16,32},{32,48},{48,64},{64,80},{80,96},{96,112},{112,128},... | collective-permute-start | bytes 18440 | tf_op jit(solution)/shard_map/ppermute | solution.py:76
  6.1 0.7 slice_bitcast_fusion.8
  6.9 0.8 copy.17
  7.7 0.8 multiply_bitcast_fusion.3
  8.5 0.8 multiply_exponential_fusion.2
  10.7 3.1 %fusion.2 = f32[128,8192]{1,0:T(8,128)S(1)} fusion(f32[128,8192]{1,0:T(8,128)S(1)} %constant_dynamic-update-slice_fusion, f32[8192]{0:T(1024)S(1)} %bitcast.67, f32[128]{0:T(128)S(1)} %iota_convert_fusion), kind=kOutput, calls=%fused_computation.4 | convolution fusion | flops 1612726272 | bytes 8421888 | tf_op jit(solution)/shard_map/dot_general | solution.py:311
  13.9 2.0 %copy-done.1 = f32[128,8192]{1,0:T(8,128)} copy-done((f32[128,8192]{1,0:T(8,128)}, f32[128,8192]{1,0:T(8,128)S(1)}, u32[]{:S(2)}) %copy-start.1) | copy-done | bytes 4194328
  16.6 56.5 %shard_map.120 = (bf16[16,512,512]{2,1,0:T(8,128)(2,1)}, bf16[16,128,512]{2,1,0:T(8,128)(2,1)}, bf16[16,16,512]{2,1,0:T(8,128)(2,1)}) custom-call(bf16[512,512]{1,0:T(8,128)(2,1)} %w_ref.1, bf16[128,512]{1,0:T(8,128)(2,1)} %g_ref.1, bf16[16,512]{1,0:T(8,128)(2,1)} %convert_element_type.65.f_ref), custom_call_target="tpu_custom_call" | custom-call | tf_op jit(solution)/shard_map/pallas_call | solution.py:245
  73.1 1.1 multiply_reduce_fusion.1
  74.3 3.2 %add_multiply_fusion.1 = f32[128,8192]{1,0:T(8,128)S(1)} fusion(f32[128,8192]{1,0:T(8,128)} %copy-done.1, f32[8192]{0:T(1024)S(1)} %exponential_multiply_fusion.1, f32[8192]{0:T(1024)S(1)} %bitcast.77, f32[128]{0:T(128)S(1)} %iota_convert_fusion, f32[8192]{0:T(1024)S(1)} %neg.24), kind=kLoop, calls=%fused_computation.3 | loop fusion | flops 4194304 | bytes 8487424 | tf_op jit(solution)/shard_map/mul | solution.py:333
  78.1 0.9 copy-done
  78.9 3.8 %convert_bitcast_fusion = bf16[16,128,512]{1,2,0:T(8,128)(2,1)} fusion(bf16[16,512,512]{2,1,0:T(8,128)(2,1)S(1)} %copy-done, f32[128,512]{1,0:T(8,128)S(1)} %fusion.14, f32[3,128,512]{2,1,0:T(8,128)S(1)} %fusion.11), kind=kOutput, calls=%fused_computation.8 | convolution fusion | flops 1074921472 | bytes 11010048 | tf_op jit(solution)/shard_map/tr,jrc->jtc/dot_general | solution.py:335
  82.7 6.5 %all-to-all-start = ((bf16[16,128,512]{1,2,0:T(8,128)(2,1)}), bf16[16,128,512]{1,2,0:T(8,128)(2,1)S(1)}, u32[]{:S(2)}, u32[]{:S(2)}) async-start(bf16[16,128,512]{1,2,0:T(8,128)(2,1)} %convert_bitcast_fusion), calls=%async_computation | async-start | bytes 4194304 | tf_op jit(solution)/shard_map/all_to_all | solution.py:338
  89.3 6.8 %constant_dynamic-update-slice_fusion.31 = (f32[128,8192]{1,0:T(8,128)S(1)}, f32[128,512]{1,0:T(8,128)S(1)}, f32[1,128,512]{2,1,0:T(8,128)S(1)}) fusion(f32[3,128,512]{2,1,0:T(8,128)S(1)} %fusion.11, f32[128,512]{1,0:T(8,128)} %copy-done.3, bf16[16,128,512]{2,1,0:T(8,128)(2,1)} %get-tuple-element.14, bf16[16,512,512]{2,1,0:T(8,128)(2,1)} %get-tuple-element.15), kind=kOutput, calls=%fused_computation.105 | convolution fusion | flops 1073872896 | bytes 11796480 | tf_op jit(solution)/shard_map/jtc,jrc->tr/dot_general | solution.py:341
  96.7 3.1 %fusion = f32[128,8192]{1,0:T(8,128)S(1)} fusion(f32[128,8192]{1,0:T(8,128)S(1)} %constant_dynamic-update-slice_fusion.16, f32[128]{0:T(128)S(1)} %copy-done.10, f32[8192]{0:T(1024)S(1)} %neg.24), kind=kOutput, calls=%fused_computation.1 | convolution fusion | flops 1612726272 | bytes 8421888 | tf_op jit(solution)/shard_map/dot_general | solution.py:311
  99.8 1.9 %copy-done.2 = f32[128,8192]{1,0:T(8,128)} copy-done((f32[128,8192]{1,0:T(8,128)}, f32[128,8192]{1,0:T(8,128)S(1)}, u32[]{:S(2)}) %copy-start.2) | copy-done | bytes 4194328
  102.5 14.7 %shard_map.121 = bf16[16,16,512]{2,1,0:T(8,128)(2,1)} custom-call(bf16[16,512]{1,0:T(8,128)(2,1)} %convert_element_type.72.final_ref), custom_call_target="tpu_custom_call" | custom-call | tf_op jit(solution)/shard_map/pallas_call | solution.py:60
  117.2 1.2 multiply_reduce_fusion
  118.4 3.1 %add_multiply_fusion = f32[128,8192]{1,0:T(8,128)S(1)} fusion(f32[128,8192]{1,0:T(8,128)} %copy-done.2, f32[8192]{0:T(1024)S(1)} %exponential_multiply_fusion, f32[8192]{0:T(1024)S(1)} %bitcast.78, f32[8192]{0:T(1024)S(1)} %bitcast.70, f32[128]{0:T(128)} %copy-done.9), kind=kLoop, calls=%fused_computation | loop fusion | flops 4194304 | bytes 8487424 | tf_op jit(solution)/shard_map/mul | solution.py:350
  122.2 2.3 %collective-permute-start.1 = (f32[3,2,512]{2,1,0:T(2,128)S(1)}, f32[3,2,512]{2,1,0:T(2,128)S(1)}, u32[]{:S(2)}, u32[]{:S(2)}) collective-permute-start(f32[3,2,512]{2,1,0:T(2,128)S(1)} %slice.249), channel_id=1, source_target_pairs={{16,0},{32,16},{48,32},{64,48},{80,64},{96,80},{112,96},{128,112},... | collective-permute-start | bytes 36872 | tf_op jit(solution)/shard_map/ppermute | solution.py:76
  124.5 2.7 %collective-permute-done.1 = f32[3,2,512]{2,1,0:T(2,128)S(1)} collective-permute-done((f32[3,2,512]{2,1,0:T(2,128)S(1)}, f32[3,2,512]{2,1,0:T(2,128)S(1)}, u32[]{:S(2)}, u32[]{:S(2)}) %collective-permute-start.1) | collective-permute-done | bytes 12320 | tf_op jit(solution)/shard_map/ppermute | solution.py:76
  127.6 0.8 slice_bitcast_fusion.3
  128.6 0.8 copy.15
  (81 shorter events, 5.7 us)
Async XLA Ops:
  0.6 9.2 %copy-start.4 = (bf16[128,512]{1,0:T(8,128)(2,1)S(1)}, bf16[128,512]{1,0:T(8,128)(2,1)}, u32[]{:S(2)}) copy-start(bf16[128,512]{1,0:T(8,128)(2,1)} %param.11) | copy-start | bytes 393220
  0.6 9.2 %copy-start.5 = (bf16[128,512]{1,0:T(8,128)(2,1)S(1)}, bf16[128,512]{1,0:T(8,128)(2,1)}, u32[]{:S(2)}) copy-start(bf16[128,512]{1,0:T(8,128)(2,1)} %param.10) | copy-start | bytes 393220
  0.7 9.2 %copy-start.6 = (bf16[128,512]{1,0:T(8,128)(2,1)S(1)}, bf16[128,512]{1,0:T(8,128)(2,1)}, u32[]{:S(2)}) copy-start(bf16[128,512]{1,0:T(8,128)(2,1)} %param.9) | copy-start | bytes 393220
  1.5 8.4 %collective-permute-start = (bf16[3,2,512]{2,1,0:T(2,128)(2,1)S(1)}, bf16[3,2,512]{2,1,0:T(2,128)(2,1)S(1)}, u32[]{:S(2)}, u32[]{:S(2)}) collective-permute-start(bf16[3,2,512]{2,1,0:T(2,128)(2,1)S(1)} %pad_maximum_fusion.2), channel_id=1, source_target_pairs={{0,16},{16,32},{32,48},{48,64},{64,80},{80,96},{96,112},{112,128},... | collective-permute-start | bytes 18440 | tf_op jit(solution)/shard_map/ppermute | solution.py:76
  5.6 68.7 %copy-start.9 = (f32[128]{0:T(128)}, f32[128]{0:T(128)S(1)}, u32[]{:S(2)}) copy-start(f32[128]{0:T(128)S(1)} %iota_convert_fusion) | copy-start | bytes 1540
  6.9 3.4 %copy-start.7 = (f32[3,512]{1,0:T(4,128)}, f32[3,512]{1,0:T(4,128)S(1)}, u32[]{:S(2)}) copy-start(f32[3,512]{1,0:T(4,128)S(1)} %get-tuple-element.34) | copy-start | bytes 18436
  13.9 2.0 %copy-start.1 = (f32[128,8192]{1,0:T(8,128)}, f32[128,8192]{1,0:T(8,128)S(1)}, u32[]{:S(2)}) copy-start(f32[128,8192]{1,0:T(8,128)S(1)} %fusion.2) | copy-start | bytes 12582916
  74.3 3.2 %copy-start.11 = (f32[512]{0:T(512)S(1)}, f32[512]{0:T(512)}, u32[]{:S(2)}) copy-start(f32[512]{0:T(512)} %param.15) | copy-start | bytes 6148
  74.3 4.6 %copy-start = (bf16[16,512,512]{2,1,0:T(8,128)(2,1)S(1)}, bf16[16,512,512]{2,1,0:T(8,128)(2,1)}, u32[]{:S(2)}) copy-start(bf16[16,512,512]{2,1,0:T(8,128)(2,1)} %get-tuple-element.15) | copy-start | bytes 25165828
  78.1 4.7 %copy-start.3 = (f32[128,512]{1,0:T(8,128)}, f32[128,512]{1,0:T(8,128)S(1)}, u32[]{:S(2)}) copy-start(f32[128,512]{1,0:T(8,128)S(1)} %fusion.14) | copy-start | bytes 786436
  82.7 45.6 %all-to-all-start = ((bf16[16,128,512]{1,2,0:T(8,128)(2,1)}), bf16[16,128,512]{1,2,0:T(8,128)(2,1)S(1)}, u32[]{:S(2)}, u32[]{:S(2)}) async-start(bf16[16,128,512]{1,2,0:T(8,128)(2,1)} %convert_bitcast_fusion), calls=%async_computation | async-start | bytes 4194304 | tf_op jit(solution)/shard_map/all_to_all | solution.py:338
  96.0 0.7 copy-start.10
  99.8 1.9 %copy-start.2 = (f32[128,8192]{1,0:T(8,128)}, f32[128,8192]{1,0:T(8,128)S(1)}, u32[]{:S(2)}) copy-start(f32[128,8192]{1,0:T(8,128)S(1)} %fusion) | copy-start | bytes 12582916
  118.4 3.1 %copy-start.12 = (f32[512]{0:T(512)S(1)}, f32[512]{0:T(512)}, u32[]{:S(2)}) copy-start(f32[512]{0:T(512)} %param.15) | copy-start | bytes 6148
  121.5 5.8 %copy-start.8 = (f32[3,512]{1,0:T(4,128)S(1)}, f32[3,512]{1,0:T(4,128)}, u32[]{:S(2)}) copy-start(f32[3,512]{1,0:T(4,128)} %copy-done.7) | copy-start | bytes 18436
  122.2 5.0 %collective-permute-start.1 = (f32[3,2,512]{2,1,0:T(2,128)S(1)}, f32[3,2,512]{2,1,0:T(2,128)S(1)}, u32[]{:S(2)}, u32[]{:S(2)}) collective-permute-start(f32[3,2,512]{2,1,0:T(2,128)S(1)} %slice.249), channel_id=1, source_target_pairs={{16,0},{32,16},{48,32},{64,48},{80,64},{96,80},{112,96},{128,112},... | collective-permute-start | bytes 36872 | tf_op jit(solution)/shard_map/ppermute | solution.py:76

commit v13 on v11

--- a/solution.py
+++ b/solution.py
@@ -323,12 +323,13 @@
         held = jnp.where((gap >= 0)[:, None], got.astype(jnp.float32), 0.0)
         return jnp.sum(jnp.exp(-rate * span) * held, axis=0, keepdims=True)
 
-    fwd_sums = prefix(lower, grow, gated)
-    fwd_final = (shrink[tok_rows - 1] * fwd_sums[tok_rows - 1]).astype(jnp.bfloat16)
+    spread_gated = jnp.concatenate([gated] * mode_count, axis=1)
+    fwd_final = jnp.sum(shrink[::-1] * spread_gated, axis=0).astype(jnp.bfloat16)
     w_all, g_all, fwd_got = fetch(
         out_weight, grad_out, fwd_final.reshape(mode_count, chan_width), count, lanes
     )
     fwd_got = fwd_got.reshape(count, width)
+    fwd_sums = prefix(lower, grow, gated)
     fwd_entry = entry(place - 1 - source, fwd_got) * one_step
     long_out = over_modes(scaled_shrink * (fwd_sums + fwd_entry)) + skip_gain[None, :] * gated
     mixer = (q_short * long_out).astype(jnp.bfloat16)

time: 130 us -> 184 us (1.42)
  local copies, waits for them, and re-layouts: 10.1 us -> 43 us
  waiting for transfers between devices: 2.72 us -> 24.6 us
    rev x0 -> x1, local copies, waits for them, and re-layouts: none -> 32.8 us  [per_device(): shrink[::-1] * spread_gated]
    all_to_all x1, waiting for transfers between devices: 0.01 us -> 21.9 us  [per_device(): received = lax.all_to_all(parts, 'ch', 0, 0, tiled=True)]
    dot_general x1, matrix products: 6.75 us -> 2.77 us  [per_device(): jnp.einsum('jtc,jrc->tr', g_all, w_all, preferred_element_type=jnp.float32)]
    dot_general x2, matrix products: 6.26 us -> 9.53 us  [prefix(): jnp.dot(tri, spread, precision=highest, preferred_element_type=jnp.float32)]
    mul x1 -> x0, other arithmetic: 3.21 us -> none  [per_device(): scaled_shrink * (fwd_sums + fwd_entry)]
    unnamed x59 -> x53, local copies, waits for them, and re-layouts: 7.19 us -> 7.36 us
  transfers between devices with their start and end apart: 3 -> 3, of which waited for: 1 -> 2; matrix products, arithmetic and copies ran while one was open for 16% -> 24% of each run, Pallas kernels for 11% -> 0%
where the time goes in v13:
time: 184 us; the launch traced here: 181 us
  Pallas kernels  70.8 us (38%)
  local copies, waits for them, and re-layouts  43 us (23%)
  waiting for transfers between devices  24.6 us (13%)
  matrix products  16 us (9%)
  other arithmetic  12.6 us (7%)
  starting transfers between devices  12.4 us (7%)
    pallas_call x1, Pallas kernels, fetch(): pl.pallas_call(functools.partial(fetch_kernel, count, lanes), out_shape=(...  55.9 us
    rev x1, local copies, waits for them, and re-layouts, per_device(): shrink[::-1] * spread_gated  32.8 us
    all_to_all x1, waiting for transfers between devices, per_device(): received = lax.all_to_all(parts, 'ch', 0, 0, tiled=True)  21.9 us
    pallas_call x1, Pallas kernels, exchange(): pl.pallas_call(functools.partial(exchange_kernel, count, later), out_shap...  14.9 us
    dot_general x2, matrix products, prefix(): jnp.dot(tri, spread, precision=highest, preferred_element_type=jnp.float32)  9.53 us
    unnamed x53, local copies, waits for them, and re-layouts  7.36 us
    ppermute x2, starting transfers between devices, from_behind(): return lax.ppermute(block, axis, route)  6.68 us
    all_to_all x1, starting transfers between devices, per_device(): received = lax.all_to_all(parts, 'ch', 0, 0, tiled=True)  5.76 us
  transfers between devices with their start and end apart: 3, of which 2 were waited for; matrix products, arithmetic and copies ran while one was open for 24% of the time, Pallas kernels for 0%

profile of v13, /device:TPU:65, one launch (start us, length us, event | category | flops | bytes accessed | tf_op | source)
XLA Modules:
  0.0 180.6 jit_solution(13148657798534173750)
XLA Ops:
  0.6 0.7 pad_maximum_fusion.2
  1.4 4.1 %collective-permute-start = (bf16[3,2,512]{2,1,0:T(2,128)(2,1)S(1)}, bf16[3,2,512]{2,1,0:T(2,128)(2,1)S(1)}, u32[]{:S(2)}, u32[]{:S(2)}) collective-permute-start(bf16[3,2,512]{2,1,0:T(2,128)(2,1)S(1)} %pad_maximum_fusion.2), channel_id=1, source_target_pairs={{0,16},{16,32},{32,48},{48,64},{64,80},{80,96},{96,112},{112,128},... | collective-permute-start | bytes 18440 | tf_op jit(solution)/shard_map/ppermute | solution.py:76
  6.3 0.8 copy.17
  7.1 0.8 multiply_bitcast_fusion.3
  7.9 2.6 %multiply_exponential_fusion.2 = f32[128,8192]{1,0:T(8,128)} fusion(f32[128]{0:T(128)S(1)} %iota_convert_fusion, f32[8192]{0:T(1024)S(1)} %neg.24), kind=kLoop, calls=%fused_computation.8 | loop fusion | flops 1048576 | bytes 4227584 | tf_op jit(solution)/shard_map/exp | solution.py:299
  10.5 32.8 %rev.3 = f32[128,8192]{1,0:T(8,128)} reverse(f32[128,8192]{1,0:T(8,128)} %multiply_exponential_fusion.2), dimensions={0} | reverse | bytes 8388608 | tf_op jit(solution)/shard_map/rev | solution.py:327
  44.2 2.1 %copy-done.2 = f32[128,8192]{1,0:T(8,128)} copy-done((f32[128,8192]{1,0:T(8,128)}, f32[128,8192]{1,0:T(8,128)S(1)}, u32[]{:S(2)}) %copy-start.2) | copy-done | bytes 4194328
  46.3 1.1 copy-done.1
  48.8 55.9 %shard_map.120 = (bf16[16,512,512]{2,1,0:T(8,128)(2,1)}, bf16[16,128,512]{2,1,0:T(8,128)(2,1)}, bf16[16,16,512]{2,1,0:T(8,128)(2,1)}) custom-call(bf16[512,512]{1,0:T(8,128)(2,1)} %w_ref.1, bf16[128,512]{1,0:T(8,128)(2,1)} %g_ref.1, bf16[16,512]{1,0:T(8,128)(2,1)} %convert_element_type.65.f_ref), custom_call_target="tpu_custom_call" | custom-call | tf_op jit(solution)/shard_map/pallas_call | solution.py:245
  104.7 1.3 multiply_reduce_fusion.2
  106.0 6.2 %fusion = f32[128,8192]{1,0:T(8,128)S(1)} fusion(f32[128,8192]{1,0:T(8,128)} %copy-done.2, f32[8192]{0:T(1024)S(1)} %exponential_multiply_fusion.1, f32[8192]{0:T(1024)S(1)} %bitcast.70, f32[8192]{0:T(1024)S(1)} %bitcast.79, f32[128]{0:T(128)S(1)} %iota_convert_fusion, f32[8192]{0:T(1024)S(1)} %neg.24), kind=kOutput, calls=%fused_computation.1 | convolution fusion | flops 1616920576 | bytes 8520192 | tf_op jit(solution)/shard_map/dot_general | solution.py:311
  112.8 3.7 %convert_bitcast_fusion = bf16[16,128,512]{1,2,0:T(8,128)(2,1)} fusion(bf16[16,512,512]{2,1,0:T(8,128)(2,1)S(1)} %bitcast.67, f32[128,512]{1,0:T(8,128)S(1)} %fusion.14, f32[3,128,512]{2,1,0:T(8,128)S(1)} %fusion.11), kind=kOutput, calls=%fused_computation.9 | convolution fusion | flops 1074921472 | bytes 11010048 | tf_op jit(solution)/shard_map/tr,jrc->jtc/dot_general | solution.py:336
  116.5 2.8 %constant_dynamic-update-slice_fusion.31 = (f32[128,8192]{1,0:T(8,128)S(1)}, f32[128,512]{1,0:T(8,128)S(1)}, f32[1,128,512]{2,1,0:T(8,128)S(1)}) fusion(f32[3,128,512]{2,1,0:T(8,128)S(1)} %fusion.11, f32[128,512]{1,0:T(8,128)S(1)} %fusion.14, bf16[16,128,512]{2,1,0:T(8,128)(2,1)S(1)} %copy-done.3, bf16[16,512,512]{2,1,0:T(8,128)(2,1)S(1)} %bitcast.67), kind=kOutput, calls=%fused_computation.106 | convolution fusion | flops 1073872896 | bytes 11796480 | tf_op jit(solution)/shard_map/jtc,jrc->tr/dot_general | solution.py:342
  119.7 3.4 %fusion.1 = f32[128,8192]{1,0:T(8,128)S(1)} fusion(f32[128,8192]{1,0:T(8,128)S(1)} %constant_dynamic-update-slice_fusion.16, f32[128]{0:T(128)S(1)} %iota_convert_fusion, f32[8192]{0:T(1024)S(1)} %neg.24), kind=kOutput, calls=%fused_computation.3 | convolution fusion | flops 1612726272 | bytes 8421888 | tf_op jit(solution)/shard_map/dot_general | solution.py:311
  123.1 1.9 %copy-done = f32[128,8192]{1,0:T(8,128)} copy-done((f32[128,8192]{1,0:T(8,128)}, f32[128,8192]{1,0:T(8,128)S(1)}, u32[]{:S(2)}) %copy-start) | copy-done | bytes 4194328
  125.7 14.9 %shard_map.121 = bf16[16,16,512]{2,1,0:T(8,128)(2,1)} custom-call(bf16[16,512]{1,0:T(8,128)(2,1)} %convert_element_type.72.final_ref), custom_call_target="tpu_custom_call" | custom-call | tf_op jit(solution)/shard_map/pallas_call | solution.py:60
  140.6 1.1 multiply_reduce_fusion.1
  141.8 5.8 %all-to-all-start = ((bf16[16,128,512]{1,2,0:T(8,128)(2,1)}), bf16[16,128,512]{1,2,0:T(8,128)(2,1)S(1)}, u32[]{:S(2)}, u32[]{:S(2)}) async-start(bf16[16,128,512]{1,2,0:T(8,128)(2,1)} %convert_bitcast_fusion), calls=%async_computation | async-start | bytes 4194304 | tf_op jit(solution)/shard_map/all_to_all | solution.py:339
  147.6 3.1 %add_multiply_fusion = f32[128,8192]{1,0:T(8,128)S(1)} fusion(f32[128,8192]{1,0:T(8,128)} %copy-done, f32[8192]{0:T(1024)S(1)} %exponential_multiply_fusion, f32[8192]{0:T(1024)S(1)} %bitcast.72, f32[8192]{0:T(1024)S(1)} %bitcast.80, f32[128]{0:T(128)S(1)} %iota_convert_fusion), kind=kLoop, calls=%fused_computation.2 | loop fusion | flops 4194304 | bytes 8487424 | tf_op jit(solution)/shard_map/mul | solution.py:351
  151.3 2.6 %collective-permute-start.1 = (f32[3,2,512]{2,1,0:T(2,128)S(1)}, f32[3,2,512]{2,1,0:T(2,128)S(1)}, u32[]{:S(2)}, u32[]{:S(2)}) collective-permute-start(f32[3,2,512]{2,1,0:T(2,128)S(1)} %slice.239), channel_id=1, source_target_pairs={{16,0},{32,16},{48,32},{64,48},{80,64},{96,80},{112,96},{128,112},... | collective-permute-start | bytes 36872 | tf_op jit(solution)/shard_map/ppermute | solution.py:76
  153.9 2.7 %collective-permute-done.1 = f32[3,2,512]{2,1,0:T(2,128)S(1)} collective-permute-done((f32[3,2,512]{2,1,0:T(2,128)S(1)}, f32[3,2,512]{2,1,0:T(2,128)S(1)}, u32[]{:S(2)}, u32[]{:S(2)}) %collective-permute-start.1) | collective-permute-done | bytes 12320 | tf_op jit(solution)/shard_map/ppermute | solution.py:76
  156.9 0.8 slice_bitcast_fusion.3
  157.7 21.9 %all-to-all-done = bf16[16,128,512]{1,2,0:T(8,128)(2,1)S(1)} async-done(((bf16[16,128,512]{1,2,0:T(8,128)(2,1)}), bf16[16,128,512]{1,2,0:T(8,128)(2,1)S(1)}, u32[]{:S(2)}, u32[]{:S(2)}) %all-to-all-start) | async-done | bytes 2097184 | tf_op jit(solution)/shard_map/all_to_all | solution.py:339
  179.9 0.8 copy.15
  (76 shorter events, 5.7 us)
Async XLA Ops:
  1.4 41.9 %collective-permute-start = (bf16[3,2,512]{2,1,0:T(2,128)(2,1)S(1)}, bf16[3,2,512]{2,1,0:T(2,128)(2,1)S(1)}, u32[]{:S(2)}, u32[]{:S(2)}) collective-permute-start(bf16[3,2,512]{2,1,0:T(2,128)(2,1)S(1)} %pad_maximum_fusion.2), channel_id=1, source_target_pairs={{0,16},{16,32},{32,48},{48,64},{64,80},{80,96},{96,112},{112,128},... | collective-permute-start | bytes 18440 | tf_op jit(solution)/shard_map/ppermute | solution.py:76
  10.5 32.8 %copy-start.4 = (bf16[128,512]{1,0:T(8,128)(2,1)S(1)}, bf16[128,512]{1,0:T(8,128)(2,1)}, u32[]{:S(2)}) copy-start(bf16[128,512]{1,0:T(8,128)(2,1)} %param.11) | copy-start | bytes 393220
  10.5 32.8 %copy-start.5 = (bf16[128,512]{1,0:T(8,128)(2,1)S(1)}, bf16[128,512]{1,0:T(8,128)(2,1)}, u32[]{:S(2)}) copy-start(bf16[128,512]{1,0:T(8,128)(2,1)} %param.10) | copy-start | bytes 393220
  10.5 32.8 %copy-start.6 = (bf16[128,512]{1,0:T(8,128)(2,1)S(1)}, bf16[128,512]{1,0:T(8,128)(2,1)}, u32[]{:S(2)}) copy-start(bf16[128,512]{1,0:T(8,128)(2,1)} %param.9) | copy-start | bytes 393220
  43.7 3.7 %copy-start.1 = (f32[128,8192]{1,0:T(8,128)S(1)}, f32[128,8192]{1,0:T(8,128)}, u32[]{:S(2)}) copy-start(f32[128,8192]{1,0:T(8,128)} %rev.3) | copy-start | bytes 12582916
  44.2 2.1 %copy-start.2 = (f32[128,8192]{1,0:T(8,128)}, f32[128,8192]{1,0:T(8,128)S(1)}, u32[]{:S(2)}) copy-start(f32[128,8192]{1,0:T(8,128)S(1)} %constant_dynamic-update-slice_fusion) | copy-start | bytes 12582916
  104.7 8.1 %slice-start = ((s8[8388608]{0:T(1024)(128)(4,1)}), s8[4194304]{0:T(1024)(128)(4,1)S(1)}, s32[]{:S(2)}) async-start(s8[8388608]{0:T(1024)(128)(4,1)} %bitcast.66), calls=%async_computation.1 | async-start | bytes 8388608
  106.0 6.2 %copy-start.7 = (f32[512]{0:T(512)S(1)}, f32[512]{0:T(512)}, u32[]{:S(2)}) copy-start(f32[512]{0:T(512)} %param.15) | copy-start | bytes 6148
  106.0 6.7 %slice-start.1 = ((s8[8388608]{0:T(1024)(128)(4,1)}), s8[4194304]{0:T(1024)(128)(4,1)S(1)}, s32[]{:S(2)}) async-start(s8[8388608]{0:T(1024)(128)(4,1)} %bitcast.66), calls=%async_computation.2 | async-start | bytes 8388608
  112.8 3.7 %copy-start.3 = (bf16[16,128,512]{2,1,0:T(8,128)(2,1)S(1)}, bf16[16,128,512]{2,1,0:T(8,128)(2,1)}, u32[]{:S(2)}) copy-start(bf16[16,128,512]{2,1,0:T(8,128)(2,1)} %get-tuple-element.14) | copy-start | bytes 6291460
  123.1 1.9 %copy-start = (f32[128,8192]{1,0:T(8,128)}, f32[128,8192]{1,0:T(8,128)S(1)}, u32[]{:S(2)}) copy-start(f32[128,8192]{1,0:T(8,128)S(1)} %fusion.1) | copy-start | bytes 12582916
  141.8 37.8 %all-to-all-start = ((bf16[16,128,512]{1,2,0:T(8,128)(2,1)}), bf16[16,128,512]{1,2,0:T(8,128)(2,1)S(1)}, u32[]{:S(2)}, u32[]{:S(2)}) async-start(bf16[16,128,512]{1,2,0:T(8,128)(2,1)} %convert_bitcast_fusion), calls=%async_computation | async-start | bytes 4194304 | tf_op jit(solution)/shard_map/all_to_all | solution.py:339
  151.3 5.3 %collective-permute-start.1 = (f32[3,2,512]{2,1,0:T(2,128)S(1)}, f32[3,2,512]{2,1,0:T(2,128)S(1)}, u32[]{:S(2)}, u32[]{:S(2)}) collective-permute-start(f32[3,2,512]{2,1,0:T(2,128)S(1)} %slice.239), channel_id=1, source_target_pairs={{16,0},{32,16},{48,32},{64,48},{80,64},{96,80},{112,96},{128,112},... | collective-permute-start | bytes 36872 | tf_op jit(solution)/shard_map/ppermute | solution.py:76

commit v14 on v11

--- a/solution.py
+++ b/solution.py
@@ -138,12 +138,6 @@
             device_id_type=MESH,
         )
 
-    for other in range(lanes):
-
-        @pl.when(lane != other)
-        def _():
-            grad_link(other).start()
-
     own_w = pltpu.make_async_copy(w_ref, w_all.at[me], own_sem.at[0])
     own_g = pltpu.make_async_copy(g_ref, g_all.at[lane], own_sem.at[1])
     own_w.start()
@@ -198,6 +192,12 @@
         if left_steps(piece) >= 1:
             send(me, piece, left, True)
         send(me, piece, partner, True)
+    for other in range(lanes):
+
+        @pl.when(lane != other)
+        def _():
+            grad_link(other).start()
+
     for step in range(2, longest + 2):
         for piece in range(pieces):
             if step <= right_steps(piece) + 1:

time: 130 us -> 130 us (level)
  no operation moved by 1% of the time
where the time goes in v14:
time: 130 us; the launch traced here: 128 us
  Pallas kernels  70.6 us (54%)
  matrix products  16.8 us (13%)
  other arithmetic  14.4 us (11%)
  starting transfers between devices  12.5 us (10%)
  local copies, waits for them, and re-layouts  10.1 us (8%)
  waiting for transfers between devices  2.72 us (2%)
    pallas_call x1, Pallas kernels, fetch(): pl.pallas_call(functools.partial(fetch_kernel, count, lanes), out_shape=(...  55.9 us
    pallas_call x1, Pallas kernels, exchange(): pl.pallas_call(functools.partial(exchange_kernel, count, later), out_shap...  14.7 us
    unnamed x59, local copies, waits for them, and re-layouts  7.19 us
    dot_general x1, matrix products, per_device(): jnp.einsum('jtc,jrc->tr', g_all, w_all, preferred_element_type=jnp.float32)  6.75 us
    ppermute x2, starting transfers between devices, from_behind(): return lax.ppermute(block, axis, route)  6.4 us
    dot_general x2, matrix products, prefix(): jnp.dot(tri, spread, precision=highest, preferred_element_type=jnp.float32)  6.26 us
    all_to_all x1, starting transfers between devices, per_device(): received = lax.all_to_all(parts, 'ch', 0, 0, tiled=True)  6.15 us
    dot_general x1, matrix products, per_device(): jnp.einsum('tr,jrc->jtc', mixer, w_all, preferred_element_type=jnp.float32)  3.77 us
  transfers between devices with their start and end apart: 3, of which 1 were waited for; matrix products, arithmetic and copies ran while one was open for 16% of the time, Pallas kernels for 11%

profile of v14, /device:TPU:65, one launch (start us, length us, event | category | flops | bytes accessed | tf_op | source)
XLA Modules:
  0.0 128.4 jit_solution(3541845024226526170)
XLA Ops:
  0.7 0.8 pad_maximum_fusion.2
  1.5 4.1 %collective-permute-start = (bf16[3,2,512]{2,1,0:T(2,128)(2,1)S(1)}, bf16[3,2,512]{2,1,0:T(2,128)(2,1)S(1)}, u32[]{:S(2)}, u32[]{:S(2)}) collective-permute-start(bf16[3,2,512]{2,1,0:T(2,128)(2,1)S(1)} %pad_maximum_fusion.2), channel_id=1, source_target_pairs={{0,16},{16,32},{32,48},{48,64},{64,80},{80,96},{96,112},{112,128},... | collective-permute-start | bytes 18440 | tf_op jit(solution)/shard_map/ppermute | solution.py:76
  6.1 0.7 slice_bitcast_fusion.8
  6.9 0.8 copy.17
  7.7 0.8 multiply_bitcast_fusion.3
  8.5 0.8 multiply_exponential_fusion.2
  10.7 3.1 %fusion.2 = f32[128,8192]{1,0:T(8,128)S(1)} fusion(f32[128,8192]{1,0:T(8,128)S(1)} %constant_dynamic-update-slice_fusion, f32[8192]{0:T(1024)S(1)} %bitcast.67, f32[128]{0:T(128)S(1)} %iota_convert_fusion), kind=kOutput, calls=%fused_computation.4 | convolution fusion | flops 1612726272 | bytes 8421888 | tf_op jit(solution)/shard_map/dot_general | solution.py:311
  13.9 2.0 %copy-done.1 = f32[128,8192]{1,0:T(8,128)} copy-done((f32[128,8192]{1,0:T(8,128)}, f32[128,8192]{1,0:T(8,128)S(1)}, u32[]{:S(2)}) %copy-start.1) | copy-done | bytes 4194328
  16.6 55.9 %shard_map.120 = (bf16[16,512,512]{2,1,0:T(8,128)(2,1)}, bf16[16,128,512]{2,1,0:T(8,128)(2,1)}, bf16[16,16,512]{2,1,0:T(8,128)(2,1)}) custom-call(bf16[512,512]{1,0:T(8,128)(2,1)} %w_ref.1, bf16[128,512]{1,0:T(8,128)(2,1)} %g_ref.1, bf16[16,512]{1,0:T(8,128)(2,1)} %convert_element_type.65.f_ref), custom_call_target="tpu_custom_call" | custom-call | tf_op jit(solution)/shard_map/pallas_call | solution.py:245
  72.5 1.1 multiply_reduce_fusion.1
  73.7 3.2 %add_multiply_fusion.1 = f32[128,8192]{1,0:T(8,128)S(1)} fusion(f32[128,8192]{1,0:T(8,128)} %copy-done.1, f32[8192]{0:T(1024)S(1)} %exponential_multiply_fusion.1, f32[8192]{0:T(1024)S(1)} %bitcast.77, f32[128]{0:T(128)S(1)} %iota_convert_fusion, f32[8192]{0:T(1024)S(1)} %neg.24), kind=kLoop, calls=%fused_computation.3 | loop fusion | flops 4194304 | bytes 8487424 | tf_op jit(solution)/shard_map/mul | solution.py:333
  77.5 0.9 copy-done
  78.4 3.8 %convert_bitcast_fusion = bf16[16,128,512]{1,2,0:T(8,128)(2,1)} fusion(bf16[16,512,512]{2,1,0:T(8,128)(2,1)S(1)} %copy-done, f32[128,512]{1,0:T(8,128)S(1)} %fusion.14, f32[3,128,512]{2,1,0:T(8,128)S(1)} %fusion.11), kind=kOutput, calls=%fused_computation.8 | convolution fusion | flops 1074921472 | bytes 11010048 | tf_op jit(solution)/shard_map/tr,jrc->jtc/dot_general | solution.py:335
  82.1 6.1 %all-to-all-start = ((bf16[16,128,512]{1,2,0:T(8,128)(2,1)}), bf16[16,128,512]{1,2,0:T(8,128)(2,1)S(1)}, u32[]{:S(2)}, u32[]{:S(2)}) async-start(bf16[16,128,512]{1,2,0:T(8,128)(2,1)} %convert_bitcast_fusion), calls=%async_computation | async-start | bytes 4194304 | tf_op jit(solution)/shard_map/all_to_all | solution.py:338
  88.3 6.7 %constant_dynamic-update-slice_fusion.31 = (f32[128,8192]{1,0:T(8,128)S(1)}, f32[128,512]{1,0:T(8,128)S(1)}, f32[1,128,512]{2,1,0:T(8,128)S(1)}) fusion(f32[3,128,512]{2,1,0:T(8,128)S(1)} %fusion.11, f32[128,512]{1,0:T(8,128)} %copy-done.3, bf16[16,128,512]{2,1,0:T(8,128)(2,1)} %get-tuple-element.14, bf16[16,512,512]{2,1,0:T(8,128)(2,1)} %get-tuple-element.15), kind=kOutput, calls=%fused_computation.105 | convolution fusion | flops 1073872896 | bytes 11796480 | tf_op jit(solution)/shard_map/jtc,jrc->tr/dot_general | solution.py:341
  95.7 3.1 %fusion = f32[128,8192]{1,0:T(8,128)S(1)} fusion(f32[128,8192]{1,0:T(8,128)S(1)} %constant_dynamic-update-slice_fusion.16, f32[128]{0:T(128)S(1)} %copy-done.10, f32[8192]{0:T(1024)S(1)} %neg.24), kind=kOutput, calls=%fused_computation.1 | convolution fusion | flops 1612726272 | bytes 8421888 | tf_op jit(solution)/shard_map/dot_general | solution.py:311
  98.9 1.9 %copy-done.2 = f32[128,8192]{1,0:T(8,128)} copy-done((f32[128,8192]{1,0:T(8,128)}, f32[128,8192]{1,0:T(8,128)S(1)}, u32[]{:S(2)}) %copy-start.2) | copy-done | bytes 4194328
  101.5 14.7 %shard_map.121 = bf16[16,16,512]{2,1,0:T(8,128)(2,1)} custom-call(bf16[16,512]{1,0:T(8,128)(2,1)} %convert_element_type.72.final_ref), custom_call_target="tpu_custom_call" | custom-call | tf_op jit(solution)/shard_map/pallas_call | solution.py:60
  116.2 1.2 multiply_reduce_fusion
  117.4 3.1 %add_multiply_fusion = f32[128,8192]{1,0:T(8,128)S(1)} fusion(f32[128,8192]{1,0:T(8,128)} %copy-done.2, f32[8192]{0:T(1024)S(1)} %exponential_multiply_fusion, f32[8192]{0:T(1024)S(1)} %bitcast.78, f32[8192]{0:T(1024)S(1)} %bitcast.70, f32[128]{0:T(128)} %copy-done.9), kind=kLoop, calls=%fused_computation | loop fusion | flops 4194304 | bytes 8487424 | tf_op jit(solution)/shard_map/mul | solution.py:350
  121.2 2.3 %collective-permute-start.1 = (f32[3,2,512]{2,1,0:T(2,128)S(1)}, f32[3,2,512]{2,1,0:T(2,128)S(1)}, u32[]{:S(2)}, u32[]{:S(2)}) collective-permute-start(f32[3,2,512]{2,1,0:T(2,128)S(1)} %slice.249), channel_id=1, source_target_pairs={{16,0},{32,16},{48,32},{64,48},{80,64},{96,80},{112,96},{128,112},... | collective-permute-start | bytes 36872 | tf_op jit(solution)/shard_map/ppermute | solution.py:76
  123.5 2.7 %collective-permute-done.1 = f32[3,2,512]{2,1,0:T(2,128)S(1)} collective-permute-done((f32[3,2,512]{2,1,0:T(2,128)S(1)}, f32[3,2,512]{2,1,0:T(2,128)S(1)}, u32[]{:S(2)}, u32[]{:S(2)}) %collective-permute-start.1) | collective-permute-done | bytes 12320 | tf_op jit(solution)/shard_map/ppermute | solution.py:76
  126.6 0.8 slice_bitcast_fusion.3
  127.6 0.8 copy.15
  (81 shorter events, 5.7 us)
Async XLA Ops:
  0.6 9.2 %copy-start.4 = (bf16[128,512]{1,0:T(8,128)(2,1)S(1)}, bf16[128,512]{1,0:T(8,128)(2,1)}, u32[]{:S(2)}) copy-start(bf16[128,512]{1,0:T(8,128)(2,1)} %param.11) | copy-start | bytes 393220
  0.6 9.2 %copy-start.5 = (bf16[128,512]{1,0:T(8,128)(2,1)S(1)}, bf16[128,512]{1,0:T(8,128)(2,1)}, u32[]{:S(2)}) copy-start(bf16[128,512]{1,0:T(8,128)(2,1)} %param.10) | copy-start | bytes 393220
  0.7 9.2 %copy-start.6 = (bf16[128,512]{1,0:T(8,128)(2,1)S(1)}, bf16[128,512]{1,0:T(8,128)(2,1)}, u32[]{:S(2)}) copy-start(bf16[128,512]{1,0:T(8,128)(2,1)} %param.9) | copy-start | bytes 393220
  1.5 8.4 %collective-permute-start = (bf16[3,2,512]{2,1,0:T(2,128)(2,1)S(1)}, bf16[3,2,512]{2,1,0:T(2,128)(2,1)S(1)}, u32[]{:S(2)}, u32[]{:S(2)}) collective-permute-start(bf16[3,2,512]{2,1,0:T(2,128)(2,1)S(1)} %pad_maximum_fusion.2), channel_id=1, source_target_pairs={{0,16},{16,32},{32,48},{48,64},{64,80},{80,96},{96,112},{112,128},... | collective-permute-start | bytes 18440 | tf_op jit(solution)/shard_map/ppermute | solution.py:76
  5.6 68.1 %copy-start.9 = (f32[128]{0:T(128)}, f32[128]{0:T(128)S(1)}, u32[]{:S(2)}) copy-start(f32[128]{0:T(128)S(1)} %iota_convert_fusion) | copy-start | bytes 1540
  6.9 3.4 %copy-start.7 = (f32[3,512]{1,0:T(4,128)}, f32[3,512]{1,0:T(4,128)S(1)}, u32[]{:S(2)}) copy-start(f32[3,512]{1,0:T(4,128)S(1)} %get-tuple-element.34) | copy-start | bytes 18436
  13.9 2.0 %copy-start.1 = (f32[128,8192]{1,0:T(8,128)}, f32[128,8192]{1,0:T(8,128)S(1)}, u32[]{:S(2)}) copy-start(f32[128,8192]{1,0:T(8,128)S(1)} %fusion.2) | copy-start | bytes 12582916
  73.7 3.2 %copy-start.11 = (f32[512]{0:T(512)S(1)}, f32[512]{0:T(512)}, u32[]{:S(2)}) copy-start(f32[512]{0:T(512)} %param.15) | copy-start | bytes 6148
  73.7 4.6 %copy-start = (bf16[16,512,512]{2,1,0:T(8,128)(2,1)S(1)}, bf16[16,512,512]{2,1,0:T(8,128)(2,1)}, u32[]{:S(2)}) copy-start(bf16[16,512,512]{2,1,0:T(8,128)(2,1)} %get-tuple-element.15) | copy-start | bytes 25165828
  77.5 4.7 %copy-start.3 = (f32[128,512]{1,0:T(8,128)}, f32[128,512]{1,0:T(8,128)S(1)}, u32[]{:S(2)}) copy-start(f32[128,512]{1,0:T(8,128)S(1)} %fusion.14) | copy-start | bytes 786436
  82.1 45.2 %all-to-all-start = ((bf16[16,128,512]{1,2,0:T(8,128)(2,1)}), bf16[16,128,512]{1,2,0:T(8,128)(2,1)S(1)}, u32[]{:S(2)}, u32[]{:S(2)}) async-start(bf16[16,128,512]{1,2,0:T(8,128)(2,1)} %convert_bitcast_fusion), calls=%async_computation | async-start | bytes 4194304 | tf_op jit(solution)/shard_map/all_to_all | solution.py:338
  95.1 0.7 copy-start.10
  98.9 1.9 %copy-start.2 = (f32[128,8192]{1,0:T(8,128)}, f32[128,8192]{1,0:T(8,128)S(1)}, u32[]{:S(2)}) copy-start(f32[128,8192]{1,0:T(8,128)S(1)} %fusion) | copy-start | bytes 12582916
  117.4 3.1 %copy-start.12 = (f32[512]{0:T(512)S(1)}, f32[512]{0:T(512)}, u32[]{:S(2)}) copy-start(f32[512]{0:T(512)} %param.15) | copy-start | bytes 6148
  120.5 5.8 %copy-start.8 = (f32[3,512]{1,0:T(4,128)S(1)}, f32[3,512]{1,0:T(4,128)}, u32[]{:S(2)}) copy-start(f32[3,512]{1,0:T(4,128)} %copy-done.7) | copy-start | bytes 18436
  121.2 5.0 %collective-permute-start.1 = (f32[3,2,512]{2,1,0:T(2,128)S(1)}, f32[3,2,512]{2,1,0:T(2,128)S(1)}, u32[]{:S(2)}, u32[]{:S(2)}) collective-permute-start(f32[3,2,512]{2,1,0:T(2,128)S(1)} %slice.249), channel_id=1, source_target_pairs={{16,0},{32,16},{48,32},{64,48},{80,64},{96,80},{112,96},{128,112},... | collective-permute-start | bytes 36872 | tf_op jit(solution)/shard_map/ppermute | solution.py:76

commit v15 on v12

--- a/solution.py
+++ b/solution.py
@@ -239,7 +239,7 @@
     own_g.wait()
 
 
-def fetch(out_weight, grad_out, final, count, lanes, pieces=8):
+def fetch(out_weight, grad_out, final, count, lanes, pieces=2):
     half = count // 2
     sends = (half + half // 2 + (half - 1 - half // 2)) * pieces
     return pl.pallas_call(

time: 131 us -> 132 us (level)
  Pallas kernels: 71.2 us -> 72.7 us
    pallas_call x1, Pallas kernels: 56.5 us -> 58.3 us  [fetch(): pl.pallas_call(functools.partial(fetch_kernel, count, lanes), out_shape=(...]
where the time goes in v15:
time: 132 us; the launch traced here: 130 us
  Pallas kernels  72.7 us (55%)
  matrix products  16.8 us (13%)
  other arithmetic  14.4 us (11%)
  starting transfers between devices  12.4 us (9%)
  local copies, waits for them, and re-layouts  10.1 us (8%)
  waiting for transfers between devices  2.72 us (2%)
    pallas_call x1, Pallas kernels, fetch(): pl.pallas_call(functools.partial(fetch_kernel, count, lanes), out_shape=(...  58.3 us
    pallas_call x1, Pallas kernels, exchange(): pl.pallas_call(functools.partial(exchange_kernel, count, later), out_shap...  14.4 us
    unnamed x59, local copies, waits for them, and re-layouts  7.19 us
    dot_general x1, matrix products, per_device(): jnp.einsum('jtc,jrc->tr', g_all, w_all, preferred_element_type=jnp.float32)  6.76 us
    ppermute x2, starting transfers between devices, from_behind(): return lax.ppermute(block, axis, route)  6.4 us
    dot_general x2, matrix products, prefix(): jnp.dot(tri, spread, precision=highest, preferred_element_type=jnp.float32)  6.26 us
    all_to_all x1, starting transfers between devices, per_device(): received = lax.all_to_all(parts, 'ch', 0, 0, tiled=True)  6.03 us
    dot_general x1, matrix products, per_device(): jnp.einsum('tr,jrc->jtc', mixer, w_all, preferred_element_type=jnp.float32)  3.77 us
  transfers between devices with their start and end apart: 3, of which 1 were waited for; matrix products, arithmetic and copies ran while one was open for 16% of the time, Pallas kernels for 11%

profile of v15, /device:TPU:65, one launch (start us, length us, event | category | flops | bytes accessed | tf_op | source)
XLA Modules:
  0.0 130.4 jit_solution(9016539392209922673)
XLA Ops:
  0.7 0.8 pad_maximum_fusion.2
  1.5 4.1 %collective-permute-start = (bf16[3,2,512]{2,1,0:T(2,128)(2,1)S(1)}, bf16[3,2,512]{2,1,0:T(2,128)(2,1)S(1)}, u32[]{:S(2)}, u32[]{:S(2)}) collective-permute-start(bf16[3,2,512]{2,1,0:T(2,128)(2,1)S(1)} %pad_maximum_fusion.2), channel_id=1, source_target_pairs={{0,16},{16,32},{32,48},{48,64},{64,80},{80,96},{96,112},{112,128},... | collective-permute-start | bytes 18440 | tf_op jit(solution)/shard_map/ppermute | solution.py:76
  6.1 0.7 slice_bitcast_fusion.8
  6.9 0.8 copy.17
  7.7 0.8 multiply_bitcast_fusion.3
  8.5 0.8 multiply_exponential_fusion.2
  10.7 3.1 %fusion.2 = f32[128,8192]{1,0:T(8,128)S(1)} fusion(f32[128,8192]{1,0:T(8,128)S(1)} %constant_dynamic-update-slice_fusion, f32[8192]{0:T(1024)S(1)} %bitcast.67, f32[128]{0:T(128)S(1)} %iota_convert_fusion), kind=kOutput, calls=%fused_computation.4 | convolution fusion | flops 1612726272 | bytes 8421888 | tf_op jit(solution)/shard_map/dot_general | solution.py:311
  13.9 2.0 %copy-done.1 = f32[128,8192]{1,0:T(8,128)} copy-done((f32[128,8192]{1,0:T(8,128)}, f32[128,8192]{1,0:T(8,128)S(1)}, u32[]{:S(2)}) %copy-start.1) | copy-done | bytes 4194328
  16.6 58.3 %shard_map.120 = (bf16[16,512,512]{2,1,0:T(8,128)(2,1)}, bf16[16,128,512]{2,1,0:T(8,128)(2,1)}, bf16[16,16,512]{2,1,0:T(8,128)(2,1)}) custom-call(bf16[512,512]{1,0:T(8,128)(2,1)} %w_ref.1, bf16[128,512]{1,0:T(8,128)(2,1)} %g_ref.1, bf16[16,512]{1,0:T(8,128)(2,1)} %convert_element_type.65.f_ref), custom_call_target="tpu_custom_call" | custom-call | tf_op jit(solution)/shard_map/pallas_call | solution.py:245
  74.9 1.1 multiply_reduce_fusion.1
  76.1 3.2 %add_multiply_fusion.1 = f32[128,8192]{1,0:T(8,128)S(1)} fusion(f32[128,8192]{1,0:T(8,128)} %copy-done.1, f32[8192]{0:T(1024)S(1)} %exponential_multiply_fusion.1, f32[8192]{0:T(1024)S(1)} %bitcast.77, f32[128]{0:T(128)S(1)} %iota_convert_fusion, f32[8192]{0:T(1024)S(1)} %neg.24), kind=kLoop, calls=%fused_computation.3 | loop fusion | flops 4194304 | bytes 8487424 | tf_op jit(solution)/shard_map/mul | solution.py:333
  79.9 0.9 copy-done
  80.8 3.8 %convert_bitcast_fusion = bf16[16,128,512]{1,2,0:T(8,128)(2,1)} fusion(bf16[16,512,512]{2,1,0:T(8,128)(2,1)S(1)} %copy-done, f32[128,512]{1,0:T(8,128)S(1)} %fusion.14, f32[3,128,512]{2,1,0:T(8,128)S(1)} %fusion.11), kind=kOutput, calls=%fused_computation.8 | convolution fusion | flops 1074921472 | bytes 11010048 | tf_op jit(solution)/shard_map/tr,jrc->jtc/dot_general | solution.py:335
  84.5 6.0 %all-to-all-start = ((bf16[16,128,512]{1,2,0:T(8,128)(2,1)}), bf16[16,128,512]{1,2,0:T(8,128)(2,1)S(1)}, u32[]{:S(2)}, u32[]{:S(2)}) async-start(bf16[16,128,512]{1,2,0:T(8,128)(2,1)} %convert_bitcast_fusion), calls=%async_computation | async-start | bytes 4194304 | tf_op jit(solution)/shard_map/all_to_all | solution.py:338
  90.6 6.8 %constant_dynamic-update-slice_fusion.31 = (f32[128,8192]{1,0:T(8,128)S(1)}, f32[128,512]{1,0:T(8,128)S(1)}, f32[1,128,512]{2,1,0:T(8,128)S(1)}) fusion(f32[3,128,512]{2,1,0:T(8,128)S(1)} %fusion.11, f32[128,512]{1,0:T(8,128)} %copy-done.3, bf16[16,128,512]{2,1,0:T(8,128)(2,1)} %get-tuple-element.14, bf16[16,512,512]{2,1,0:T(8,128)(2,1)} %get-tuple-element.15), kind=kOutput, calls=%fused_computation.105 | convolution fusion | flops 1073872896 | bytes 11796480 | tf_op jit(solution)/shard_map/jtc,jrc->tr/dot_general | solution.py:341
  98.0 3.1 %fusion = f32[128,8192]{1,0:T(8,128)S(1)} fusion(f32[128,8192]{1,0:T(8,128)S(1)} %constant_dynamic-update-slice_fusion.16, f32[128]{0:T(128)S(1)} %copy-done.10, f32[8192]{0:T(1024)S(1)} %neg.24), kind=kOutput, calls=%fused_computation.1 | convolution fusion | flops 1612726272 | bytes 8421888 | tf_op jit(solution)/shard_map/dot_general | solution.py:311
  101.2 1.9 %copy-done.2 = f32[128,8192]{1,0:T(8,128)} copy-done((f32[128,8192]{1,0:T(8,128)}, f32[128,8192]{1,0:T(8,128)S(1)}, u32[]{:S(2)}) %copy-start.2) | copy-done | bytes 4194328
  103.8 14.4 %shard_map.121 = bf16[16,16,512]{2,1,0:T(8,128)(2,1)} custom-call(bf16[16,512]{1,0:T(8,128)(2,1)} %convert_element_type.72.final_ref), custom_call_target="tpu_custom_call" | custom-call | tf_op jit(solution)/shard_map/pallas_call | solution.py:60
  118.2 1.2 multiply_reduce_fusion
  119.4 3.1 %add_multiply_fusion = f32[128,8192]{1,0:T(8,128)S(1)} fusion(f32[128,8192]{1,0:T(8,128)} %copy-done.2, f32[8192]{0:T(1024)S(1)} %exponential_multiply_fusion, f32[8192]{0:T(1024)S(1)} %bitcast.78, f32[8192]{0:T(1024)S(1)} %bitcast.70, f32[128]{0:T(128)} %copy-done.9), kind=kLoop, calls=%fused_computation | loop fusion | flops 4194304 | bytes 8487424 | tf_op jit(solution)/shard_map/mul | solution.py:350
  123.2 2.3 %collective-permute-start.1 = (f32[3,2,512]{2,1,0:T(2,128)S(1)}, f32[3,2,512]{2,1,0:T(2,128)S(1)}, u32[]{:S(2)}, u32[]{:S(2)}) collective-permute-start(f32[3,2,512]{2,1,0:T(2,128)S(1)} %slice.249), channel_id=1, source_target_pairs={{16,0},{32,16},{48,32},{64,48},{80,64},{96,80},{112,96},{128,112},... | collective-permute-start | bytes 36872 | tf_op jit(solution)/shard_map/ppermute | solution.py:76
  125.5 2.7 %collective-permute-done.1 = f32[3,2,512]{2,1,0:T(2,128)S(1)} collective-permute-done((f32[3,2,512]{2,1,0:T(2,128)S(1)}, f32[3,2,512]{2,1,0:T(2,128)S(1)}, u32[]{:S(2)}, u32[]{:S(2)}) %collective-permute-start.1) | collective-permute-done | bytes 12320 | tf_op jit(solution)/shard_map/ppermute | solution.py:76
  128.6 0.8 slice_bitcast_fusion.3
  129.6 0.8 copy.15
  (81 shorter events, 5.7 us)
Async XLA Ops:
  0.6 9.2 %copy-start.4 = (bf16[128,512]{1,0:T(8,128)(2,1)S(1)}, bf16[128,512]{1,0:T(8,128)(2,1)}, u32[]{:S(2)}) copy-start(bf16[128,512]{1,0:T(8,128)(2,1)} %param.11) | copy-start | bytes 393220
  0.6 9.2 %copy-start.5 = (bf16[128,512]{1,0:T(8,128)(2,1)S(1)}, bf16[128,512]{1,0:T(8,128)(2,1)}, u32[]{:S(2)}) copy-start(bf16[128,512]{1,0:T(8,128)(2,1)} %param.10) | copy-start | bytes 393220
  0.7 9.2 %copy-start.6 = (bf16[128,512]{1,0:T(8,128)(2,1)S(1)}, bf16[128,512]{1,0:T(8,128)(2,1)}, u32[]{:S(2)}) copy-start(bf16[128,512]{1,0:T(8,128)(2,1)} %param.9) | copy-start | bytes 393220
  1.5 8.4 %collective-permute-start = (bf16[3,2,512]{2,1,0:T(2,128)(2,1)S(1)}, bf16[3,2,512]{2,1,0:T(2,128)(2,1)S(1)}, u32[]{:S(2)}, u32[]{:S(2)}) collective-permute-start(bf16[3,2,512]{2,1,0:T(2,128)(2,1)S(1)} %pad_maximum_fusion.2), channel_id=1, source_target_pairs={{0,16},{16,32},{32,48},{48,64},{64,80},{80,96},{96,112},{112,128},... | collective-permute-start | bytes 18440 | tf_op jit(solution)/shard_map/ppermute | solution.py:76
  5.6 70.5 %copy-start.9 = (f32[128]{0:T(128)}, f32[128]{0:T(128)S(1)}, u32[]{:S(2)}) copy-start(f32[128]{0:T(128)S(1)} %iota_convert_fusion) | copy-start | bytes 1540
  6.9 3.4 %copy-start.7 = (f32[3,512]{1,0:T(4,128)}, f32[3,512]{1,0:T(4,128)S(1)}, u32[]{:S(2)}) copy-start(f32[3,512]{1,0:T(4,128)S(1)} %get-tuple-element.34) | copy-start | bytes 18436
  13.9 2.0 %copy-start.1 = (f32[128,8192]{1,0:T(8,128)}, f32[128,8192]{1,0:T(8,128)S(1)}, u32[]{:S(2)}) copy-start(f32[128,8192]{1,0:T(8,128)S(1)} %fusion.2) | copy-start | bytes 12582916
  76.1 3.2 %copy-start.11 = (f32[512]{0:T(512)S(1)}, f32[512]{0:T(512)}, u32[]{:S(2)}) copy-start(f32[512]{0:T(512)} %param.15) | copy-start | bytes 6148
  76.1 4.6 %copy-start = (bf16[16,512,512]{2,1,0:T(8,128)(2,1)S(1)}, bf16[16,512,512]{2,1,0:T(8,128)(2,1)}, u32[]{:S(2)}) copy-start(bf16[16,512,512]{2,1,0:T(8,128)(2,1)} %get-tuple-element.15) | copy-start | bytes 25165828
  79.9 4.7 %copy-start.3 = (f32[128,512]{1,0:T(8,128)}, f32[128,512]{1,0:T(8,128)S(1)}, u32[]{:S(2)}) copy-start(f32[128,512]{1,0:T(8,128)S(1)} %fusion.14) | copy-start | bytes 786436
  84.5 44.8 %all-to-all-start = ((bf16[16,128,512]{1,2,0:T(8,128)(2,1)}), bf16[16,128,512]{1,2,0:T(8,128)(2,1)S(1)}, u32[]{:S(2)}, u32[]{:S(2)}) async-start(bf16[16,128,512]{1,2,0:T(8,128)(2,1)} %convert_bitcast_fusion), calls=%async_computation | async-start | bytes 4194304 | tf_op jit(solution)/shard_map/all_to_all | solution.py:338
  97.3 0.7 copy-start.10
  101.1 1.9 %copy-start.2 = (f32[128,8192]{1,0:T(8,128)}, f32[128,8192]{1,0:T(8,128)S(1)}, u32[]{:S(2)}) copy-start(f32[128,8192]{1,0:T(8,128)S(1)} %fusion) | copy-start | bytes 12582916
  119.4 3.1 %copy-start.12 = (f32[512]{0:T(512)S(1)}, f32[512]{0:T(512)}, u32[]{:S(2)}) copy-start(f32[512]{0:T(512)} %param.15) | copy-start | bytes 6148
  122.5 5.8 %copy-start.8 = (f32[3,512]{1,0:T(4,128)S(1)}, f32[3,512]{1,0:T(4,128)}, u32[]{:S(2)}) copy-start(f32[3,512]{1,0:T(4,128)} %copy-done.7) | copy-start | bytes 18436
  123.2 5.0 %collective-permute-start.1 = (f32[3,2,512]{2,1,0:T(2,128)S(1)}, f32[3,2,512]{2,1,0:T(2,128)S(1)}, u32[]{:S(2)}, u32[]{:S(2)}) collective-permute-start(f32[3,2,512]{2,1,0:T(2,128)S(1)} %slice.249), channel_id=1, source_target_pairs={{16,0},{32,16},{48,32},{64,48},{80,64},{96,80},{112,96},{128,112},... | collective-permute-start | bytes 36872 | tf_op jit(solution)/shard_map/ppermute | solution.py:76

commit v16 on v11

--- a/solution.py
+++ b/solution.py
@@ -144,10 +144,6 @@
         def _():
             grad_link(other).start()
 
-    own_w = pltpu.make_async_copy(w_ref, w_all.at[me], own_sem.at[0])
-    own_g = pltpu.make_async_copy(g_ref, g_all.at[lane], own_sem.at[1])
-    own_w.start()
-    own_g.start()
 
     sends = []
     pieces = w_recv.shape[0] // count
@@ -198,6 +194,10 @@
         if left_steps(piece) >= 1:
             send(me, piece, left, True)
         send(me, piece, partner, True)
+    own_w = pltpu.make_async_copy(w_ref, w_all.at[me], own_sem.at[0])
+    own_g = pltpu.make_async_copy(g_ref, g_all.at[lane], own_sem.at[1])
+    own_w.start()
+    own_g.start()
     for step in range(2, longest + 2):
         for piece in range(pieces):
             if step <= right_steps(piece) + 1:

time: 130 us -> 130 us (level)
  no operation moved by 1% of the time
where the time goes in v16:
time: 130 us; the launch traced here: 128 us
  Pallas kernels  70.6 us (54%)
  matrix products  16.8 us (13%)
  other arithmetic  14.4 us (11%)
  starting transfers between devices  12.5 us (10%)
  local copies, waits for them, and re-layouts  10.1 us (8%)
  waiting for transfers between devices  2.72 us (2%)
    pallas_call x1, Pallas kernels, fetch(): pl.pallas_call(functools.partial(fetch_kernel, count, lanes), out_shape=(...  55.9 us
    pallas_call x1, Pallas kernels, exchange(): pl.pallas_call(functools.partial(exchange_kernel, count, later), out_shap...  14.7 us
    unnamed x59, local copies, waits for them, and re-layouts  7.19 us
    dot_general x1, matrix products, per_device(): jnp.einsum('jtc,jrc->tr', g_all, w_all, preferred_element_type=jnp.float32)  6.75 us
    ppermute x2, starting transfers between devices, from_behind(): return lax.ppermute(block, axis, route)  6.4 us
    dot_general x2, matrix products, prefix(): jnp.dot(tri, spread, precision=highest, preferred_element_type=jnp.float32)  6.26 us
    all_to_all x1, starting transfers between devices, per_device(): received = lax.all_to_all(parts, 'ch', 0, 0, tiled=True)  6.15 us
    dot_general x1, matrix products, per_device(): jnp.einsum('tr,jrc->jtc', mixer, w_all, preferred_element_type=jnp.float32)  3.77 us
  transfers between devices with their start and end apart: 3, of which 1 were waited for; matrix products, arithmetic and copies ran while one was open for 16% of the time, Pallas kernels for 11%

profile of v16, /device:TPU:65, one launch (start us, length us, event | category | flops | bytes accessed | tf_op | source)
XLA Modules:
  0.0 128.4 jit_solution(406975019442808624)
XLA Ops:
  0.7 0.8 pad_maximum_fusion.2
  1.5 4.1 %collective-permute-start = (bf16[3,2,512]{2,1,0:T(2,128)(2,1)S(1)}, bf16[3,2,512]{2,1,0:T(2,128)(2,1)S(1)}, u32[]{:S(2)}, u32[]{:S(2)}) collective-permute-start(bf16[3,2,512]{2,1,0:T(2,128)(2,1)S(1)} %pad_maximum_fusion.2), channel_id=1, source_target_pairs={{0,16},{16,32},{32,48},{48,64},{64,80},{80,96},{96,112},{112,128},... | collective-permute-start | bytes 18440 | tf_op jit(solution)/shard_map/ppermute | solution.py:76
  6.1 0.7 slice_bitcast_fusion.8
  6.9 0.8 copy.17
  7.7 0.8 multiply_bitcast_fusion.3
  8.5 0.8 multiply_exponential_fusion.2
  10.7 3.1 %fusion.2 = f32[128,8192]{1,0:T(8,128)S(1)} fusion(f32[128,8192]{1,0:T(8,128)S(1)} %constant_dynamic-update-slice_fusion, f32[8192]{0:T(1024)S(1)} %bitcast.67, f32[128]{0:T(128)S(1)} %iota_convert_fusion), kind=kOutput, calls=%fused_computation.4 | convolution fusion | flops 1612726272 | bytes 8421888 | tf_op jit(solution)/shard_map/dot_general | solution.py:311
  13.9 2.0 %copy-done.1 = f32[128,8192]{1,0:T(8,128)} copy-done((f32[128,8192]{1,0:T(8,128)}, f32[128,8192]{1,0:T(8,128)S(1)}, u32[]{:S(2)}) %copy-start.1) | copy-done | bytes 4194328
  16.6 55.9 %shard_map.120 = (bf16[16,512,512]{2,1,0:T(8,128)(2,1)}, bf16[16,128,512]{2,1,0:T(8,128)(2,1)}, bf16[16,16,512]{2,1,0:T(8,128)(2,1)}) custom-call(bf16[512,512]{1,0:T(8,128)(2,1)} %w_ref.1, bf16[128,512]{1,0:T(8,128)(2,1)} %g_ref.1, bf16[16,512]{1,0:T(8,128)(2,1)} %convert_element_type.65.f_ref), custom_call_target="tpu_custom_call" | custom-call | tf_op jit(solution)/shard_map/pallas_call | solution.py:245
  72.5 1.1 multiply_reduce_fusion.1
  73.7 3.2 %add_multiply_fusion.1 = f32[128,8192]{1,0:T(8,128)S(1)} fusion(f32[128,8192]{1,0:T(8,128)} %copy-done.1, f32[8192]{0:T(1024)S(1)} %exponential_multiply_fusion.1, f32[8192]{0:T(1024)S(1)} %bitcast.77, f32[128]{0:T(128)S(1)} %iota_convert_fusion, f32[8192]{0:T(1024)S(1)} %neg.24), kind=kLoop, calls=%fused_computation.3 | loop fusion | flops 4194304 | bytes 8487424 | tf_op jit(solution)/shard_map/mul | solution.py:333
  77.5 0.9 copy-done
  78.4 3.8 %convert_bitcast_fusion = bf16[16,128,512]{1,2,0:T(8,128)(2,1)} fusion(bf16[16,512,512]{2,1,0:T(8,128)(2,1)S(1)} %copy-done, f32[128,512]{1,0:T(8,128)S(1)} %fusion.14, f32[3,128,512]{2,1,0:T(8,128)S(1)} %fusion.11), kind=kOutput, calls=%fused_computation.8 | convolution fusion | flops 1074921472 | bytes 11010048 | tf_op jit(solution)/shard_map/tr,jrc->jtc/dot_general | solution.py:335
  82.1 6.1 %all-to-all-start = ((bf16[16,128,512]{1,2,0:T(8,128)(2,1)}), bf16[16,128,512]{1,2,0:T(8,128)(2,1)S(1)}, u32[]{:S(2)}, u32[]{:S(2)}) async-start(bf16[16,128,512]{1,2,0:T(8,128)(2,1)} %convert_bitcast_fusion), calls=%async_computation | async-start | bytes 4194304 | tf_op jit(solution)/shard_map/all_to_all | solution.py:338
  88.3 6.7 %constant_dynamic-update-slice_fusion.31 = (f32[128,8192]{1,0:T(8,128)S(1)}, f32[128,512]{1,0:T(8,128)S(1)}, f32[1,128,512]{2,1,0:T(8,128)S(1)}) fusion(f32[3,128,512]{2,1,0:T(8,128)S(1)} %fusion.11, f32[128,512]{1,0:T(8,128)} %copy-done.3, bf16[16,128,512]{2,1,0:T(8,128)(2,1)} %get-tuple-element.14, bf16[16,512,512]{2,1,0:T(8,128)(2,1)} %get-tuple-element.15), kind=kOutput, calls=%fused_computation.105 | convolution fusion | flops 1073872896 | bytes 11796480 | tf_op jit(solution)/shard_map/jtc,jrc->tr/dot_general | solution.py:341
  95.7 3.1 %fusion = f32[128,8192]{1,0:T(8,128)S(1)} fusion(f32[128,8192]{1,0:T(8,128)S(1)} %constant_dynamic-update-slice_fusion.16, f32[128]{0:T(128)S(1)} %copy-done.10, f32[8192]{0:T(1024)S(1)} %neg.24), kind=kOutput, calls=%fused_computation.1 | convolution fusion | flops 1612726272 | bytes 8421888 | tf_op jit(solution)/shard_map/dot_general | solution.py:311
  98.9 1.9 %copy-done.2 = f32[128,8192]{1,0:T(8,128)} copy-done((f32[128,8192]{1,0:T(8,128)}, f32[128,8192]{1,0:T(8,128)S(1)}, u32[]{:S(2)}) %copy-start.2) | copy-done | bytes 4194328
  101.5 14.7 %shard_map.121 = bf16[16,16,512]{2,1,0:T(8,128)(2,1)} custom-call(bf16[16,512]{1,0:T(8,128)(2,1)} %convert_element_type.72.final_ref), custom_call_target="tpu_custom_call" | custom-call | tf_op jit(solution)/shard_map/pallas_call | solution.py:60
  116.2 1.2 multiply_reduce_fusion
  117.4 3.1 %add_multiply_fusion = f32[128,8192]{1,0:T(8,128)S(1)} fusion(f32[128,8192]{1,0:T(8,128)} %copy-done.2, f32[8192]{0:T(1024)S(1)} %exponential_multiply_fusion, f32[8192]{0:T(1024)S(1)} %bitcast.78, f32[8192]{0:T(1024)S(1)} %bitcast.70, f32[128]{0:T(128)} %copy-done.9), kind=kLoop, calls=%fused_computation | loop fusion | flops 4194304 | bytes 8487424 | tf_op jit(solution)/shard_map/mul | solution.py:350
  121.2 2.3 %collective-permute-start.1 = (f32[3,2,512]{2,1,0:T(2,128)S(1)}, f32[3,2,512]{2,1,0:T(2,128)S(1)}, u32[]{:S(2)}, u32[]{:S(2)}) collective-permute-start(f32[3,2,512]{2,1,0:T(2,128)S(1)} %slice.249), channel_id=1, source_target_pairs={{16,0},{32,16},{48,32},{64,48},{80,64},{96,80},{112,96},{128,112},... | collective-permute-start | bytes 36872 | tf_op jit(solution)/shard_map/ppermute | solution.py:76
  123.5 2.7 %collective-permute-done.1 = f32[3,2,512]{2,1,0:T(2,128)S(1)} collective-permute-done((f32[3,2,512]{2,1,0:T(2,128)S(1)}, f32[3,2,512]{2,1,0:T(2,128)S(1)}, u32[]{:S(2)}, u32[]{:S(2)}) %collective-permute-start.1) | collective-permute-done | bytes 12320 | tf_op jit(solution)/shard_map/ppermute | solution.py:76
  126.6 0.8 slice_bitcast_fusion.3
  127.6 0.8 copy.15
  (81 shorter events, 5.7 us)
Async XLA Ops:
  0.6 9.2 %copy-start.4 = (bf16[128,512]{1,0:T(8,128)(2,1)S(1)}, bf16[128,512]{1,0:T(8,128)(2,1)}, u32[]{:S(2)}) copy-start(bf16[128,512]{1,0:T(8,128)(2,1)} %param.11) | copy-start | bytes 393220
  0.6 9.2 %copy-start.5 = (bf16[128,512]{1,0:T(8,128)(2,1)S(1)}, bf16[128,512]{1,0:T(8,128)(2,1)}, u32[]{:S(2)}) copy-start(bf16[128,512]{1,0:T(8,128)(2,1)} %param.10) | copy-start | bytes 393220
  0.7 9.2 %copy-start.6 = (bf16[128,512]{1,0:T(8,128)(2,1)S(1)}, bf16[128,512]{1,0:T(8,128)(2,1)}, u32[]{:S(2)}) copy-start(bf16[128,512]{1,0:T(8,128)(2,1)} %param.9) | copy-start | bytes 393220
  1.5 8.4 %collective-permute-start = (bf16[3,2,512]{2,1,0:T(2,128)(2,1)S(1)}, bf16[3,2,512]{2,1,0:T(2,128)(2,1)S(1)}, u32[]{:S(2)}, u32[]{:S(2)}) collective-permute-start(bf16[3,2,512]{2,1,0:T(2,128)(2,1)S(1)} %pad_maximum_fusion.2), channel_id=1, source_target_pairs={{0,16},{16,32},{32,48},{48,64},{64,80},{80,96},{96,112},{112,128},... | collective-permute-start | bytes 18440 | tf_op jit(solution)/shard_map/ppermute | solution.py:76
  5.6 68.1 %copy-start.9 = (f32[128]{0:T(128)}, f32[128]{0:T(128)S(1)}, u32[]{:S(2)}) copy-start(f32[128]{0:T(128)S(1)} %iota_convert_fusion) | copy-start | bytes 1540
  6.9 3.4 %copy-start.7 = (f32[3,512]{1,0:T(4,128)}, f32[3,512]{1,0:T(4,128)S(1)}, u32[]{:S(2)}) copy-start(f32[3,512]{1,0:T(4,128)S(1)} %get-tuple-element.34) | copy-start | bytes 18436
  13.9 2.0 %copy-start.1 = (f32[128,8192]{1,0:T(8,128)}, f32[128,8192]{1,0:T(8,128)S(1)}, u32[]{:S(2)}) copy-start(f32[128,8192]{1,0:T(8,128)S(1)} %fusion.2) | copy-start | bytes 12582916
  73.7 3.2 %copy-start.11 = (f32[512]{0:T(512)S(1)}, f32[512]{0:T(512)}, u32[]{:S(2)}) copy-start(f32[512]{0:T(512)} %param.15) | copy-start | bytes 6148
  73.7 4.6 %copy-start = (bf16[16,512,512]{2,1,0:T(8,128)(2,1)S(1)}, bf16[16,512,512]{2,1,0:T(8,128)(2,1)}, u32[]{:S(2)}) copy-start(bf16[16,512,512]{2,1,0:T(8,128)(2,1)} %get-tuple-element.15) | copy-start | bytes 25165828
  77.5 4.7 %copy-start.3 = (f32[128,512]{1,0:T(8,128)}, f32[128,512]{1,0:T(8,128)S(1)}, u32[]{:S(2)}) copy-start(f32[128,512]{1,0:T(8,128)S(1)} %fusion.14) | copy-start | bytes 786436
  82.1 45.2 %all-to-all-start = ((bf16[16,128,512]{1,2,0:T(8,128)(2,1)}), bf16[16,128,512]{1,2,0:T(8,128)(2,1)S(1)}, u32[]{:S(2)}, u32[]{:S(2)}) async-start(bf16[16,128,512]{1,2,0:T(8,128)(2,1)} %convert_bitcast_fusion), calls=%async_computation | async-start | bytes 4194304 | tf_op jit(solution)/shard_map/all_to_all | solution.py:338
  95.1 0.7 copy-start.10
  98.9 1.9 %copy-start.2 = (f32[128,8192]{1,0:T(8,128)}, f32[128,8192]{1,0:T(8,128)S(1)}, u32[]{:S(2)}) copy-start(f32[128,8192]{1,0:T(8,128)S(1)} %fusion) | copy-start | bytes 12582916
  117.4 3.1 %copy-start.12 = (f32[512]{0:T(512)S(1)}, f32[512]{0:T(512)}, u32[]{:S(2)}) copy-start(f32[512]{0:T(512)} %param.15) | copy-start | bytes 6148
  120.5 5.8 %copy-start.8 = (f32[3,512]{1,0:T(4,128)S(1)}, f32[3,512]{1,0:T(4,128)}, u32[]{:S(2)}) copy-start(f32[3,512]{1,0:T(4,128)} %copy-done.7) | copy-start | bytes 18436
  121.2 5.0 %collective-permute-start.1 = (f32[3,2,512]{2,1,0:T(2,128)S(1)}, f32[3,2,512]{2,1,0:T(2,128)S(1)}, u32[]{:S(2)}, u32[]{:S(2)}) collective-permute-start(f32[3,2,512]{2,1,0:T(2,128)S(1)} %slice.249), channel_id=1, source_target_pairs={{16,0},{32,16},{48,32},{64,48},{80,64},{96,80},{112,96},{128,112},... | collective-permute-start | bytes 36872 | tf_op jit(solution)/shard_map/ppermute | solution.py:76

commit v17 on v11

--- a/solution.py
+++ b/solution.py
@@ -112,12 +112,6 @@
             device_id_type=MESH,
         )
 
-    for peer in range(count):
-
-        @pl.when(me < peer)
-        def _():
-            state_link(peer, me).start()
-
     def grad_link(other):
         return pltpu.make_async_remote_copy(
             src_ref=g_ref,
@@ -198,6 +192,12 @@
         if left_steps(piece) >= 1:
             send(me, piece, left, True)
         send(me, piece, partner, True)
+    for peer in range(count):
+
+        @pl.when(me < peer)
+        def _():
+            state_link(peer, me).start()
+
     for step in range(2, longest + 2):
         for piece in range(pieces):
             if step <= right_steps(piece) + 1:

time: 130 us -> 130 us (level)
  no operation moved by 1% of the time
where the time goes in v17:
time: 130 us; the launch traced here: 129 us
  Pallas kernels  70.7 us (54%)
  matrix products  16.8 us (13%)
  other arithmetic  14.4 us (11%)
  starting transfers between devices  12.6 us (10%)
  local copies, waits for them, and re-layouts  10.1 us (8%)
  waiting for transfers between devices  2.72 us (2%)
    pallas_call x1, Pallas kernels, fetch(): pl.pallas_call(functools.partial(fetch_kernel, count, lanes), out_shape=(...  56 us
    pallas_call x1, Pallas kernels, exchange(): pl.pallas_call(functools.partial(exchange_kernel, count, later), out_shap...  14.7 us
    unnamed x59, local copies, waits for them, and re-layouts  7.19 us
    dot_general x1, matrix products, per_device(): jnp.einsum('jtc,jrc->tr', g_all, w_all, preferred_element_type=jnp.float32)  6.75 us
    ppermute x2, starting transfers between devices, from_behind(): return lax.ppermute(block, axis, route)  6.4 us
    dot_general x2, matrix products, prefix(): jnp.dot(tri, spread, precision=highest, preferred_element_type=jnp.float32)  6.26 us
    all_to_all x1, starting transfers between devices, per_device(): received = lax.all_to_all(parts, 'ch', 0, 0, tiled=True)  6.23 us
    dot_general x1, matrix products, per_device(): jnp.einsum('tr,jrc->jtc', mixer, w_all, preferred_element_type=jnp.float32)  3.77 us
  transfers between devices with their start and end apart: 3, of which 1 were waited for; matrix products, arithmetic and copies ran while one was open for 16% of the time, Pallas kernels for 11%

profile of v17, /device:TPU:65, one launch (start us, length us, event | category | flops | bytes accessed | tf_op | source)
XLA Modules:
  0.0 128.6 jit_solution(11168796514734266349)
XLA Ops:
  0.7 0.8 pad_maximum_fusion.2
  1.5 4.1 %collective-permute-start = (bf16[3,2,512]{2,1,0:T(2,128)(2,1)S(1)}, bf16[3,2,512]{2,1,0:T(2,128)(2,1)S(1)}, u32[]{:S(2)}, u32[]{:S(2)}) collective-permute-start(bf16[3,2,512]{2,1,0:T(2,128)(2,1)S(1)} %pad_maximum_fusion.2), channel_id=1, source_target_pairs={{0,16},{16,32},{32,48},{48,64},{64,80},{80,96},{96,112},{112,128},... | collective-permute-start | bytes 18440 | tf_op jit(solution)/shard_map/ppermute | solution.py:76
  6.1 0.7 slice_bitcast_fusion.8
  6.9 0.8 copy.17
  7.7 0.8 multiply_bitcast_fusion.3
  8.5 0.8 multiply_exponential_fusion.2
  10.7 3.1 %fusion.2 = f32[128,8192]{1,0:T(8,128)S(1)} fusion(f32[128,8192]{1,0:T(8,128)S(1)} %constant_dynamic-update-slice_fusion, f32[8192]{0:T(1024)S(1)} %bitcast.67, f32[128]{0:T(128)S(1)} %iota_convert_fusion), kind=kOutput, calls=%fused_computation.4 | convolution fusion | flops 1612726272 | bytes 8421888 | tf_op jit(solution)/shard_map/dot_general | solution.py:311
  13.9 2.0 %copy-done.1 = f32[128,8192]{1,0:T(8,128)} copy-done((f32[128,8192]{1,0:T(8,128)}, f32[128,8192]{1,0:T(8,128)S(1)}, u32[]{:S(2)}) %copy-start.1) | copy-done | bytes 4194328
  16.6 56.0 %shard_map.120 = (bf16[16,512,512]{2,1,0:T(8,128)(2,1)}, bf16[16,128,512]{2,1,0:T(8,128)(2,1)}, bf16[16,16,512]{2,1,0:T(8,128)(2,1)}) custom-call(bf16[512,512]{1,0:T(8,128)(2,1)} %w_ref.1, bf16[128,512]{1,0:T(8,128)(2,1)} %g_ref.1, bf16[16,512]{1,0:T(8,128)(2,1)} %convert_element_type.65.f_ref), custom_call_target="tpu_custom_call" | custom-call | tf_op jit(solution)/shard_map/pallas_call | solution.py:245
  72.6 1.1 multiply_reduce_fusion.1
  73.9 3.2 %add_multiply_fusion.1 = f32[128,8192]{1,0:T(8,128)S(1)} fusion(f32[128,8192]{1,0:T(8,128)} %copy-done.1, f32[8192]{0:T(1024)S(1)} %exponential_multiply_fusion.1, f32[8192]{0:T(1024)S(1)} %bitcast.77, f32[128]{0:T(128)S(1)} %iota_convert_fusion, f32[8192]{0:T(1024)S(1)} %neg.24), kind=kLoop, calls=%fused_computation.3 | loop fusion | flops 4194304 | bytes 8487424 | tf_op jit(solution)/shard_map/mul | solution.py:333
  77.6 0.9 copy-done
  78.5 3.8 %convert_bitcast_fusion = bf16[16,128,512]{1,2,0:T(8,128)(2,1)} fusion(bf16[16,512,512]{2,1,0:T(8,128)(2,1)S(1)} %copy-done, f32[128,512]{1,0:T(8,128)S(1)} %fusion.14, f32[3,128,512]{2,1,0:T(8,128)S(1)} %fusion.11), kind=kOutput, calls=%fused_computation.8 | convolution fusion | flops 1074921472 | bytes 11010048 | tf_op jit(solution)/shard_map/tr,jrc->jtc/dot_general | solution.py:335
  82.3 6.2 %all-to-all-start = ((bf16[16,128,512]{1,2,0:T(8,128)(2,1)}), bf16[16,128,512]{1,2,0:T(8,128)(2,1)S(1)}, u32[]{:S(2)}, u32[]{:S(2)}) async-start(bf16[16,128,512]{1,2,0:T(8,128)(2,1)} %convert_bitcast_fusion), calls=%async_computation | async-start | bytes 4194304 | tf_op jit(solution)/shard_map/all_to_all | solution.py:338
  88.5 6.7 %constant_dynamic-update-slice_fusion.31 = (f32[128,8192]{1,0:T(8,128)S(1)}, f32[128,512]{1,0:T(8,128)S(1)}, f32[1,128,512]{2,1,0:T(8,128)S(1)}) fusion(f32[3,128,512]{2,1,0:T(8,128)S(1)} %fusion.11, f32[128,512]{1,0:T(8,128)} %copy-done.3, bf16[16,128,512]{2,1,0:T(8,128)(2,1)} %get-tuple-element.14, bf16[16,512,512]{2,1,0:T(8,128)(2,1)} %get-tuple-element.15), kind=kOutput, calls=%fused_computation.105 | convolution fusion | flops 1073872896 | bytes 11796480 | tf_op jit(solution)/shard_map/jtc,jrc->tr/dot_general | solution.py:341
  95.9 3.1 %fusion = f32[128,8192]{1,0:T(8,128)S(1)} fusion(f32[128,8192]{1,0:T(8,128)S(1)} %constant_dynamic-update-slice_fusion.16, f32[128]{0:T(128)S(1)} %copy-done.10, f32[8192]{0:T(1024)S(1)} %neg.24), kind=kOutput, calls=%fused_computation.1 | convolution fusion | flops 1612726272 | bytes 8421888 | tf_op jit(solution)/shard_map/dot_general | solution.py:311
  99.1 1.9 %copy-done.2 = f32[128,8192]{1,0:T(8,128)} copy-done((f32[128,8192]{1,0:T(8,128)}, f32[128,8192]{1,0:T(8,128)S(1)}, u32[]{:S(2)}) %copy-start.2) | copy-done | bytes 4194328
  101.7 14.7 %shard_map.121 = bf16[16,16,512]{2,1,0:T(8,128)(2,1)} custom-call(bf16[16,512]{1,0:T(8,128)(2,1)} %convert_element_type.72.final_ref), custom_call_target="tpu_custom_call" | custom-call | tf_op jit(solution)/shard_map/pallas_call | solution.py:60
  116.4 1.2 multiply_reduce_fusion
  117.6 3.1 %add_multiply_fusion = f32[128,8192]{1,0:T(8,128)S(1)} fusion(f32[128,8192]{1,0:T(8,128)} %copy-done.2, f32[8192]{0:T(1024)S(1)} %exponential_multiply_fusion, f32[8192]{0:T(1024)S(1)} %bitcast.78, f32[8192]{0:T(1024)S(1)} %bitcast.70, f32[128]{0:T(128)} %copy-done.9), kind=kLoop, calls=%fused_computation | loop fusion | flops 4194304 | bytes 8487424 | tf_op jit(solution)/shard_map/mul | solution.py:350
  121.4 2.3 %collective-permute-start.1 = (f32[3,2,512]{2,1,0:T(2,128)S(1)}, f32[3,2,512]{2,1,0:T(2,128)S(1)}, u32[]{:S(2)}, u32[]{:S(2)}) collective-permute-start(f32[3,2,512]{2,1,0:T(2,128)S(1)} %slice.249), channel_id=1, source_target_pairs={{16,0},{32,16},{48,32},{64,48},{80,64},{96,80},{112,96},{128,112},... | collective-permute-start | bytes 36872 | tf_op jit(solution)/shard_map/ppermute | solution.py:76
  123.7 2.7 %collective-permute-done.1 = f32[3,2,512]{2,1,0:T(2,128)S(1)} collective-permute-done((f32[3,2,512]{2,1,0:T(2,128)S(1)}, f32[3,2,512]{2,1,0:T(2,128)S(1)}, u32[]{:S(2)}, u32[]{:S(2)}) %collective-permute-start.1) | collective-permute-done | bytes 12320 | tf_op jit(solution)/shard_map/ppermute | solution.py:76
  126.8 0.8 slice_bitcast_fusion.3
  127.8 0.8 copy.15
  (81 shorter events, 5.7 us)
Async XLA Ops:
  0.6 9.2 %copy-start.4 = (bf16[128,512]{1,0:T(8,128)(2,1)S(1)}, bf16[128,512]{1,0:T(8,128)(2,1)}, u32[]{:S(2)}) copy-start(bf16[128,512]{1,0:T(8,128)(2,1)} %param.11) | copy-start | bytes 393220
  0.6 9.2 %copy-start.5 = (bf16[128,512]{1,0:T(8,128)(2,1)S(1)}, bf16[128,512]{1,0:T(8,128)(2,1)}, u32[]{:S(2)}) copy-start(bf16[128,512]{1,0:T(8,128)(2,1)} %param.10) | copy-start | bytes 393220
  0.7 9.2 %copy-start.6 = (bf16[128,512]{1,0:T(8,128)(2,1)S(1)}, bf16[128,512]{1,0:T(8,128)(2,1)}, u32[]{:S(2)}) copy-start(bf16[128,512]{1,0:T(8,128)(2,1)} %param.9) | copy-start | bytes 393220
  1.5 8.4 %collective-permute-start = (bf16[3,2,512]{2,1,0:T(2,128)(2,1)S(1)}, bf16[3,2,512]{2,1,0:T(2,128)(2,1)S(1)}, u32[]{:S(2)}, u32[]{:S(2)}) collective-permute-start(bf16[3,2,512]{2,1,0:T(2,128)(2,1)S(1)} %pad_maximum_fusion.2), channel_id=1, source_target_pairs={{0,16},{16,32},{32,48},{48,64},{64,80},{80,96},{96,112},{112,128},... | collective-permute-start | bytes 18440 | tf_op jit(solution)/shard_map/ppermute | solution.py:76
  5.6 68.3 %copy-start.9 = (f32[128]{0:T(128)}, f32[128]{0:T(128)S(1)}, u32[]{:S(2)}) copy-start(f32[128]{0:T(128)S(1)} %iota_convert_fusion) | copy-start | bytes 1540
  6.9 3.4 %copy-start.7 = (f32[3,512]{1,0:T(4,128)}, f32[3,512]{1,0:T(4,128)S(1)}, u32[]{:S(2)}) copy-start(f32[3,512]{1,0:T(4,128)S(1)} %get-tuple-element.34) | copy-start | bytes 18436
  13.9 2.0 %copy-start.1 = (f32[128,8192]{1,0:T(8,128)}, f32[128,8192]{1,0:T(8,128)S(1)}, u32[]{:S(2)}) copy-start(f32[128,8192]{1,0:T(8,128)S(1)} %fusion.2) | copy-start | bytes 12582916
  73.8 3.2 %copy-start.11 = (f32[512]{0:T(512)S(1)}, f32[512]{0:T(512)}, u32[]{:S(2)}) copy-start(f32[512]{0:T(512)} %param.15) | copy-start | bytes 6148
  73.9 4.6 %copy-start = (bf16[16,512,512]{2,1,0:T(8,128)(2,1)S(1)}, bf16[16,512,512]{2,1,0:T(8,128)(2,1)}, u32[]{:S(2)}) copy-start(bf16[16,512,512]{2,1,0:T(8,128)(2,1)} %get-tuple-element.15) | copy-start | bytes 25165828
  77.6 4.7 %copy-start.3 = (f32[128,512]{1,0:T(8,128)}, f32[128,512]{1,0:T(8,128)S(1)}, u32[]{:S(2)}) copy-start(f32[128,512]{1,0:T(8,128)S(1)} %fusion.14) | copy-start | bytes 786436
  82.3 45.3 %all-to-all-start = ((bf16[16,128,512]{1,2,0:T(8,128)(2,1)}), bf16[16,128,512]{1,2,0:T(8,128)(2,1)S(1)}, u32[]{:S(2)}, u32[]{:S(2)}) async-start(bf16[16,128,512]{1,2,0:T(8,128)(2,1)} %convert_bitcast_fusion), calls=%async_computation | async-start | bytes 4194304 | tf_op jit(solution)/shard_map/all_to_all | solution.py:338
  95.3 0.7 copy-start.10
  99.1 1.9 %copy-start.2 = (f32[128,8192]{1,0:T(8,128)}, f32[128,8192]{1,0:T(8,128)S(1)}, u32[]{:S(2)}) copy-start(f32[128,8192]{1,0:T(8,128)S(1)} %fusion) | copy-start | bytes 12582916
  117.6 3.1 %copy-start.12 = (f32[512]{0:T(512)S(1)}, f32[512]{0:T(512)}, u32[]{:S(2)}) copy-start(f32[512]{0:T(512)} %param.15) | copy-start | bytes 6148
  120.7 5.8 %copy-start.8 = (f32[3,512]{1,0:T(4,128)S(1)}, f32[3,512]{1,0:T(4,128)}, u32[]{:S(2)}) copy-start(f32[3,512]{1,0:T(4,128)} %copy-done.7) | copy-start | bytes 18436
  121.4 5.0 %collective-permute-start.1 = (f32[3,2,512]{2,1,0:T(2,128)S(1)}, f32[3,2,512]{2,1,0:T(2,128)S(1)}, u32[]{:S(2)}, u32[]{:S(2)}) collective-permute-start(f32[3,2,512]{2,1,0:T(2,128)S(1)} %slice.249), channel_id=1, source_target_pairs={{16,0},{32,16},{48,32},{64,48},{80,64},{96,80},{112,96},{128,112},... | collective-permute-start | bytes 36872 | tf_op jit(solution)/shard_map/ppermute | solution.py:76
